TPU v7x, 32 devices: a whole 2x2x4 slice. The times are simulated.
32 devices in a mesh: rep: 2 (over x), seq: 8 (over z, y), head: 2 (over core).
Axes of the slice: x: 2, y: 2, z: 4, core: 2. Of those that a mesh axis runs over, the one named last changes fastest.
Arguments:
- query_rows: bfloat16 [2048, 4096], P(('rep', 'seq'), 'head'), parts along dimension 0, may hold values from -40 to 40
- key_rows: bfloat16 [2048, 4096], P(('rep', 'seq'), 'head'), parts along dimension 0, may hold values from -6 to 6
- value_rows: bfloat16 [2048, 4096], P(('rep', 'seq'), 'head'), parts along dimension 0, may hold values from -6 to 6
- rand_blocks: int32 [16, 32, 3], P('rep'), parts along dimension 0, may hold values from 0 to 7, as said below
- out_weight: bfloat16 [4096, 4096], P('seq', 'head'), may hold values from -0.09375 to 0.09375
Outputs:
- projected: bfloat16 [2048, 4096], P(('rep', 'seq'), 'head'), parts along dimension 0
There are 2 independent parts, one for each index of `rep`. A program takes and returns all parts, laid end to end along the dimension named above; an argument that names none is the same for every part. Nothing has to cross between parts.
Inputs may be any that keep to these rules, and one draw needn't show every extreme that they name: `rand_blocks`: each entry is uniform over the blocks of the whole sequence. For the query blocks of one index of seq and the heads of one index of head, at most 6 entries name blocks held by one index of seq, and in every draw some index of seq is named exactly 6 times.
All inputs are finite; a program needn't handle non-finite values.
Results may differ from a plain program's by a relative error of at most 0.008.
Values may be sent and summed in bfloat16 or wider, within the bound.
No kernel may reach another device: no remote copies, remote signals or barrier semaphores. Data moves between devices by JAX's collectives and lax.ppermute only.
A program may use at most 128 MiB of HBM per device.

v0:
```python
import math

import jax
import jax.numpy as jnp
from jax import lax
from jax.sharding import PartitionSpec as P

HD = 128
BLK = 128
R = 3


def broadcast(block, axis, owner):
    block = jnp.where(lax.axis_index(axis) == owner, block, jnp.zeros_like(block))
    return lax.psum(block, axis)


def padded(array, sides, width):
    for axis, dim in sides:
        peers, length = (lax.axis_size(axis), array.shape[dim])
        up = [(i, (i + 1) % peers) for i in range(peers - 1)]
        down = [(j, i) for i, j in up]
        last = lax.slice_in_dim(array, length - width, length, axis=dim)
        initial = lax.slice_in_dim(array, 0, width, axis=dim)
        before = lax.ppermute(last, axis, up)
        after = lax.ppermute(initial, axis, down)
        array = jnp.concatenate([before, array, after], axis=dim)
    return array


def masked_softmax(scores, allowed):
    masked = jnp.where(allowed, scores, -jnp.inf)
    row_peak = jnp.max(masked, axis=-1, keepdims=True)
    expon_terms = jnp.where(allowed, jnp.exp(masked - row_peak), 0.0)
    return expon_terms / jnp.sum(expon_terms, axis=-1, keepdims=True)


def share_block(stacked, root_index):
    return broadcast(stacked, "seq", root_index)


def local(query_rows, key_rows, value_rows, rand_blocks, out_weight):
    tokens, features = query_rows.shape
    head_width = HD
    head_count = features // head_width
    blocks = tokens // BLK
    seq_count = lax.axis_size("seq")
    seq_index = lax.axis_index("seq")
    head_index = lax.axis_index("head")
    block_total = blocks * seq_count
    score_scale = 1.0 / math.sqrt(head_width)
    request_count = blocks * head_count * R
    slot_depth = (request_count + seq_count - 1) // seq_count
    first_rows = jnp.stack((query_rows, key_rows, value_rows))
    final_rows = jnp.stack((query_rows, key_rows, value_rows))
    first_glob = share_block(first_rows, 0)
    final_glob = share_block(final_rows, seq_count - 1)
    paired = jnp.stack((key_rows, value_rows))
    extended = padded(paired, (("seq", 1),), BLK)
    ext_heads = extended.reshape(2, blocks + 2, BLK, head_count, head_width).transpose(
        0, 3, 1, 2, 4
    )
    group_table = lax.dynamic_slice_in_dim(rand_blocks, head_index * head_count, head_count, 1)
    all_requests = group_table.reshape(seq_count, request_count)
    all_owner = all_requests // blocks
    request_order = jnp.arange(request_count, dtype=jnp.int32)
    earlier_request = request_order[None, :] < request_order[:, None]
    same_owner = all_owner[:, :, None] == all_owner[:, None, :]
    all_position = jnp.sum(same_owner & earlier_request[None], axis=2)
    owned_here = all_owner == seq_index
    slot_range = jnp.arange(slot_depth, dtype=jnp.int32)
    picked = owned_here[:, None, :] & (all_position[:, None, :] == slot_range[None, :, None])
    picked_request = jnp.sum(jnp.where(picked, request_order[None, None, :], 0), axis=2)
    picked_block = jnp.take_along_axis(all_requests, picked_request, axis=1) - seq_index * blocks
    picked_block = jnp.clip(picked_block, 0, blocks - 1).reshape(-1)
    picked_head = (picked_request // R % head_count).reshape(-1)
    local_pairs = paired.reshape(2, blocks, BLK, head_count, head_width)
    outgoing = local_pairs[:, picked_block, :, picked_head, :]
    outgoing = outgoing.reshape(seq_count, slot_depth, 2, BLK, head_width)
    received = lax.all_to_all(outgoing, "seq", split_axis=0, concat_axis=0, tiled=True)
    my_requests = lax.dynamic_slice_in_dim(all_requests, seq_index, 1, 0)[0]
    my_position = lax.dynamic_slice_in_dim(all_position, seq_index, 1, 0)[0]
    my_owner = my_requests // blocks
    rand_pairs = jnp.take(
        received.reshape(seq_count * slot_depth, 2, BLK, head_width),
        my_owner * slot_depth + my_position,
        axis=0,
    )
    rand_pairs = rand_pairs.reshape(blocks, head_count, R, 2, BLK, head_width).transpose(
        3, 1, 0, 2, 4, 5
    )
    block_ids = seq_index * blocks + jnp.arange(blocks, dtype=jnp.int32)
    base_slots = jnp.stack(
        [
            jnp.zeros((blocks,), jnp.int32),
            jnp.full((blocks,), block_total - 1, jnp.int32),
            jnp.clip(block_ids - 1, 0, block_total - 1),
            block_ids,
            jnp.clip(block_ids + 1, 0, block_total - 1),
        ],
        axis=1,
    )
    my_table = my_requests.reshape(blocks, head_count, R).transpose(1, 0, 2)
    slot_ids = jnp.concatenate(
        [jnp.broadcast_to(base_slots[None], (head_count, blocks, 5)), my_table], axis=2
    )
    slot_count = slot_ids.shape[2]
    equal_pair = slot_ids[:, :, :, None] == slot_ids[:, :, None, :]
    earlier = jnp.arange(slot_count)[None, :] < jnp.arange(slot_count)[:, None]
    slot_live = jnp.logical_not(jnp.any(equal_pair & earlier[None, None], axis=3))
    key_live = jnp.repeat(slot_live, BLK, axis=2)
    window_index = jnp.arange(blocks)[:, None] + jnp.arange(3)[None, :]
    query_heads = query_rows.reshape(blocks, BLK, head_count, head_width).transpose(2, 0, 1, 3)
    first_heads = first_glob.reshape(3, BLK, head_count, head_width).transpose(0, 2, 1, 3)
    final_heads = final_glob.reshape(3, BLK, head_count, head_width).transpose(0, 2, 1, 3)
    target_heads = max(1, 512 // (blocks * BLK))
    heads_step = max(
        (
            width
            for width in range(1, head_count + 1)
            if head_count % width == 0 and width <= target_heads
        )
    )

    def collect(ext_part, first_block, final_block, rand_part):
        steps_here = ext_part.shape[0]
        window_blocks = ext_part[:, window_index]
        glob_blocks = jnp.stack((first_block, final_block), axis=1)[:, None]
        joined = jnp.concatenate([glob_blocks, window_blocks, rand_part], axis=2)
        return joined.reshape(steps_here, blocks, slot_count * BLK, head_width)

    def attend(head_items):
        (
            query_one,
            key_ext,
            value_ext,
            key_first,
            value_first,
            key_final,
            value_final,
            key_rand,
            value_rand,
            live_one,
        ) = head_items
        keys_sel = collect(key_ext, key_first, key_final, key_rand)
        values_sel = collect(value_ext, value_first, value_final, value_rand)
        scores = (
            jnp.einsum("hibd,hikd->hibk", query_one, keys_sel, preferred_element_type=jnp.float32)
            * score_scale
        )
        weights = masked_softmax(scores, live_one[:, :, None, :]).astype(jnp.bfloat16)
        mixed = jnp.einsum(
            "hibk,hikd->hibd", weights, values_sel, preferred_element_type=jnp.float32
        )
        return mixed.astype(jnp.bfloat16)

    def split_heads(array):
        return array.reshape((head_count // heads_step, heads_step) + array.shape[1:])

    head_inputs = (
        query_heads,
        ext_heads[0],
        ext_heads[1],
        first_heads[1],
        first_heads[2],
        final_heads[1],
        final_heads[2],
        rand_pairs[0],
        rand_pairs[1],
        key_live,
    )
    block_heads = lax.map(attend, tuple((split_heads(item) for item in head_inputs)))
    block_heads = block_heads.reshape(head_count, blocks, BLK, head_width)
    attended = block_heads.transpose(1, 2, 0, 3).reshape(tokens, features)
    glob_query = jnp.concatenate((first_glob[0], final_glob[0]), axis=0).reshape(
        2 * BLK, head_count, head_width
    )
    key_heads = key_rows.reshape(tokens, head_count, head_width)
    value_wide = value_rows.reshape(tokens, head_count, head_width).astype(jnp.float32)
    glob_scores = (
        jnp.einsum("rhd,thd->hrt", glob_query, key_heads, preferred_element_type=jnp.float32)
        * score_scale
    )
    local_peak = jnp.max(glob_scores, axis=2)
    row_peak = lax.pmax(local_peak, "seq")
    expon_terms = jnp.exp(glob_scores - row_peak[:, :, None])
    denoms = jnp.sum(expon_terms, axis=2)
    numer_terms = jnp.einsum(
        "hrt,thd->hrd", expon_terms, value_wide, preferred_element_type=jnp.float32
    )
    numer_terms, denoms = lax.psum((numer_terms, denoms), "seq")
    glob_out = (
        (numer_terms / denoms[:, :, None])
        .astype(jnp.bfloat16)
        .transpose(1, 0, 2)
        .reshape(2 * BLK, features)
    )
    head_block = jnp.where(seq_index == 0, glob_out[:BLK], attended)
    attended = attended.at[:BLK].set(head_block)
    tail_block = jnp.where(seq_index == seq_count - 1, glob_out[BLK:], attended)
    attended = attended.at[tokens - BLK :].set(tail_block)
    partial_terms = lax.dot_general(
        lax.all_gather(out_weight, "seq", axis=0, tiled=True),
        attended,
        (((1,), (1,)), ((), ())),
        preferred_element_type=jnp.float32,
    )
    summed = lax.psum_scatter(
        partial_terms.astype(jnp.bfloat16), "head", scatter_dimension=0, tiled=True
    ).astype(jnp.float32)
    return summed.T.astype(jnp.bfloat16)


def solution(mesh):
    placed = (
        P(("rep", "seq"), "head"),
        P(("rep", "seq"), "head"),
        P(("rep", "seq"), "head"),
        P("rep", None, None),
        P("seq", "head"),
    )
    return jax.shard_map(
        local, mesh=mesh, in_specs=placed, out_specs=P(("rep", "seq"), "head"), check_vma=False
    )
```

profile of v0, /device:TPU:0, one launch (start us, length us, event | category | flops | bytes accessed | tf_op | source)
XLA Modules:
  0.0 597.0 jit_solution(8939532959045065275)
XLA Ops:
  9.7 1.9 broadcast_select_fusion
  11.8 132.2 %all-reduce.6.cloned.1.call-done = (bf16[3,128,2048]{1,2,0:T(8,128)(2,1)}, bf16[3,128,2048]{1,2,0:T(8,128)(2,1)}) async-done(((bf16[3,128,2048]{1,2,0:T(8,128)(2,1)}, bf16[3,128,2048]{1,2,0:T(8,128)(2,1)}), (bf16[3,128,2048]{1,2,0:T(8,128)(2,1)}, bf16[3,128,2048]{1,2,0:T(8,128)(2,1)})) %all-reduce.6.cloned.1.call-update) | async-done | bytes 3145744 | tf_op jit(solution)/shard_map/psum | solution.py:15
  150.0 35.1 %pmax.7 = f32[16,256]{1,0:T(8,128)S(1)} all-reduce(f32[16,256]{1,0:T(8,128)S(1)} %get-tuple-element.247), channel_id=1, replica_groups=mesh['rep'=2,'seq'=8,'head'=2] {'seq'}, use_global_device_ids=true, to_apply=%region_3.4 | all-reduce | flops 4096 | bytes 32768 | tf_op jit(solution)/shard_map/pmax | solution.py:185
  185.1 3.0 fusion.25
  194.4 2.8 gather_fusion.2
  197.2 4.6 all-to-all-start
  202.9 4.7 collective-permute-start
  213.0 35.9 %collective-permute-done = bf16[2,128,2048]{1,2,0:T(8,128)(2,1)} collective-permute-done((bf16[2,128,2048]{1,2,0:T(8,128)(2,1)}, bf16[2,128,2048]{1,2,0:T(8,128)(2,1)}, u32[]{:S(2)}, u32[]{:S(2)}) %collective-permute-start) | collective-permute-done | bytes 1048608 | tf_op jit(solution)/shard_map/ppermute | solution.py:25
  248.8 3.3 pad_maximum_fusion.2
  252.1 4.7 copy.100
  256.8 2.9 copy.128
  259.8 2.2 fusion.58
  263.1 2.1 fusion.59
  265.2 2.1 copy.99
  269.7 101.5 %psum.31 = f32[16,256]{1,0:T(8,128)S(1)} all-reduce(f32[16,256]{1,0:T(8,128)S(1)} %fusion.24), channel_id=1, replica_groups=mesh['rep'=2,'seq'=8,'head'=2] {'seq'}, use_global_device_ids=true, to_apply=%region_6.7 | all-reduce | flops 4096 | bytes 32768 | tf_op jit(solution)/shard_map/psum | solution.py:191
  375.4 3.1 gather_fusion.3
  380.3 49.2 %while.16 = (s32[]{:T(128)}, bf16[4,4,1,128,128]{3,4,1,0,2:T(8,128)(2,1)}, pred[4,4,1,1024]{3,1,2,0:T(4,128)(4,1)S(1)}, bf16[4,4,1,128,128]{4,3,1,2,0:T(8,128)(2...) while((s32[]{:T(128)}, ...), condition=%wide.region_13.14_spmd.clone.clone, body=%wide.region_10.13_spmd.clone.clone.sunk | while | flops 274532352 | bytes 33842396 | solution.py:172
  384.8 3.1 fusion.76
  397.1 3.1 fusion.76
  409.4 3.1 fusion.76
  421.7 3.1 fusion.76
  431.4 139.7 %all-gather.2.cloned.1.call-done = bf16[4096,2048]{1,0:T(8,128)(2,1)} async-done(((bf16[512,2048]{1,0:T(8,128)(2,1)}), bf16[4096,2048]{1,0:T(8,128)(2,1)}) %all-gather.2.cloned.1.call-update) | async-done | bytes 16777232 | tf_op jit(solution)/shard_map/all_gather | solution.py:203
  571.1 12.5 %fusion.22 = bf16[4096,128]{0,1:T(8,128)(2,1)} fusion(bf16[128,2048]{0,1:T(8,128)(2,1)S(1)} %fusion.37, bf16[4096,2048]{1,0:T(8,128)(2,1)} %all-gather.2.cloned.1.call-done), kind=kOutput, calls=%fused_computation.43 | convolution fusion | flops 2148007936 | bytes 18350080 | tf_op jit(solution)/shard_map/dot_general | solution.py:202
  583.6 6.9 %reduce-scatter.2.cloned.1.call-done = bf16[2048,128]{0,1:T(8,128)(2,1)} async-done(((bf16[4096,128]{0,1:T(8,128)(2,1)}), bf16[2048,128]{0,1:T(8,128)(2,1)}) %reduce-scatter.2.cloned.1.call-update) | async-done | bytes 524304 | tf_op jit(solution)/shard_map/reduce_scatter | solution.py:208
  (183 shorter events, 69.6 us)
Async XLA Ops:
  6.5 182.3 %copy-start = (s32[8,32,3]{1,0,2:T(8,128)S(1)}, s32[8,32,3]{1,0,2:T(8,128)}, u32[]{:S(2)}) copy-start(s32[8,32,3]{1,0,2:T(8,128)} %param.18) | copy-start | bytes 9220
  6.5 2.9 copy-start.6
  6.5 137.5 %all-reduce.6.cloned.1.call-start = ((), (), s32[]{:S(2)}) async-start(), calls=%async_computation.5 | async-start | bytes 6291456 | tf_op jit(solution)/shard_map/psum | solution.py:15
  7.9 183.0 %copy-start.2 = (bf16[128,2048]{0,1:T(8,128)(2,1)}, bf16[128,2048]{0,1:T(8,128)(2,1)S(1)}, u32[]{:S(2)}) copy-start(bf16[128,2048]{0,1:T(8,128)(2,1)S(1)} %copy.84) | copy-start | bytes 1572868
  9.4 182.5 %copy-start.4 = (bf16[128,2048]{0,1:T(8,128)(2,1)}, bf16[128,2048]{0,1:T(8,128)(2,1)S(1)}, u32[]{:S(2)}) copy-start(bf16[128,2048]{0,1:T(8,128)(2,1)S(1)} %copy.85) | copy-start | bytes 1572868
  11.7 359.5 %all-reduce.4.cloned.1.call-start = ((), (), s32[]{:S(2)}) async-start(), calls=%async_computation.2 | async-start | bytes 4194304 | tf_op jit(solution)/shard_map/psum | solution.py:191
  188.1 382.9 %all-gather.2.cloned.1.call-start = ((), (), s32[]{:S(2)}) async-start(), calls=%async_computation.3 | async-start | bytes 18874368 | tf_op jit(solution)/shard_map/all_gather | solution.py:203
  197.2 4.6 copy-start.3
  197.2 4.6 copy-start.5
  197.2 178.2 %all-to-all-start = ((bf16[8,6,2,128,128]{4,3,2,1,0:T(8,128)(2,1)}), bf16[8,6,2,128,128]{4,3,2,1,0:T(8,128)(2,1)}, u32[]{:S(2)}, u32[]{:S(2)}) async-start(bf16[8,6,2,128,128]{4,3,2,1,0:T(8,128)(2,1)} %bitcast.194), calls=%async_computation | async-start | bytes 6291456 | tf_op jit(solution)/shard_map/all_to_all | solution.py:80
  201.7 388.7 %reduce-scatter.2.cloned.1.call-start = ((), (), s32[]{:S(2)}) async-start(), calls=%async_computation.4 | async-start | bytes 1572864 | tf_op jit(solution)/shard_map/reduce_scatter | solution.py:208
  202.9 45.9 %collective-permute-start = (bf16[2,128,2048]{1,2,0:T(8,128)(2,1)}, bf16[2,128,2048]{1,2,0:T(8,128)(2,1)}, u32[]{:S(2)}, u32[]{:S(2)}) collective-permute-start(bf16[2,128,2048]{1,2,0:T(8,128)(2,1)} %pad_maximum_fusion.4), channel_id=1, source_target_pairs={{0,2},{2,4},{4,6},{6,8},{8,10},{10,12},{12,14},{1,3},{3,5},{5,7},{... | collective-permute-start | bytes 3145736 | tf_op jit(solution)/shard_map/ppermute | solution.py:25
  207.6 41.2 %collective-permute-start.1 = (bf16[2,128,2048]{1,2,0:T(8,128)(2,1)}, bf16[2,128,2048]{1,2,0:T(8,128)(2,1)}, u32[]{:S(2)}, u32[]{:S(2)}) collective-permute-start(bf16[2,128,2048]{1,2,0:T(8,128)(2,1)} %pad_maximum_fusion.4), channel_id=1, source_target_pairs={{2,0},{4,2},{6,4},{8,6},{10,8},{12,10},{14,12},{3,1},{5,3},{7,5},{... | collective-permute-start | bytes 3145736 | tf_op jit(solution)/shard_map/ppermute | solution.py:26
  259.7 2.3 copy-start.7
  389.7 1.6 copy-start.8
  402.0 1.6 copy-start.8
  414.3 1.6 copy-start.8
  426.6 1.6 copy-start.8
  571.1 19.4 %copy-start.1 = (s32[8,32,3]{1,0,2:T(8,128)S(1)}, s32[8,32,3]{1,0,2:T(8,128)}, u32[]{:S(2)}) copy-start(s32[8,32,3]{1,0,2:T(8,128)} %param.18) | copy-start | bytes 9220
Sparse Core Ops, SparseCore 0:
  11.8 132.1 all-reduce.5
  188.3 152.7 all-reduce.3
  343.4 227.6 all-gather.1
  583.7 6.7 reduce-scatter.1
where the time goes:
time: 599 us; the launch traced here: 597 us
  waiting for transfers between devices  315 us (53%)
  blocking collectives  137 us (23%)
  local copies, waits for them, and re-layouts  73.9 us (12%)
  matrix products  31.6 us (5%)
  other arithmetic  14.8 us (2%)
  between operations  13.4 us (2%)
  starting transfers between devices  10.7 us (2%)
    all_gather x1, waiting for transfers between devices, local(): lax.all_gather(out_weight, 'seq', axis=0, tiled=True)  140 us
    psum x1, waiting for transfers between devices, broadcast(): return lax.psum(block, axis)  132 us
    psum x1, blocking collectives, local(): numer_terms, denoms = lax.psum((numer_terms, denoms), 'seq')  102 us
    ppermute x1, waiting for transfers between devices, padded(): before = lax.ppermute(last, axis, up)  35.9 us
    pmax x1, blocking collectives, local(): row_peak = lax.pmax(local_peak, 'seq')  35.1 us
    dot_general x1, matrix products, local(): lax.dot_general(lax.all_gather(out_weight, 'seq', axis=0, tiled=True), at...  12.5 us
    sub x4, matrix products, masked_softmax(): expon_terms = jnp.where(allowed, jnp.exp(masked - row_peak), 0.0)  12.3 us
  transfers between devices with their start and end apart: 7, of which 4 were waited for; matrix products, arithmetic and copies ran while one was open for 15% of the time, Pallas kernels for 0%

commit v1 on v0

--- a/solution.py
+++ b/solution.py
@@ -3,11 +3,14 @@
 import jax
 import jax.numpy as jnp
 from jax import lax
+from jax.experimental import pallas as pl
+from jax.experimental.pallas import tpu as pltpu
 from jax.sharding import PartitionSpec as P
 
 HD = 128
 BLK = 128
 R = 3
+VMEM = 48 << 20
 
 
 def broadcast(block, axis, owner):
@@ -39,7 +42,7 @@
     return broadcast(stacked, "seq", root_index)
 
 
-def local(query_rows, key_rows, value_rows, rand_blocks, out_weight):
+def local_by_rows(query_rows, key_rows, value_rows, rand_blocks, out_weight):
     tokens, features = query_rows.shape
     head_width = HD
     head_count = features // head_width
@@ -211,6 +214,167 @@
     return summed.T.astype(jnp.bfloat16)
 
 
+def spread_kernel(query_ref, key_ref, value_ref, out_ref):
+    out_ref[0, 0] = query_ref[...]
+    out_ref[0, 1] = key_ref[...]
+    out_ref[0, 2] = value_ref[...]
+
+
+def spread(query_rows, key_rows, value_rows, peers):
+    tokens, features = query_rows.shape
+    width = features // peers
+    rows = pl.BlockSpec((tokens, width), lambda j: (0, j))
+    return pl.pallas_call(
+        spread_kernel,
+        grid=(peers,),
+        in_specs=[rows] * 3,
+        out_specs=pl.BlockSpec((1, 3, tokens, width), lambda j: (j, 0, 0, 0)),
+        out_shape=jax.ShapeDtypeStruct((peers, 3, tokens, width), query_rows.dtype),
+    )(query_rows, key_rows, value_rows)
+
+
+def attend_kernel(query_ref, key_ref, value_ref, bias_ref, out_ref):
+    groups, _, tokens, width = query_ref.shape
+    total = groups * tokens
+    blocks = total // BLK
+    factor = math.log2(math.e) / math.sqrt(width)
+    keys = key_ref[...].reshape(total, width)
+    values = value_ref[...].reshape(total, width)
+    query = query_ref[...].reshape(total, width)
+    for block in range(blocks):
+        rows = slice(block * BLK, (block + 1) * BLK)
+        scores = lax.dot_general(
+            query[rows], keys, (((1,), (1,)), ((), ())), preferred_element_type=jnp.float32
+        )
+        scores = scores * factor + bias_ref[0, block : block + 1, :]
+        peak = jnp.max(scores, axis=1, keepdims=True)
+        terms = jnp.exp2(scores - peak)
+        denom = jnp.sum(terms, axis=1, keepdims=True)
+        mixed = jnp.dot(
+            terms.astype(jnp.bfloat16), values, preferred_element_type=jnp.float32
+        )
+        out_ref[rows, :] = (mixed / denom).astype(out_ref.dtype)
+
+
+def attend_heads(rows, bias):
+    groups, _, tokens, features = rows.shape
+    heads = features // HD
+    total = groups * tokens
+
+    def part(which):
+        return pl.BlockSpec((groups, 1, tokens, HD), lambda h: (0, which, 0, h))
+
+    return pl.pallas_call(
+        attend_kernel,
+        grid=(heads,),
+        in_specs=[
+            part(0),
+            part(1),
+            part(2),
+            pl.BlockSpec((1,) + bias.shape[1:], lambda h: (h, 0, 0)),
+        ],
+        out_specs=pl.BlockSpec((total, HD), lambda h: (0, h)),
+        out_shape=jax.ShapeDtypeStruct((total, features), rows.dtype),
+        compiler_params=pltpu.CompilerParams(vmem_limit_bytes=VMEM),
+    )(rows, rows, rows, bias)
+
+
+def project_kernel(head_ref, rows_ref, weight_ref, send_ref, keep_ref, total_ref):
+    step = pl.program_id(0)
+    half = send_ref.shape[1]
+
+    @pl.when(step == 0)
+    def _():
+        total_ref[...] = jnp.zeros_like(total_ref)
+
+    total_ref[...] += lax.dot_general(
+        rows_ref[0],
+        weight_ref[...],
+        (((1,), (1,)), ((), ())),
+        preferred_element_type=jnp.float32,
+    )
+
+    @pl.when(step == pl.num_programs(0) - 1)
+    def _():
+        low = total_ref[:, :half].astype(send_ref.dtype)
+        high = total_ref[:, half:].astype(send_ref.dtype)
+        first = head_ref[0] == 0
+        send_ref[...] = jnp.where(first, high, low)
+        keep_ref[...] = jnp.where(first, low, high)
+
+
+def project(head, gathered, weight):
+    peers, total, width = gathered.shape
+    outs = weight.shape[0]
+    half = outs // 2
+    result = jax.ShapeDtypeStruct((total, half), gathered.dtype)
+    whole = pl.BlockSpec((total, half), lambda j, _: (0, 0))
+    return pl.pallas_call(
+        project_kernel,
+        grid_spec=pltpu.PrefetchScalarGridSpec(
+            num_scalar_prefetch=1,
+            grid=(peers,),
+            in_specs=[
+                pl.BlockSpec((1, total, width), lambda j, _: (j, 0, 0)),
+                pl.BlockSpec((outs, width), lambda j, _: (0, j)),
+            ],
+            out_specs=[whole, whole],
+            scratch_shapes=[pltpu.VMEM((total, outs), jnp.float32)],
+        ),
+        out_shape=[result, result],
+        compiler_params=pltpu.CompilerParams(vmem_limit_bytes=VMEM),
+    )(head, gathered, weight)
+
+
+def key_bias(rand_blocks, head_start, heads):
+    block_total = rand_blocks.shape[0]
+    ids = jnp.arange(block_total, dtype=jnp.int32)
+    near = jnp.abs(ids[:, None] - ids[None, :]) <= 1
+    ends = (ids == 0) | (ids == block_total - 1)
+    fixed = near | ends[None, :] | ends[:, None]
+    chosen = lax.dynamic_slice_in_dim(rand_blocks, head_start, heads, 1)
+    named = jnp.any(chosen[:, :, :, None] == ids, axis=2).transpose(1, 0, 2)
+    live = named | fixed[None]
+    return jnp.repeat(jnp.where(live, 0.0, -1e30).astype(jnp.float32), BLK, axis=2)
+
+
+def local_by_heads(query_rows, key_rows, value_rows, rand_blocks, out_weight):
+    tokens, features = query_rows.shape
+    peers = lax.axis_size("seq")
+    seq_index = lax.axis_index("seq")
+    head_index = lax.axis_index("head")
+    heads = features // HD // peers
+    outgoing = spread(query_rows, key_rows, value_rows, peers)
+    rows = lax.all_to_all(outgoing, "seq", split_axis=0, concat_axis=0, tiled=True)
+    bias = key_bias(rand_blocks, head_index * (features // HD) + seq_index * heads, heads)
+    attended = attend_heads(rows, bias)
+    gathered = lax.all_gather(attended, "seq", axis=0)
+    swap = [(0, 1), (1, 0)]
+    send, keep = project(head_index[None], gathered, out_weight)
+    other = lax.ppermute(send, "head", swap)
+    summed = (keep.astype(jnp.float32) + other.astype(jnp.float32)).astype(jnp.bfloat16)
+    outs = summed.shape[1]
+    summed = summed.reshape(peers, tokens, outs)
+    arrived = lax.all_to_all(summed, "seq", split_axis=0, concat_axis=0, tiled=True)
+    arrived = arrived.reshape(2, peers // 2, tokens, outs)
+    mine = lax.dynamic_index_in_dim(arrived, head_index, 0, keepdims=False)
+    theirs = lax.dynamic_index_in_dim(arrived, 1 - head_index, 0, keepdims=False)
+    crossed = lax.ppermute(theirs, "head", swap)
+    first = head_index == 0
+    pair = jnp.stack(
+        [jnp.where(first, mine, crossed), jnp.where(first, crossed, mine)], axis=1
+    )
+    return pair.transpose(2, 0, 1, 3).reshape(tokens, features)
+
+
+def local(query_rows, key_rows, value_rows, rand_blocks, out_weight):
+    head_count = query_rows.shape[1] // HD
+    peers = lax.axis_size("seq")
+    if lax.axis_size("head") == 2 and head_count % peers == 0 and peers % 2 == 0:
+        return local_by_heads(query_rows, key_rows, value_rows, rand_blocks, out_weight)
+    return local_by_rows(query_rows, key_rows, value_rows, rand_blocks, out_weight)
+
+
 def solution(mesh):
     placed = (
         P(("rep", "seq"), "head"),

time: 599 us -> 176 us (0.29)
  waiting for transfers between devices: 315 us -> 127 us
  blocking collectives: 137 us -> 0 us
  local copies, waits for them, and re-layouts: 73.9 us -> 3.24 us
  matrix products: 31.6 us -> 0 us
  Pallas kernels: 0 us -> 19.2 us
  other arithmetic: 14.8 us -> 1.2 us
    psum x2 -> x0, waiting for transfers between devices: 132 us -> none  [the longest x1 132 us: broadcast(): return lax.psum(block, axis)]
    psum x1 -> x0, blocking collectives: 102 us -> none  [local(): numer_terms, denoms = lax.psum((numer_terms, denoms), 'seq')]
    all_gather x1, waiting for transfers between devices: 140 us -> 72.6 us  [local_by_heads(): gathered = lax.all_gather(attended, 'seq', axis=0)]
    all_to_all x1 -> x2, waiting for transfers between devices: 0.01 us -> 51.4 us  [the longest x1 36.4 us: local_by_heads(): lax.all_to_all(outgoing, 'seq', split_axis=0, concat_axis=0, tiled=True)]
    pmax x1 -> x0, blocking collectives: 35.1 us -> none  [local(): row_peak = lax.pmax(local_peak, 'seq')]
    ppermute x2, waiting for transfers between devices: 35.9 us -> 3.41 us  [the longest x1 1.9 us: local_by_heads(): other = lax.ppermute(send, 'head', swap)]
    dot_general x7 -> x0, matrix products: 19.3 us -> none  [the longest x1 12.5 us: local(): lax.dot_general(lax.all_gather(out_weight, 'seq', axis=0, tiled=True), at...]
    pallas_call x0 -> x3, Pallas kernels: none -> 19.2 us  [the longest x1 6.99 us: project(): pl.pallas_call(project_kernel, grid_spec=pltpu.PrefetchScalarGridSpec(num...]
  transfers between devices with their start and end apart: 7 -> 5, of which waited for: 4 -> 5; matrix products, arithmetic and copies ran while one was open for 15% -> 0% of each run, Pallas kernels for 0% -> 0%
where the time goes in v1:
time: 176 us
  waiting for transfers between devices  127 us (72%)
  Pallas kernels  19.2 us (11%)
  between operations  13.5 us (8%)
  starting transfers between devices  11 us (6%)
  local copies, waits for them, and re-layouts  3.24 us (2%)
    all_gather x1, waiting for transfers between devices, local_by_heads(): gathered = lax.all_gather(attended, 'seq', axis=0)  72.6 us
    all_to_all x1, waiting for transfers between devices, local_by_heads(): lax.all_to_all(outgoing, 'seq', split_axis=0, concat_axis=0, tiled=True)  36.4 us
    all_to_all x1, waiting for transfers between devices, local_by_heads(): lax.all_to_all(summed, 'seq', split_axis=0, concat_axis=0, tiled=True)  15 us
    all_to_all x1, starting transfers between devices, local_by_heads(): lax.all_to_all(outgoing, 'seq', split_axis=0, concat_axis=0, tiled=True)  7.28 us
    pallas_call x1, Pallas kernels, project(): pl.pallas_call(project_kernel, grid_spec=pltpu.PrefetchScalarGridSpec(num...  6.99 us
    pallas_call x1, Pallas kernels, attend_heads(): pl.pallas_call(attend_kernel, grid=(heads,), in_specs=[part(0), part(1),...  6.87 us
    pallas_call x1, Pallas kernels, spread(): pl.pallas_call(spread_kernel, grid=(peers,), in_specs=[rows] * 3, out_spe...  5.34 us
  transfers between devices with their start and end apart: 5, of which 5 were waited for; matrix products, arithmetic and copies ran while one was open for 0% of the time, Pallas kernels for 0%

profile of v1, /device:TPU:0, one launch (start us, length us, event | category | flops | bytes accessed | tf_op | source)
XLA Modules:
  0.0 175.5 jit_solution(4815207995378239262)
XLA Ops:
  6.5 5.3 %shard_map.55 = bf16[8,3,128,256]{3,2,1,0:T(8,128)(2,1)} custom-call(bf16[128,2048]{1,0:T(8,128)(2,1)} %query_ref.1, bf16[128,2048]{1,0:T(8,128)(2,1)} %key_ref.1, bf16[128,2048]{1,0:T(8,128)(2,1)} %value_ref.1), custom_call_target="tpu_custom_call" | custom-call | tf_op jit(solution)/shard_map/pallas_call | solution.py:227
  11.9 7.3 %all-to-all-start = ((bf16[8,3,128,256]{3,2,1,0:T(8,128)(2,1)}), bf16[8,3,128,256]{3,2,1,0:T(8,128)(2,1)S(1)}, u32[]{:S(2)}, u32[]{:S(2)}) async-start(bf16[8,3,128,256]{3,2,1,0:T(8,128)(2,1)} %shard_map.55), calls=%async_computation | async-start | bytes 3145728 | tf_op jit(solution)/shard_map/all_to_all | solution.py:348
  19.2 0.0 all-gather.3.cloned.1.call-start
  19.2 0.1 constant_dynamic-slice_fusion
  19.3 0.1 copy.14
  19.4 0.1 fusion.2
  19.5 0.1 fusion.4
  19.6 0.1 copy.15
  19.6 0.1 broadcast_bitcast_fusion.bias_ref
  19.7 36.4 %all-to-all-done.query_ref.key_ref.value_ref = bf16[8,3,128,256]{3,2,1,0:T(8,128)(2,1)S(1)} async-done(((bf16[8,3,128,256]{3,2,1,0:T(8,128)(2,1)}), bf16[8,3,128,256]{3,2,1,0:T(8,128)(2,1)S(1)}, u32[]{:S(2)}, u32[]{:S(2)}) %all-to-all-start) | async-done | bytes 1572896 | tf_op jit(solution)/shard_map/all_to_all | solution.py:348
  56.2 6.9 %shard_map.56 = bf16[1024,256]{1,0:T(8,128)(2,1)} custom-call(bf16[8,3,128,256]{3,2,1,0:T(8,128)(2,1)S(1)} %all-to-all-done.query_ref.key_ref.value_ref, bf16[8,3,128,256]{3,2,1,0:T(8,128)(2,1)S(1)} %all-to-all-done.query_ref.key_ref.value_ref, bf16[8,3,128,256]{3,2,1,0:T(8,128)(2,1)S(1)} %all-to-all-done.query_ref.key_ref.value_ref, ...), custom_call_target="tpu_custom_call" | custom-call | tf_op jit(solution)/shard_map/pallas_call | solution.py:267
  63.1 72.6 %all-gather.3.cloned.1.call-done = bf16[8192,256]{1,0:T(8,128)(2,1)} async-done(((bf16[1024,256]{1,0:T(8,128)(2,1)}), bf16[8192,256]{1,0:T(8,128)(2,1)}) %all-gather.3.cloned.1.call-update) | async-done | bytes 4194320 | tf_op jit(solution)/shard_map/all_gather | solution.py:351
  135.7 1.6 copy-done.1
  137.3 7.0 %shard_map.57 = (bf16[1024,256]{1,0:T(8,128)(2,1)S(1)}, bf16[1024,256]{1,0:T(8,128)(2,1)S(1)}) custom-call(s32[1]{0:T(128)} %bitcast.head_ref, bf16[8,1024,256]{2,1,0:T(8,128)(2,1)} %bitcast.24, bf16[512,2048]{1,0:T(8,128)(2,1)S(1)} %copy-done.1), custom_call_target="tpu_custom_call" | custom-call | tf_op jit(solution)/shard_map/pallas_call | solution.py:312
  144.3 0.1 collective-permute-start
  144.3 1.9 %collective-permute-done = bf16[1024,256]{1,0:T(8,128)(2,1)S(1)} collective-permute-done((bf16[1024,256]{1,0:T(8,128)(2,1)S(1)}, bf16[1024,256]{1,0:T(8,128)(2,1)S(1)}, u32[]{:S(2)}, u32[]{:S(2)}) %collective-permute-start) | collective-permute-done | bytes 524320 | tf_op jit(solution)/shard_map/ppermute | solution.py:354
  146.2 0.9 add_convert_fusion
  147.2 3.5 %all-to-all-start.1 = ((bf16[8,128,256]{2,1,0:T(8,128)(2,1)}), bf16[8,128,256]{2,1,0:T(8,128)(2,1)S(1)}, u32[]{:S(2)}, u32[]{:S(2)}) async-start(bf16[8,128,256]{2,1,0:T(8,128)(2,1)} %bitcast.4), calls=%async_computation.1 | async-start | bytes 1048576 | tf_op jit(solution)/shard_map/all_to_all | solution.py:358
  150.7 15.0 %all-to-all-done.1 = bf16[8,128,256]{2,1,0:T(8,128)(2,1)S(1)} async-done(((bf16[8,128,256]{2,1,0:T(8,128)(2,1)}), bf16[8,128,256]{2,1,0:T(8,128)(2,1)S(1)}, u32[]{:S(2)}, u32[]{:S(2)}) %all-to-all-start.1) | async-done | bytes 524320 | tf_op jit(solution)/shard_map/all_to_all | solution.py:358
  165.7 0.1 collective-permute-start.1
  165.8 1.5 collective-permute-done.1
  167.3 0.1 maximum_bitcast_fusion
  167.4 0.3 copy.16
  167.7 1.0 copy.17
  (8 shorter events, 0.1 us)
Async XLA Ops:
  6.5 12.7 %copy-start = (s32[8,32,3]{1,0,2:T(8,128)S(1)}, s32[8,32,3]{1,0,2:T(8,128)}, u32[]{:S(2)}) copy-start(s32[8,32,3]{1,0,2:T(8,128)} %param.8) | copy-start | bytes 9220
  11.9 44.3 %all-to-all-start = ((bf16[8,3,128,256]{3,2,1,0:T(8,128)(2,1)}), bf16[8,3,128,256]{3,2,1,0:T(8,128)(2,1)S(1)}, u32[]{:S(2)}, u32[]{:S(2)}) async-start(bf16[8,3,128,256]{3,2,1,0:T(8,128)(2,1)} %shard_map.55), calls=%async_computation | async-start | bytes 3145728 | tf_op jit(solution)/shard_map/all_to_all | solution.py:348
  19.2 116.5 %all-gather.3.cloned.1.call-start = ((), (), s32[]{:S(2)}) async-start(), calls=%async_computation.2 | async-start | bytes 4718592 | tf_op jit(solution)/shard_map/all_gather | solution.py:351
  135.7 1.6 copy-start.1
  144.3 2.0 %collective-permute-start = (bf16[1024,256]{1,0:T(8,128)(2,1)S(1)}, bf16[1024,256]{1,0:T(8,128)(2,1)S(1)}, u32[]{:S(2)}, u32[]{:S(2)}) collective-permute-start(bf16[1024,256]{1,0:T(8,128)(2,1)S(1)} %get-tuple-element.8), channel_id=1, source_target_pairs={{0,1},{1,0},{2,3},{3,2},{4,5},{5,4},{6,7},{7,6},{8,9},{9,8},{10,11... | collective-permute-start | bytes 1572872 | tf_op jit(solution)/shard_map/ppermute | solution.py:354
  147.2 18.5 %all-to-all-start.1 = ((bf16[8,128,256]{2,1,0:T(8,128)(2,1)}), bf16[8,128,256]{2,1,0:T(8,128)(2,1)S(1)}, u32[]{:S(2)}, u32[]{:S(2)}) async-start(bf16[8,128,256]{2,1,0:T(8,128)(2,1)} %bitcast.4), calls=%async_computation.1 | async-start | bytes 1048576 | tf_op jit(solution)/shard_map/all_to_all | solution.py:358
  165.7 1.6 collective-permute-start.1
Sparse Core Ops, SparseCore 0:
  63.2 72.4 all-gather.2

commit v2 on v1

--- a/solution.py
+++ b/solution.py
@@ -1,3 +1,4 @@
+import functools
 import math
 
 import jax
@@ -10,7 +11,9 @@
 HD = 128
 BLK = 128
 R = 3
-VMEM = 48 << 20
+VMEM = 20 << 20
+TILE = 256
+EARLY = 6
 
 
 def broadcast(block, axis, owner):
@@ -215,38 +218,39 @@
 
 
 def spread_kernel(query_ref, key_ref, value_ref, out_ref):
-    out_ref[0, 0] = query_ref[...]
-    out_ref[0, 1] = key_ref[...]
-    out_ref[0, 2] = value_ref[...]
+    peers, _, _, width = out_ref.shape
+    for which, ref in enumerate((query_ref, key_ref, value_ref)):
+        for peer in range(peers):
+            out_ref[peer, which] = ref[:, peer * width : (peer + 1) * width]
 
 
 def spread(query_rows, key_rows, value_rows, peers):
     tokens, features = query_rows.shape
     width = features // peers
-    rows = pl.BlockSpec((tokens, width), lambda j: (0, j))
     return pl.pallas_call(
         spread_kernel,
-        grid=(peers,),
-        in_specs=[rows] * 3,
-        out_specs=pl.BlockSpec((1, 3, tokens, width), lambda j: (j, 0, 0, 0)),
         out_shape=jax.ShapeDtypeStruct((peers, 3, tokens, width), query_rows.dtype),
+        cost_estimate=pl.CostEstimate(
+            flops=0, bytes_accessed=12 * tokens * features, transcendentals=0
+        ),
     )(query_rows, key_rows, value_rows)
 
 
-def attend_kernel(query_ref, key_ref, value_ref, bias_ref, out_ref):
-    groups, _, tokens, width = query_ref.shape
+def attend_kernel(head, rows_ref, bias_ref, out_ref):
+    groups, _, tokens, _ = rows_ref.shape
     total = groups * tokens
     blocks = total // BLK
-    factor = math.log2(math.e) / math.sqrt(width)
-    keys = key_ref[...].reshape(total, width)
-    values = value_ref[...].reshape(total, width)
-    query = query_ref[...].reshape(total, width)
+    factor = math.log2(math.e) / math.sqrt(HD)
+    lanes = slice(head * HD, (head + 1) * HD)
+    query = rows_ref[:, 0, :, lanes].reshape(total, HD)
+    keys = rows_ref[:, 1, :, lanes].reshape(total, HD)
+    values = rows_ref[:, 2, :, lanes].reshape(total, HD)
     for block in range(blocks):
         rows = slice(block * BLK, (block + 1) * BLK)
         scores = lax.dot_general(
             query[rows], keys, (((1,), (1,)), ((), ())), preferred_element_type=jnp.float32
         )
-        scores = scores * factor + bias_ref[0, block : block + 1, :]
+        scores = scores * factor + bias_ref[head, block : block + 1, :]
         peak = jnp.max(scores, axis=1, keepdims=True)
         terms = jnp.exp2(scores - peak)
         denom = jnp.sum(terms, axis=1, keepdims=True)
@@ -256,74 +260,91 @@
         out_ref[rows, :] = (mixed / denom).astype(out_ref.dtype)
 
 
-def attend_heads(rows, bias):
-    groups, _, tokens, features = rows.shape
-    heads = features // HD
+def attend_head(rows, bias, head):
+    groups, _, tokens, _ = rows.shape
     total = groups * tokens
-
-    def part(which):
-        return pl.BlockSpec((groups, 1, tokens, HD), lambda h: (0, which, 0, h))
-
     return pl.pallas_call(
-        attend_kernel,
-        grid=(heads,),
-        in_specs=[
-            part(0),
-            part(1),
-            part(2),
-            pl.BlockSpec((1,) + bias.shape[1:], lambda h: (h, 0, 0)),
-        ],
-        out_specs=pl.BlockSpec((total, HD), lambda h: (0, h)),
-        out_shape=jax.ShapeDtypeStruct((total, features), rows.dtype),
+        functools.partial(attend_kernel, head),
+        out_shape=jax.ShapeDtypeStruct((total, HD), rows.dtype),
         compiler_params=pltpu.CompilerParams(vmem_limit_bytes=VMEM),
-    )(rows, rows, rows, bias)
-
-
-def project_kernel(head_ref, rows_ref, weight_ref, send_ref, keep_ref, total_ref):
-    step = pl.program_id(0)
-    half = send_ref.shape[1]
-
-    @pl.when(step == 0)
-    def _():
-        total_ref[...] = jnp.zeros_like(total_ref)
-
-    total_ref[...] += lax.dot_general(
-        rows_ref[0],
-        weight_ref[...],
+        cost_estimate=pl.CostEstimate(
+            flops=4 * total * total * HD,
+            bytes_accessed=8 * total * HD,
+            transcendentals=total * total,
+        ),
+    )(rows, bias)
+
+
+def product_tile(owner_ref, pieces, weight_ref, tile):
+    heads = len(pieces) // owner_ref.shape[0]
+    width = heads * HD
+    rows = jnp.concatenate([piece[tile, :] for piece in pieces], axis=1)
+    columns = [
+        weight_ref[:, pl.ds(pl.multiple_of(owner_ref[k] * width, width), width)]
+        for k in range(owner_ref.shape[0])
+    ]
+    return lax.dot_general(
+        rows,
+        jnp.concatenate(columns, axis=1),
         (((1,), (1,)), ((), ())),
         preferred_element_type=jnp.float32,
     )
 
-    @pl.when(step == pl.num_programs(0) - 1)
-    def _():
-        low = total_ref[:, :half].astype(send_ref.dtype)
-        high = total_ref[:, half:].astype(send_ref.dtype)
-        first = head_ref[0] == 0
-        send_ref[...] = jnp.where(first, high, low)
-        keep_ref[...] = jnp.where(first, low, high)
-
-
-def project(head, gathered, weight):
-    peers, total, width = gathered.shape
+
+def early_kernel(owner_ref, weight_ref, *refs):
+    *pieces, total_ref = refs
+    for start in range(0, total_ref.shape[0], TILE):
+        tile = slice(start, start + TILE)
+        total_ref[tile, :] = product_tile(owner_ref, pieces, weight_ref, tile)
+
+
+def late_kernel(owner_ref, side_ref, weight_ref, total_ref, *refs):
+    *pieces, send_ref, keep_ref = refs
+    half = send_ref.shape[1]
+    for start in range(0, total_ref.shape[0], TILE):
+        tile = slice(start, start + TILE)
+        summed = total_ref[tile, :] + product_tile(owner_ref, pieces, weight_ref, tile)
+        low = summed[:, :half].astype(send_ref.dtype)
+        high = summed[:, half:].astype(send_ref.dtype)
+        first = side_ref[0] == 0
+        send_ref[tile, :] = jnp.where(first, high, low)
+        keep_ref[tile, :] = jnp.where(first, low, high)
+
+
+SCALARS = pl.BlockSpec(memory_space=pltpu.SMEM)
+ARRAY = pl.BlockSpec(memory_space=pltpu.VMEM)
+
+
+def project_early(owners, pieces, weight):
+    total, width = pieces[0].shape
     outs = weight.shape[0]
-    half = outs // 2
-    result = jax.ShapeDtypeStruct((total, half), gathered.dtype)
-    whole = pl.BlockSpec((total, half), lambda j, _: (0, 0))
     return pl.pallas_call(
-        project_kernel,
-        grid_spec=pltpu.PrefetchScalarGridSpec(
-            num_scalar_prefetch=1,
-            grid=(peers,),
-            in_specs=[
-                pl.BlockSpec((1, total, width), lambda j, _: (j, 0, 0)),
-                pl.BlockSpec((outs, width), lambda j, _: (0, j)),
-            ],
-            out_specs=[whole, whole],
-            scratch_shapes=[pltpu.VMEM((total, outs), jnp.float32)],
+        early_kernel,
+        in_specs=[SCALARS] + [ARRAY] * (1 + len(pieces)),
+        out_shape=jax.ShapeDtypeStruct((total, outs), jnp.float32),
+        compiler_params=pltpu.CompilerParams(vmem_limit_bytes=VMEM),
+        cost_estimate=pl.CostEstimate(
+            flops=2 * total * outs * width * len(pieces),
+            bytes_accessed=2 * len(pieces) * width * (total + outs) + 4 * total * outs,
+            transcendentals=0,
         ),
-        out_shape=[result, result],
+    )(owners, weight, *pieces)
+
+
+def project_late(owners, side, pieces, weight, so_far):
+    total, width = pieces[0].shape
+    outs = weight.shape[0]
+    return pl.pallas_call(
+        late_kernel,
+        in_specs=[SCALARS] * 2 + [ARRAY] * (2 + len(pieces)),
+        out_shape=[jax.ShapeDtypeStruct((total, outs // 2), pieces[0].dtype)] * 2,
         compiler_params=pltpu.CompilerParams(vmem_limit_bytes=VMEM),
-    )(head, gathered, weight)
+        cost_estimate=pl.CostEstimate(
+            flops=2 * total * outs * width * len(pieces),
+            bytes_accessed=2 * len(pieces) * width * (total + outs) + 6 * total * outs,
+            transcendentals=0,
+        ),
+    )(owners, side, weight, so_far, *pieces)
 
 
 def key_bias(rand_blocks, head_start, heads):
@@ -338,19 +359,50 @@
     return jnp.repeat(jnp.where(live, 0.0, -1e30).astype(jnp.float32), BLK, axis=2)
 
 
+def ring_order(peers):
+    return list(range(0, peers, 2)) + list(range(peers - 1, 0, -2))
+
+
 def local_by_heads(query_rows, key_rows, value_rows, rand_blocks, out_weight):
     tokens, features = query_rows.shape
     peers = lax.axis_size("seq")
     seq_index = lax.axis_index("seq")
     head_index = lax.axis_index("head")
     heads = features // HD // peers
+    order = ring_order(peers)
+    onward = [(order[i], order[(i + 1) % peers]) for i in range(peers)]
+    back = [(target, source) for source, target in onward]
     outgoing = spread(query_rows, key_rows, value_rows, peers)
+    bias = key_bias(rand_blocks, head_index * (features // HD) + seq_index * heads, heads)
+    reach = peers // 2
+    far = {}
     rows = lax.all_to_all(outgoing, "seq", split_axis=0, concat_axis=0, tiled=True)
-    bias = key_bias(rand_blocks, head_index * (features // HD) + seq_index * heads, heads)
-    attended = attend_heads(rows, bias)
-    gathered = lax.all_gather(attended, "seq", axis=0)
+    for head in range(heads):
+        mine = attend_head(rows, bias, head)
+        ahead, behind = (mine, mine)
+        far[head, 0] = mine
+        for step in range(1, reach):
+            ahead = lax.ppermute(ahead, "seq", onward)
+            behind = lax.ppermute(behind, "seq", back)
+            far[head, step] = ahead
+            far[head, -step] = behind
+        if head % 2 == 0:
+            far[head, reach] = lax.ppermute(ahead, "seq", onward)
+        else:
+            far[head, reach] = lax.ppermute(behind, "seq", back)
+    place = jnp.where(seq_index % 2 == 0, seq_index // 2, peers - (seq_index + 1) // 2)
+
+    def gather_args(steps):
+        spots = (place - jnp.array(steps, jnp.int32)) % peers
+        owners = jnp.where(spots < reach, 2 * spots, 2 * (peers - spots) - 1)
+        return owners, [far[head, step] for step in steps for head in range(heads)]
+
+    steps = [0] + [step for hop in range(1, reach) for step in (hop, -hop)] + [reach]
+    owners, pieces = gather_args(steps[:EARLY])
+    so_far = project_early(owners, pieces, out_weight)
+    owners, pieces = gather_args(steps[EARLY:])
+    send, keep = project_late(owners, head_index[None], pieces, out_weight, so_far)
     swap = [(0, 1), (1, 0)]
-    send, keep = project(head_index[None], gathered, out_weight)
     other = lax.ppermute(send, "head", swap)
     summed = (keep.astype(jnp.float32) + other.astype(jnp.float32)).astype(jnp.bfloat16)
     outs = summed.shape[1]
@@ -370,7 +422,7 @@
 def local(query_rows, key_rows, value_rows, rand_blocks, out_weight):
     head_count = query_rows.shape[1] // HD
     peers = lax.axis_size("seq")
-    if lax.axis_size("head") == 2 and head_count % peers == 0 and peers % 2 == 0:
+    if lax.axis_size("head") == 2 and head_count % peers == 0 and peers % 2 == 0 and peers > 2:
         return local_by_heads(query_rows, key_rows, value_rows, rand_blocks, out_weight)
     return local_by_rows(query_rows, key_rows, value_rows, rand_blocks, out_weight)
 

time: 176 us -> 124 us (0.70)
  waiting for transfers between devices: 127 us -> 78.1 us
  starting transfers between devices: 11 us -> 26.7 us
  between operations: 13.5 us -> 0.14 us
  Pallas kernels: 19.2 us -> 15.9 us
    all_gather x1 -> x0, waiting for transfers between devices: 72.6 us -> none  [local_by_heads(): gathered = lax.all_gather(attended, 'seq', axis=0)]
    ppermute x0 -> x14, waiting for transfers between devices: none -> 23.3 us  [the longest x6 19.7 us: local_by_heads(): behind = lax.ppermute(behind, 'seq', back)]
    ppermute x0 -> x14, starting transfers between devices: none -> 14.3 us  [the longest x6 12 us: local_by_heads(): behind = lax.ppermute(behind, 'seq', back)]
    pallas_call x3 -> x5, Pallas kernels: 19.2 us -> 15.9 us  [the longest x2 8.67 us: attend_head(): pl.pallas_call(functools.partial(attend_kernel, head), out_shape=jax.Shap...]
  transfers between devices with their start and end apart: 5 -> 18, of which waited for: 5 -> 12; matrix products, arithmetic and copies ran while one was open for 0% -> 0% of each run, Pallas kernels for 0% -> 6%
where the time goes in v2:
time: 124 us
  waiting for transfers between devices  78.1 us (63%)
  starting transfers between devices  26.7 us (22%)
  Pallas kernels  15.9 us (13%)
  local copies, waits for them, and re-layouts  1.67 us (1%)
  other arithmetic  1.24 us (1%)
    all_to_all x1, waiting for transfers between devices, local_by_heads(): lax.all_to_all(outgoing, 'seq', split_axis=0, concat_axis=0, tiled=True)  36.6 us
    ppermute x6, waiting for transfers between devices, local_by_heads(): behind = lax.ppermute(behind, 'seq', back)  19.7 us
    all_to_all x1, waiting for transfers between devices, local_by_heads(): lax.all_to_all(summed, 'seq', split_axis=0, concat_axis=0, tiled=True)  14.8 us
    ppermute x6, starting transfers between devices, local_by_heads(): behind = lax.ppermute(behind, 'seq', back)  12 us
    pallas_call x2, Pallas kernels, attend_head(): pl.pallas_call(functools.partial(attend_kernel, head), out_shape=jax.Shap...  8.67 us
    all_to_all x1, starting transfers between devices, local_by_heads(): lax.all_to_all(outgoing, 'seq', split_axis=0, concat_axis=0, tiled=True)  7.28 us
    all_to_all x1, starting transfers between devices, local_by_heads(): lax.all_to_all(summed, 'seq', split_axis=0, concat_axis=0, tiled=True)  5.03 us
    ppermute x1, waiting for transfers between devices, local_by_heads(): far[head, reach] = lax.ppermute(behind, 'seq', back)  3.47 us
  transfers between devices with their start and end apart: 18, of which 12 were waited for; matrix products, arithmetic and copies ran while one was open for 0% of the time, Pallas kernels for 6%

profile of v2, /device:TPU:0, one launch (start us, length us, event | category | flops | bytes accessed | tf_op | source)
XLA Modules:
  0.0 123.7 jit_solution(14085206679968936711)
XLA Ops:
  0.0 2.6 %shard_map.73 = bf16[8,3,128,256]{3,2,1,0:T(8,128)(2,1)} custom-call(bf16[128,2048]{1,0:T(8,128)(2,1)} %query_ref.1, bf16[128,2048]{1,0:T(8,128)(2,1)} %key_ref.1, bf16[128,2048]{1,0:T(8,128)(2,1)} %value_ref.1), custom_call_target="tpu_custom_call" | custom-call | bytes 3145728 | tf_op jit(solution)/shard_map/pallas_call | solution.py:230
  2.6 7.3 %all-to-all-start = ((bf16[8,3,128,256]{3,2,1,0:T(8,128)(2,1)}), bf16[8,3,128,256]{3,2,1,0:T(8,128)(2,1)}, u32[]{:S(2)}, u32[]{:S(2)}) async-start(bf16[8,3,128,256]{3,2,1,0:T(8,128)(2,1)} %shard_map.73), calls=%async_computation | async-start | bytes 3145728 | tf_op jit(solution)/shard_map/all_to_all | solution.py:379
  10.4 36.6 %all-to-all-done.rows_ref = bf16[8,3,128,256]{3,2,1,0:T(8,128)(2,1)} async-done(((bf16[8,3,128,256]{3,2,1,0:T(8,128)(2,1)}), bf16[8,3,128,256]{3,2,1,0:T(8,128)(2,1)}, u32[]{:S(2)}, u32[]{:S(2)}) %all-to-all-start) | async-done | bytes 1572896 | tf_op jit(solution)/shard_map/all_to_all | solution.py:379
  47.0 4.3 %shard_map.74.refs_0_ = bf16[1024,128]{1,0:T(8,128)(2,1)S(1)} custom-call(bf16[8,3,128,256]{3,2,1,0:T(8,128)(2,1)} %all-to-all-done.rows_ref, f32[2,8,1024]{2,1,0:T(8,128)S(1)} %broadcast_bitcast_fusion.bias_ref), custom_call_target="tpu_custom_call" | custom-call | flops 536870912 | bytes 1048576 | tf_op jit(solution)/shard_map/pallas_call | solution.py:266
  51.4 4.3 %shard_map.75.refs_1_ = bf16[1024,128]{1,0:T(8,128)(2,1)S(1)} custom-call(bf16[8,3,128,256]{3,2,1,0:T(8,128)(2,1)} %all-to-all-done.rows_ref, f32[2,8,1024]{2,1,0:T(8,128)S(1)} %broadcast_bitcast_fusion.bias_ref), custom_call_target="tpu_custom_call" | custom-call | flops 536870912 | bytes 1048576 | tf_op jit(solution)/shard_map/pallas_call | solution.py:266
  55.7 2.1 %collective-permute-start.3 = (bf16[1024,128]{1,0:T(8,128)(2,1)S(1)}, bf16[1024,128]{1,0:T(8,128)(2,1)S(1)}, u32[]{:S(2)}, u32[]{:S(2)}) collective-permute-start(bf16[1024,128]{1,0:T(8,128)(2,1)S(1)} %shard_map.75.refs_1_), channel_id=1, source_target_pairs={{4,0},{8,4},{12,8},{14,12},{10,14},{6,10},{2,6},{0,2},{5,1},{9,5},... | collective-permute-start | bytes 786440 | tf_op jit(solution)/shard_map/ppermute | solution.py:386
  57.9 2.0 %collective-permute-start.2 = (bf16[1024,128]{1,0:T(8,128)(2,1)S(1)}, bf16[1024,128]{1,0:T(8,128)(2,1)}, u32[]{:S(2)}, u32[]{:S(2)}) collective-permute-start(bf16[1024,128]{1,0:T(8,128)(2,1)S(1)} %shard_map.74.refs_0_), channel_id=1, source_target_pairs={{4,0},{8,4},{12,8},{14,12},{10,14},{6,10},{2,6},{0,2},{5,1},{9,5},... | collective-permute-start | bytes 786440 | tf_op jit(solution)/shard_map/ppermute | solution.py:386
  59.9 5.2 %collective-permute-done.3.refs_5_ = bf16[1024,128]{1,0:T(8,128)(2,1)S(1)} collective-permute-done((bf16[1024,128]{1,0:T(8,128)(2,1)S(1)}, bf16[1024,128]{1,0:T(8,128)(2,1)S(1)}, u32[]{:S(2)}, u32[]{:S(2)}) %collective-permute-start.3) | collective-permute-done | bytes 262176 | tf_op jit(solution)/shard_map/ppermute | solution.py:386
  65.1 2.0 %collective-permute-start.7 = (bf16[1024,128]{1,0:T(8,128)(2,1)S(1)}, bf16[1024,128]{1,0:T(8,128)(2,1)}, u32[]{:S(2)}, u32[]{:S(2)}) collective-permute-start(bf16[1024,128]{1,0:T(8,128)(2,1)S(1)} %collective-permute-done.3.refs_5_), channel_id=1, source_target_pairs={{4,0},{8,4},{12,8},{14,12},{10,14},{6,10},{2,6},{0,2},{5,1},{9,5},... | collective-permute-start | bytes 786440 | tf_op jit(solution)/shard_map/ppermute | solution.py:386
  67.2 3.6 %collective-permute-done.2.refs_4_ = bf16[1024,128]{1,0:T(8,128)(2,1)} collective-permute-done((bf16[1024,128]{1,0:T(8,128)(2,1)S(1)}, bf16[1024,128]{1,0:T(8,128)(2,1)}, u32[]{:S(2)}, u32[]{:S(2)}) %collective-permute-start.2) | collective-permute-done | bytes 262176 | tf_op jit(solution)/shard_map/ppermute | solution.py:386
  70.8 2.0 %collective-permute-start.6 = (bf16[1024,128]{1,0:T(8,128)(2,1)}, bf16[1024,128]{1,0:T(8,128)(2,1)}, u32[]{:S(2)}, u32[]{:S(2)}) collective-permute-start(bf16[1024,128]{1,0:T(8,128)(2,1)} %collective-permute-done.2.refs_4_), channel_id=1, source_target_pairs={{4,0},{8,4},{12,8},{14,12},{10,14},{6,10},{2,6},{0,2},{5,1},{9,5},... | collective-permute-start | bytes 786440 | tf_op jit(solution)/shard_map/ppermute | solution.py:386
  72.8 3.6 %collective-permute-done.7.refs_9_ = bf16[1024,128]{1,0:T(8,128)(2,1)} collective-permute-done((bf16[1024,128]{1,0:T(8,128)(2,1)S(1)}, bf16[1024,128]{1,0:T(8,128)(2,1)}, u32[]{:S(2)}, u32[]{:S(2)}) %collective-permute-start.7) | collective-permute-done | bytes 262176 | tf_op jit(solution)/shard_map/ppermute | solution.py:386
  76.4 2.0 %collective-permute-start.11 = (bf16[1024,128]{1,0:T(8,128)(2,1)}, bf16[1024,128]{1,0:T(8,128)(2,1)S(1)}, u32[]{:S(2)}, u32[]{:S(2)}) collective-permute-start(bf16[1024,128]{1,0:T(8,128)(2,1)} %collective-permute-done.7.refs_9_), channel_id=1, source_target_pairs={{4,0},{8,4},{12,8},{14,12},{10,14},{6,10},{2,6},{0,2},{5,1},{9,5},... | collective-permute-start | bytes 786440 | tf_op jit(solution)/shard_map/ppermute | solution.py:386
  78.5 3.6 %collective-permute-done.6.refs_8_ = bf16[1024,128]{1,0:T(8,128)(2,1)} collective-permute-done((bf16[1024,128]{1,0:T(8,128)(2,1)}, bf16[1024,128]{1,0:T(8,128)(2,1)}, u32[]{:S(2)}, u32[]{:S(2)}) %collective-permute-start.6) | collective-permute-done | bytes 262176 | tf_op jit(solution)/shard_map/ppermute | solution.py:386
  82.0 2.0 %collective-permute-start.10 = (bf16[1024,128]{1,0:T(8,128)(2,1)}, bf16[1024,128]{1,0:T(8,128)(2,1)S(1)}, u32[]{:S(2)}, u32[]{:S(2)}) collective-permute-start(bf16[1024,128]{1,0:T(8,128)(2,1)} %collective-permute-done.6.refs_8_), channel_id=1, source_target_pairs={{4,0},{8,4},{12,8},{14,12},{10,14},{6,10},{2,6},{0,2},{5,1},{9,5},... | collective-permute-start | bytes 786440 | tf_op jit(solution)/shard_map/ppermute | solution.py:386
  84.1 3.5 %collective-permute-done.11.refs_1_ = bf16[1024,128]{1,0:T(8,128)(2,1)S(1)} collective-permute-done((bf16[1024,128]{1,0:T(8,128)(2,1)}, bf16[1024,128]{1,0:T(8,128)(2,1)S(1)}, u32[]{:S(2)}, u32[]{:S(2)}) %collective-permute-start.11) | collective-permute-done | bytes 262176 | tf_op jit(solution)/shard_map/ppermute | solution.py:386
  87.5 2.0 %collective-permute-start.13 = (bf16[1024,128]{1,0:T(8,128)(2,1)S(1)}, bf16[1024,128]{1,0:T(8,128)(2,1)S(1)}, u32[]{:S(2)}, u32[]{:S(2)}) collective-permute-start(bf16[1024,128]{1,0:T(8,128)(2,1)S(1)} %collective-permute-done.11.refs_1_), channel_id=1, source_target_pairs={{4,0},{8,4},{12,8},{14,12},{10,14},{6,10},{2,6},{0,2},{5,1},{9,5},... | collective-permute-start | bytes 786440 | tf_op jit(solution)/shard_map/ppermute | solution.py:392
  89.6 3.3 %shard_map.76.total_ref = f32[1024,512]{1,0:T(8,128)S(1)} custom-call(s32[6]{0:T(128)S(1)} %compare_select_fusion.4.owner_ref, bf16[512,2048]{1,0:T(8,128)(2,1)S(1)} %copy-done.1, bf16[1024,128]{1,0:T(8,128)(2,1)S(1)} %shard_map.74.refs_0_, bf16[1024,128]{1,0:T(8,128)(2,1)S(1)} %shard_map.75.refs_1_, bf16[1024,128]{1,0:T(8,128)(2,1)S(1)} %collective-permute-done.refs_2_, ...), custom_call_target="tpu_custom_call" | custom-call | flops 1610612736 | bytes 6815744 | tf_op jit(solution)/shard_map/pallas_call | solution.py:321
  93.2 3.5 %collective-permute-done.13.refs_3_ = bf16[1024,128]{1,0:T(8,128)(2,1)S(1)} collective-permute-done((bf16[1024,128]{1,0:T(8,128)(2,1)S(1)}, bf16[1024,128]{1,0:T(8,128)(2,1)S(1)}, u32[]{:S(2)}, u32[]{:S(2)}) %collective-permute-start.13) | collective-permute-done | bytes 262176 | tf_op jit(solution)/shard_map/ppermute | solution.py:392
  96.6 1.3 %shard_map.77 = (bf16[1024,256]{1,0:T(8,128)(2,1)S(1)}, bf16[1024,256]{1,0:T(8,128)(2,1)S(1)}) custom-call(s32[2]{0:T(128)S(1)} %compare_select_fusion.5.owner_ref, s32[1]{0:T(128)} %bitcast.side_ref, bf16[512,2048]{1,0:T(8,128)(2,1)S(1)} %copy-done.1, f32[1024,512]{1,0:T(8,128)S(1)} %shard_map.76.total_ref, ...), custom_call_target="tpu_custom_call" | custom-call | flops 536870912 | bytes 4718592 | tf_op jit(solution)/shard_map/pallas_call | solution.py:337
  98.0 1.9 %collective-permute-done.14 = bf16[1024,256]{1,0:T(8,128)(2,1)S(1)} collective-permute-done((bf16[1024,256]{1,0:T(8,128)(2,1)S(1)}, bf16[1024,256]{1,0:T(8,128)(2,1)S(1)}, u32[]{:S(2)}, u32[]{:S(2)}) %collective-permute-start.14) | collective-permute-done | bytes 524320 | tf_op jit(solution)/shard_map/ppermute | solution.py:406
  100.9 5.0 %all-to-all-start.1 = ((bf16[8,128,256]{2,1,0:T(8,128)(2,1)}), bf16[8,128,256]{2,1,0:T(8,128)(2,1)S(1)}, u32[]{:S(2)}, u32[]{:S(2)}) async-start(bf16[8,128,256]{2,1,0:T(8,128)(2,1)} %bitcast.3), calls=%async_computation.1 | async-start | bytes 1048576 | tf_op jit(solution)/shard_map/all_to_all | solution.py:410
  105.9 14.8 %all-to-all-done.1 = bf16[8,128,256]{2,1,0:T(8,128)(2,1)S(1)} async-done(((bf16[8,128,256]{2,1,0:T(8,128)(2,1)}), bf16[8,128,256]{2,1,0:T(8,128)(2,1)S(1)}, u32[]{:S(2)}, u32[]{:S(2)}) %all-to-all-start.1) | async-done | bytes 524320 | tf_op jit(solution)/shard_map/all_to_all | solution.py:410
  120.8 1.5 %collective-permute-done.15 = bf16[4,128,256]{2,1,0:T(8,128)(2,1)S(1)} collective-permute-done((bf16[4,128,256]{2,1,0:T(8,128)(2,1)S(1)}, bf16[4,128,256]{2,1,0:T(8,128)(2,1)S(1)}, u32[]{:S(2)}, u32[]{:S(2)}) %collective-permute-start.15) | collective-permute-done | bytes 262176 | tf_op jit(solution)/shard_map/ppermute | solution.py:414
  (41 shorter events, 3.7 us)
Async XLA Ops:
  0.0 9.9 %copy-start = (s32[8,32,3]{1,0,2:T(8,128)S(1)}, s32[8,32,3]{1,0,2:T(8,128)}, u32[]{:S(2)}) copy-start(s32[8,32,3]{1,0,2:T(8,128)} %param.10) | copy-start | bytes 9220
  2.6 44.4 %all-to-all-start = ((bf16[8,3,128,256]{3,2,1,0:T(8,128)(2,1)}), bf16[8,3,128,256]{3,2,1,0:T(8,128)(2,1)}, u32[]{:S(2)}, u32[]{:S(2)}) async-start(bf16[8,3,128,256]{3,2,1,0:T(8,128)(2,1)} %shard_map.73), calls=%async_computation | async-start | bytes 3145728 | tf_op jit(solution)/shard_map/all_to_all | solution.py:379
  9.9 68.5 %copy-start.3 = (s32[6]{0:T(128)S(1)}, s32[6]{0:T(128)}, u32[]{:S(2)}) copy-start(s32[6]{0:T(128)} %constant.102) | copy-start | bytes 76
  9.9 79.6 %copy-start.2 = (s32[2]{0:T(128)S(1)}, s32[2]{0:T(128)}, u32[]{:S(2)}) copy-start(s32[2]{0:T(128)} %constant.101) | copy-start | bytes 28
  9.9 79.6 %copy-start.1 = (bf16[512,2048]{1,0:T(8,128)(2,1)S(1)}, bf16[512,2048]{1,0:T(8,128)(2,1)}, u32[]{:S(2)}) copy-start(bf16[512,2048]{1,0:T(8,128)(2,1)} %weight_ref.3) | copy-start | bytes 6291460
  51.3 8.5 %collective-permute-start = (bf16[1024,128]{1,0:T(8,128)(2,1)S(1)}, bf16[1024,128]{1,0:T(8,128)(2,1)S(1)}, u32[]{:S(2)}, u32[]{:S(2)}) collective-permute-start(bf16[1024,128]{1,0:T(8,128)(2,1)S(1)} %shard_map.74.refs_0_), channel_id=1, source_target_pairs={{0,4},{4,8},{8,12},{12,14},{14,10},{10,6},{6,2},{2,0},{1,5},{5,9},... | collective-permute-start | bytes 786440 | tf_op jit(solution)/shard_map/ppermute | solution.py:385
  55.7 9.3 %collective-permute-start.3 = (bf16[1024,128]{1,0:T(8,128)(2,1)S(1)}, bf16[1024,128]{1,0:T(8,128)(2,1)S(1)}, u32[]{:S(2)}, u32[]{:S(2)}) collective-permute-start(bf16[1024,128]{1,0:T(8,128)(2,1)S(1)} %shard_map.75.refs_1_), channel_id=1, source_target_pairs={{4,0},{8,4},{12,8},{14,12},{10,14},{6,10},{2,6},{0,2},{5,1},{9,5},... | collective-permute-start | bytes 786440 | tf_op jit(solution)/shard_map/ppermute | solution.py:386
  57.8 9.4 %collective-permute-start.1 = (bf16[1024,128]{1,0:T(8,128)(2,1)S(1)}, bf16[1024,128]{1,0:T(8,128)(2,1)}, u32[]{:S(2)}, u32[]{:S(2)}) collective-permute-start(bf16[1024,128]{1,0:T(8,128)(2,1)S(1)} %shard_map.75.refs_1_), channel_id=1, source_target_pairs={{0,4},{4,8},{8,12},{12,14},{14,10},{10,6},{6,2},{2,0},{1,5},{5,9},... | collective-permute-start | bytes 786440 | tf_op jit(solution)/shard_map/ppermute | solution.py:385
  57.9 12.9 %collective-permute-start.2 = (bf16[1024,128]{1,0:T(8,128)(2,1)S(1)}, bf16[1024,128]{1,0:T(8,128)(2,1)}, u32[]{:S(2)}, u32[]{:S(2)}) collective-permute-start(bf16[1024,128]{1,0:T(8,128)(2,1)S(1)} %shard_map.74.refs_0_), channel_id=1, source_target_pairs={{4,0},{8,4},{12,8},{14,12},{10,14},{6,10},{2,6},{0,2},{5,1},{9,5},... | collective-permute-start | bytes 786440 | tf_op jit(solution)/shard_map/ppermute | solution.py:386
  59.8 12.9 %collective-permute-start.4 = (bf16[1024,128]{1,0:T(8,128)(2,1)S(1)}, bf16[1024,128]{1,0:T(8,128)(2,1)}, u32[]{:S(2)}, u32[]{:S(2)}) collective-permute-start(bf16[1024,128]{1,0:T(8,128)(2,1)S(1)} %collective-permute-done.refs_2_), channel_id=1, source_target_pairs={{0,4},{4,8},{8,12},{12,14},{14,10},{10,6},{6,2},{2,0},{1,5},{5,9},... | collective-permute-start | bytes 786440 | tf_op jit(solution)/shard_map/ppermute | solution.py:385
  65.1 11.3 %collective-permute-start.7 = (bf16[1024,128]{1,0:T(8,128)(2,1)S(1)}, bf16[1024,128]{1,0:T(8,128)(2,1)}, u32[]{:S(2)}, u32[]{:S(2)}) collective-permute-start(bf16[1024,128]{1,0:T(8,128)(2,1)S(1)} %collective-permute-done.3.refs_5_), channel_id=1, source_target_pairs={{4,0},{8,4},{12,8},{14,12},{10,14},{6,10},{2,6},{0,2},{5,1},{9,5},... | collective-permute-start | bytes 786440 | tf_op jit(solution)/shard_map/ppermute | solution.py:386
  67.2 11.2 %collective-permute-start.5 = (bf16[1024,128]{1,0:T(8,128)(2,1)}, bf16[1024,128]{1,0:T(8,128)(2,1)}, u32[]{:S(2)}, u32[]{:S(2)}) collective-permute-start(bf16[1024,128]{1,0:T(8,128)(2,1)} %collective-permute-done.1.refs_3_), channel_id=1, source_target_pairs={{0,4},{4,8},{8,12},{12,14},{14,10},{10,6},{6,2},{2,0},{1,5},{5,9},... | collective-permute-start | bytes 786440 | tf_op jit(solution)/shard_map/ppermute | solution.py:385
  70.8 11.2 %collective-permute-start.6 = (bf16[1024,128]{1,0:T(8,128)(2,1)}, bf16[1024,128]{1,0:T(8,128)(2,1)}, u32[]{:S(2)}, u32[]{:S(2)}) collective-permute-start(bf16[1024,128]{1,0:T(8,128)(2,1)} %collective-permute-done.2.refs_4_), channel_id=1, source_target_pairs={{4,0},{8,4},{12,8},{14,12},{10,14},{6,10},{2,6},{0,2},{5,1},{9,5},... | collective-permute-start | bytes 786440 | tf_op jit(solution)/shard_map/ppermute | solution.py:386
  72.8 11.2 %collective-permute-start.8 = (bf16[1024,128]{1,0:T(8,128)(2,1)}, bf16[1024,128]{1,0:T(8,128)(2,1)}, u32[]{:S(2)}, u32[]{:S(2)}) collective-permute-start(bf16[1024,128]{1,0:T(8,128)(2,1)} %collective-permute-done.4.refs_6_), channel_id=1, source_target_pairs={{0,4},{4,8},{8,12},{12,14},{14,10},{10,6},{6,2},{2,0},{1,5},{5,9},... | collective-permute-start | bytes 786440 | tf_op jit(solution)/shard_map/ppermute | solution.py:385
  76.4 11.1 %collective-permute-start.11 = (bf16[1024,128]{1,0:T(8,128)(2,1)}, bf16[1024,128]{1,0:T(8,128)(2,1)S(1)}, u32[]{:S(2)}, u32[]{:S(2)}) collective-permute-start(bf16[1024,128]{1,0:T(8,128)(2,1)} %collective-permute-done.7.refs_9_), channel_id=1, source_target_pairs={{4,0},{8,4},{12,8},{14,12},{10,14},{6,10},{2,6},{0,2},{5,1},{9,5},... | collective-permute-start | bytes 786440 | tf_op jit(solution)/shard_map/ppermute | solution.py:386
  78.4 11.1 %collective-permute-start.9 = (bf16[1024,128]{1,0:T(8,128)(2,1)}, bf16[1024,128]{1,0:T(8,128)(2,1)S(1)}, u32[]{:S(2)}, u32[]{:S(2)}) collective-permute-start(bf16[1024,128]{1,0:T(8,128)(2,1)} %collective-permute-done.5.refs_7_), channel_id=1, source_target_pairs={{0,4},{4,8},{8,12},{12,14},{14,10},{10,6},{6,2},{2,0},{1,5},{5,9},... | collective-permute-start | bytes 786440 | tf_op jit(solution)/shard_map/ppermute | solution.py:385
  82.0 11.1 %collective-permute-start.10 = (bf16[1024,128]{1,0:T(8,128)(2,1)}, bf16[1024,128]{1,0:T(8,128)(2,1)S(1)}, u32[]{:S(2)}, u32[]{:S(2)}) collective-permute-start(bf16[1024,128]{1,0:T(8,128)(2,1)} %collective-permute-done.6.refs_8_), channel_id=1, source_target_pairs={{4,0},{8,4},{12,8},{14,12},{10,14},{6,10},{2,6},{0,2},{5,1},{9,5},... | collective-permute-start | bytes 786440 | tf_op jit(solution)/shard_map/ppermute | solution.py:386
  84.0 9.1 %collective-permute-start.12 = (bf16[1024,128]{1,0:T(8,128)(2,1)}, bf16[1024,128]{1,0:T(8,128)(2,1)S(1)}, u32[]{:S(2)}, u32[]{:S(2)}) collective-permute-start(bf16[1024,128]{1,0:T(8,128)(2,1)} %collective-permute-done.8.refs_10_), channel_id=1, source_target_pairs={{0,4},{4,8},{8,12},{12,14},{14,10},{10,6},{6,2},{2,0},{1,5},{5,9},... | collective-permute-start | bytes 786440 | tf_op jit(solution)/shard_map/ppermute | solution.py:390
  87.5 9.1 %collective-permute-start.13 = (bf16[1024,128]{1,0:T(8,128)(2,1)S(1)}, bf16[1024,128]{1,0:T(8,128)(2,1)S(1)}, u32[]{:S(2)}, u32[]{:S(2)}) collective-permute-start(bf16[1024,128]{1,0:T(8,128)(2,1)S(1)} %collective-permute-done.11.refs_1_), channel_id=1, source_target_pairs={{4,0},{8,4},{12,8},{14,12},{10,14},{6,10},{2,6},{0,2},{5,1},{9,5},... | collective-permute-start | bytes 786440 | tf_op jit(solution)/shard_map/ppermute | solution.py:392
  98.0 2.0 %collective-permute-start.14 = (bf16[1024,256]{1,0:T(8,128)(2,1)S(1)}, bf16[1024,256]{1,0:T(8,128)(2,1)S(1)}, u32[]{:S(2)}, u32[]{:S(2)}) collective-permute-start(bf16[1024,256]{1,0:T(8,128)(2,1)S(1)} %get-tuple-element.8), channel_id=1, source_target_pairs={{0,1},{1,0},{2,3},{3,2},{4,5},{5,4},{6,7},{7,6},{8,9},{9,8},{10,11... | collective-permute-start | bytes 1572872 | tf_op jit(solution)/shard_map/ppermute | solution.py:406
  100.9 19.8 %all-to-all-start.1 = ((bf16[8,128,256]{2,1,0:T(8,128)(2,1)}), bf16[8,128,256]{2,1,0:T(8,128)(2,1)S(1)}, u32[]{:S(2)}, u32[]{:S(2)}) async-start(bf16[8,128,256]{2,1,0:T(8,128)(2,1)} %bitcast.3), calls=%async_computation.1 | async-start | bytes 1048576 | tf_op jit(solution)/shard_map/all_to_all | solution.py:410
  120.7 1.6 %collective-permute-start.15 = (bf16[4,128,256]{2,1,0:T(8,128)(2,1)S(1)}, bf16[4,128,256]{2,1,0:T(8,128)(2,1)S(1)}, u32[]{:S(2)}, u32[]{:S(2)}) collective-permute-start(bf16[4,128,256]{2,1,0:T(8,128)(2,1)S(1)} %dynamic-slice_bitcast_fusion), channel_id=1, source_target_pairs={{0,1},{1,0},{2,3},{3,2},{4,5},{5,4},{6,7},{7,6},{8,9},{9,8},{10,11... | collective-permute-start | bytes 786440 | tf_op jit(solution)/shard_map/ppermute | solution.py:414

commit v3 on v2

--- a/solution.py
+++ b/solution.py
@@ -14,6 +14,9 @@
 VMEM = 20 << 20
 TILE = 256
 EARLY = 6
+SEND_ORDER = (4, 6, 5, 7, 2, 3, 1)
+SCALARS = pl.BlockSpec(memory_space=pltpu.SMEM)
+ARRAY = pl.BlockSpec(memory_space=pltpu.VMEM)
 
 
 def broadcast(block, axis, owner):
@@ -218,18 +221,20 @@
 
 
 def spread_kernel(query_ref, key_ref, value_ref, out_ref):
-    peers, _, _, width = out_ref.shape
+    peers, heads, _, _, width = out_ref.shape
     for which, ref in enumerate((query_ref, key_ref, value_ref)):
         for peer in range(peers):
-            out_ref[peer, which] = ref[:, peer * width : (peer + 1) * width]
+            for head in range(heads):
+                start = (peer * heads + head) * width
+                out_ref[peer, head, which] = ref[:, start : start + width]
 
 
 def spread(query_rows, key_rows, value_rows, peers):
     tokens, features = query_rows.shape
-    width = features // peers
+    heads = features // HD // peers
     return pl.pallas_call(
         spread_kernel,
-        out_shape=jax.ShapeDtypeStruct((peers, 3, tokens, width), query_rows.dtype),
+        out_shape=jax.ShapeDtypeStruct((peers, heads, 3, tokens, HD), query_rows.dtype),
         cost_estimate=pl.CostEstimate(
             flops=0, bytes_accessed=12 * tokens * features, transcendentals=0
         ),
@@ -237,34 +242,34 @@
 
 
 def attend_kernel(head, rows_ref, bias_ref, out_ref):
-    groups, _, tokens, _ = rows_ref.shape
-    total = groups * tokens
-    blocks = total // BLK
+    groups = rows_ref.shape[0]
+    tokens = rows_ref.shape[3]
     factor = math.log2(math.e) / math.sqrt(HD)
-    lanes = slice(head * HD, (head + 1) * HD)
-    query = rows_ref[:, 0, :, lanes].reshape(total, HD)
-    keys = rows_ref[:, 1, :, lanes].reshape(total, HD)
-    values = rows_ref[:, 2, :, lanes].reshape(total, HD)
-    for block in range(blocks):
-        rows = slice(block * BLK, (block + 1) * BLK)
+    keys = jnp.concatenate([rows_ref[group, head, 1] for group in range(groups)], axis=0)
+    values = jnp.concatenate([rows_ref[group, head, 2] for group in range(groups)], axis=0)
+    for group in range(groups):
         scores = lax.dot_general(
-            query[rows], keys, (((1,), (1,)), ((), ())), preferred_element_type=jnp.float32
+            rows_ref[group, head, 0],
+            keys,
+            (((1,), (1,)), ((), ())),
+            preferred_element_type=jnp.float32,
         )
-        scores = scores * factor + bias_ref[head, block : block + 1, :]
+        scores = scores * factor + bias_ref[head, group : group + 1, :]
         peak = jnp.max(scores, axis=1, keepdims=True)
         terms = jnp.exp2(scores - peak)
         denom = jnp.sum(terms, axis=1, keepdims=True)
         mixed = jnp.dot(
             terms.astype(jnp.bfloat16), values, preferred_element_type=jnp.float32
         )
-        out_ref[rows, :] = (mixed / denom).astype(out_ref.dtype)
+        out_ref[group * tokens : (group + 1) * tokens, :] = (mixed / denom).astype(out_ref.dtype)
 
 
 def attend_head(rows, bias, head):
-    groups, _, tokens, _ = rows.shape
+    groups, _, _, tokens, _ = rows.shape
     total = groups * tokens
     return pl.pallas_call(
         functools.partial(attend_kernel, head),
+        in_specs=[ARRAY] * 2,
         out_shape=jax.ShapeDtypeStruct((total, HD), rows.dtype),
         compiler_params=pltpu.CompilerParams(vmem_limit_bytes=VMEM),
         cost_estimate=pl.CostEstimate(
@@ -311,10 +316,6 @@
         keep_ref[tile, :] = jnp.where(first, low, high)
 
 
-SCALARS = pl.BlockSpec(memory_space=pltpu.SMEM)
-ARRAY = pl.BlockSpec(memory_space=pltpu.VMEM)
-
-
 def project_early(owners, pieces, weight):
     total, width = pieces[0].shape
     outs = weight.shape[0]
@@ -345,6 +346,51 @@
             transcendentals=0,
         ),
     )(owners, side, weight, so_far, *pieces)
+
+
+def add_kernel(row_ref, keep_ref, other_ref, *out_refs):
+    tokens = out_refs[0].shape[0]
+    for apart, out_ref in enumerate(out_refs):
+        rows = pl.ds(pl.multiple_of((row_ref[0] ^ apart) * tokens, tokens), tokens)
+        out_ref[...] = (
+            keep_ref[rows, :].astype(jnp.float32) + other_ref[rows, :].astype(jnp.float32)
+        ).astype(out_ref.dtype)
+
+
+def add_and_part(row, keep, other, parts):
+    total, width = keep.shape
+    return pl.pallas_call(
+        add_kernel,
+        in_specs=[SCALARS] + [ARRAY] * 2,
+        out_shape=[jax.ShapeDtypeStruct((total // parts, width), keep.dtype)] * parts,
+        compiler_params=pltpu.CompilerParams(vmem_limit_bytes=VMEM),
+        cost_estimate=pl.CostEstimate(
+            flops=total * width, bytes_accessed=6 * total * width, transcendentals=0
+        ),
+    )(row[None], keep, other)
+
+
+def assemble_kernel(seq_ref, head_ref, near_ref, crossed_ref, *refs):
+    *arrived, out_ref = refs
+    reach = len(arrived) // 2
+    width = arrived[0].shape[1]
+    near = near_ref[0] == 1
+    for i in range(reach):
+        spot = 2 * ((seq_ref[0] % reach) ^ i)
+        mine = pl.ds(pl.multiple_of((spot + head_ref[0]) * width, width), width)
+        theirs = pl.ds(pl.multiple_of((spot + 1 - head_ref[0]) * width, width), width)
+        out_ref[:, mine] = jnp.where(near, arrived[i][...], arrived[i + reach][...])
+        out_ref[:, theirs] = crossed_ref[i]
+
+
+def assemble(seq_index, head_index, near, crossed, arrived):
+    tokens, width = arrived[0].shape
+    return pl.pallas_call(
+        assemble_kernel,
+        in_specs=[SCALARS] * 3 + [ARRAY] * (1 + len(arrived)),
+        out_shape=jax.ShapeDtypeStruct((tokens, width * len(arrived)), crossed.dtype),
+        compiler_params=pltpu.CompilerParams(vmem_limit_bytes=VMEM),
+    )(seq_index[None], head_index[None], near[None], crossed, *arrived)
 
 
 def key_bias(rand_blocks, head_start, heads):
@@ -403,26 +449,22 @@
     owners, pieces = gather_args(steps[EARLY:])
     send, keep = project_late(owners, head_index[None], pieces, out_weight, so_far)
     swap = [(0, 1), (1, 0)]
-    other = lax.ppermute(send, "head", swap)
-    summed = (keep.astype(jnp.float32) + other.astype(jnp.float32)).astype(jnp.bfloat16)
-    outs = summed.shape[1]
-    summed = summed.reshape(peers, tokens, outs)
-    arrived = lax.all_to_all(summed, "seq", split_axis=0, concat_axis=0, tiled=True)
-    arrived = arrived.reshape(2, peers // 2, tokens, outs)
-    mine = lax.dynamic_index_in_dim(arrived, head_index, 0, keepdims=False)
-    theirs = lax.dynamic_index_in_dim(arrived, 1 - head_index, 0, keepdims=False)
-    crossed = lax.ppermute(theirs, "head", swap)
-    first = head_index == 0
-    pair = jnp.stack(
-        [jnp.where(first, mine, crossed), jnp.where(first, crossed, mine)], axis=1
-    )
-    return pair.transpose(2, 0, 1, 3).reshape(tokens, features)
+    parts = add_and_part(seq_index, keep, lax.ppermute(send, "head", swap), peers)
+    arrived = {0: parts[0]}
+    for apart in SEND_ORDER:
+        pairs = [(i, i ^ apart) for i in range(peers)]
+        arrived[apart] = lax.ppermute(parts[apart], "seq", pairs)
+    near = (seq_index // reach == head_index).astype(jnp.int32)
+    theirs = [jnp.where(near == 1, arrived[i + reach], arrived[i]) for i in range(reach)]
+    crossed = lax.ppermute(jnp.stack(theirs), "head", swap)
+    return assemble(seq_index, head_index, near, crossed, [arrived[i] for i in range(peers)])
 
 
 def local(query_rows, key_rows, value_rows, rand_blocks, out_weight):
-    head_count = query_rows.shape[1] // HD
+    tokens, features = query_rows.shape
     peers = lax.axis_size("seq")
-    if lax.axis_size("head") == 2 and head_count % peers == 0 and peers % 2 == 0 and peers > 2:
+    even = features // HD % peers == 0
+    if tokens == BLK and peers == 8 and lax.axis_size("head") == 2 and even:
         return local_by_heads(query_rows, key_rows, value_rows, rand_blocks, out_weight)
     return local_by_rows(query_rows, key_rows, value_rows, rand_blocks, out_weight)
 

time: 124 us -> 120 us (0.968)
  waiting for transfers between devices: 78.1 us -> 68.9 us
  starting transfers between devices: 26.7 us -> 32.8 us
  local copies, waits for them, and re-layouts: 1.67 us -> 0.35 us
    all_to_all x1 -> x0, waiting for transfers between devices: 14.8 us -> none  [local_by_heads(): lax.all_to_all(summed, 'seq', split_axis=0, concat_axis=0, tiled=True)]
    ppermute x2 -> x9, starting transfers between devices: 0.14 us -> 11.3 us  [the longest x7 11.1 us: local_by_heads(): arrived[apart] = lax.ppermute(parts[apart], 'seq', pairs)]
    ppermute x2 -> x9, waiting for transfers between devices: 3.41 us -> 9.01 us  [the longest x7 5.6 us: local_by_heads(): arrived[apart] = lax.ppermute(parts[apart], 'seq', pairs)]
    all_to_all x1 -> x0, starting transfers between devices: 5.03 us -> none  [local_by_heads(): lax.all_to_all(summed, 'seq', split_axis=0, concat_axis=0, tiled=True)]
    pallas_call x3 -> x5, Pallas kernels: 11.3 us -> 12.4 us  [the longest x2 8.67 us: attend_head(): pl.pallas_call(functools.partial(attend_kernel, head), in_specs=[ARRAY] *...]
  transfers between devices with their start and end apart: 18 -> 24, of which waited for: 12 -> 15; matrix products, arithmetic and copies ran while one was open for 0% -> 0% of each run, Pallas kernels for 6% -> 6%
where the time goes in v3:
time: 120 us
  waiting for transfers between devices  68.9 us (57%)
  starting transfers between devices  32.8 us (27%)
  Pallas kernels  17 us (14%)
    all_to_all x1, waiting for transfers between devices, local_by_heads(): lax.all_to_all(outgoing, 'seq', split_axis=0, concat_axis=0, tiled=True)  36.6 us
    ppermute x6, waiting for transfers between devices, local_by_heads(): behind = lax.ppermute(behind, 'seq', back)  19.7 us
    ppermute x6, starting transfers between devices, local_by_heads(): behind = lax.ppermute(behind, 'seq', back)  12.1 us
    ppermute x7, starting transfers between devices, local_by_heads(): arrived[apart] = lax.ppermute(parts[apart], 'seq', pairs)  11.1 us
    pallas_call x2, Pallas kernels, attend_head(): pl.pallas_call(functools.partial(attend_kernel, head), in_specs=[ARRAY] *...  8.67 us
    all_to_all x1, starting transfers between devices, local_by_heads(): lax.all_to_all(outgoing, 'seq', split_axis=0, concat_axis=0, tiled=True)  7.28 us
    ppermute x7, waiting for transfers between devices, local_by_heads(): arrived[apart] = lax.ppermute(parts[apart], 'seq', pairs)  5.6 us
    ppermute x1, waiting for transfers between devices, local_by_heads(): far[head, reach] = lax.ppermute(behind, 'seq', back)  3.47 us
  transfers between devices with their start and end apart: 24, of which 15 were waited for; matrix products, arithmetic and copies ran while one was open for 0% of the time, Pallas kernels for 6%

profile of v3, /device:TPU:0, one launch (start us, length us, event | category | flops | bytes accessed | tf_op | source)
XLA Modules:
  0.0 119.5 jit_solution(11206311155357168987)
XLA Ops:
  0.0 2.8 %shard_map.73 = bf16[8,2,3,128,128]{4,3,2,1,0:T(8,128)(2,1)} custom-call(bf16[128,2048]{1,0:T(8,128)(2,1)} %query_ref.1, bf16[128,2048]{1,0:T(8,128)(2,1)} %key_ref.1, bf16[128,2048]{1,0:T(8,128)(2,1)} %value_ref.1), custom_call_target="tpu_custom_call" | custom-call | bytes 3145728 | tf_op jit(solution)/shard_map/pallas_call | solution.py:235
  2.8 7.3 %all-to-all-start = ((bf16[8,2,3,128,128]{4,3,2,1,0:T(8,128)(2,1)}), bf16[8,2,3,128,128]{4,3,2,1,0:T(8,128)(2,1)}, u32[]{:S(2)}, u32[]{:S(2)}) async-start(bf16[8,2,3,128,128]{4,3,2,1,0:T(8,128)(2,1)} %shard_map.73), calls=%async_computation | async-start | bytes 3145728 | tf_op jit(solution)/shard_map/all_to_all | solution.py:425
  10.6 36.6 %all-to-all-done.rows_ref = bf16[8,2,3,128,128]{4,3,2,1,0:T(8,128)(2,1)} async-done(((bf16[8,2,3,128,128]{4,3,2,1,0:T(8,128)(2,1)}), bf16[8,2,3,128,128]{4,3,2,1,0:T(8,128)(2,1)}, u32[]{:S(2)}, u32[]{:S(2)}) %all-to-all-start) | async-done | bytes 1572896 | tf_op jit(solution)/shard_map/all_to_all | solution.py:425
  47.2 4.3 %shard_map.74.refs_0_ = bf16[1024,128]{1,0:T(8,128)(2,1)S(1)} custom-call(bf16[8,2,3,128,128]{4,3,2,1,0:T(8,128)(2,1)} %all-to-all-done.rows_ref, f32[2,8,1024]{2,1,0:T(8,128)S(1)} %broadcast_bitcast_fusion.bias_ref), custom_call_target="tpu_custom_call" | custom-call | flops 536870912 | bytes 1048576 | tf_op jit(solution)/shard_map/pallas_call | solution.py:270
  51.6 4.3 %shard_map.75.refs_1_ = bf16[1024,128]{1,0:T(8,128)(2,1)S(1)} custom-call(bf16[8,2,3,128,128]{4,3,2,1,0:T(8,128)(2,1)} %all-to-all-done.rows_ref, f32[2,8,1024]{2,1,0:T(8,128)S(1)} %broadcast_bitcast_fusion.bias_ref), custom_call_target="tpu_custom_call" | custom-call | flops 536870912 | bytes 1048576 | tf_op jit(solution)/shard_map/pallas_call | solution.py:270
  55.9 2.1 %collective-permute-start.3 = (bf16[1024,128]{1,0:T(8,128)(2,1)S(1)}, bf16[1024,128]{1,0:T(8,128)(2,1)S(1)}, u32[]{:S(2)}, u32[]{:S(2)}) collective-permute-start(bf16[1024,128]{1,0:T(8,128)(2,1)S(1)} %shard_map.75.refs_1_), channel_id=1, source_target_pairs={{4,0},{8,4},{12,8},{14,12},{10,14},{6,10},{2,6},{0,2},{5,1},{9,5},... | collective-permute-start | bytes 786440 | tf_op jit(solution)/shard_map/ppermute | solution.py:432
  58.0 2.0 %collective-permute-start.2 = (bf16[1024,128]{1,0:T(8,128)(2,1)S(1)}, bf16[1024,128]{1,0:T(8,128)(2,1)}, u32[]{:S(2)}, u32[]{:S(2)}) collective-permute-start(bf16[1024,128]{1,0:T(8,128)(2,1)S(1)} %shard_map.74.refs_0_), channel_id=1, source_target_pairs={{4,0},{8,4},{12,8},{14,12},{10,14},{6,10},{2,6},{0,2},{5,1},{9,5},... | collective-permute-start | bytes 786440 | tf_op jit(solution)/shard_map/ppermute | solution.py:432
  60.1 5.2 %collective-permute-done.3.refs_5_ = bf16[1024,128]{1,0:T(8,128)(2,1)S(1)} collective-permute-done((bf16[1024,128]{1,0:T(8,128)(2,1)S(1)}, bf16[1024,128]{1,0:T(8,128)(2,1)S(1)}, u32[]{:S(2)}, u32[]{:S(2)}) %collective-permute-start.3) | collective-permute-done | bytes 262176 | tf_op jit(solution)/shard_map/ppermute | solution.py:432
  65.2 2.0 %collective-permute-start.7 = (bf16[1024,128]{1,0:T(8,128)(2,1)S(1)}, bf16[1024,128]{1,0:T(8,128)(2,1)}, u32[]{:S(2)}, u32[]{:S(2)}) collective-permute-start(bf16[1024,128]{1,0:T(8,128)(2,1)S(1)} %collective-permute-done.3.refs_5_), channel_id=1, source_target_pairs={{4,0},{8,4},{12,8},{14,12},{10,14},{6,10},{2,6},{0,2},{5,1},{9,5},... | collective-permute-start | bytes 786440 | tf_op jit(solution)/shard_map/ppermute | solution.py:432
  67.4 3.6 %collective-permute-done.2.refs_4_ = bf16[1024,128]{1,0:T(8,128)(2,1)} collective-permute-done((bf16[1024,128]{1,0:T(8,128)(2,1)S(1)}, bf16[1024,128]{1,0:T(8,128)(2,1)}, u32[]{:S(2)}, u32[]{:S(2)}) %collective-permute-start.2) | collective-permute-done | bytes 262176 | tf_op jit(solution)/shard_map/ppermute | solution.py:432
  71.0 2.0 %collective-permute-start.6 = (bf16[1024,128]{1,0:T(8,128)(2,1)}, bf16[1024,128]{1,0:T(8,128)(2,1)}, u32[]{:S(2)}, u32[]{:S(2)}) collective-permute-start(bf16[1024,128]{1,0:T(8,128)(2,1)} %collective-permute-done.2.refs_4_), channel_id=1, source_target_pairs={{4,0},{8,4},{12,8},{14,12},{10,14},{6,10},{2,6},{0,2},{5,1},{9,5},... | collective-permute-start | bytes 786440 | tf_op jit(solution)/shard_map/ppermute | solution.py:432
  73.0 3.6 %collective-permute-done.7.refs_9_ = bf16[1024,128]{1,0:T(8,128)(2,1)} collective-permute-done((bf16[1024,128]{1,0:T(8,128)(2,1)S(1)}, bf16[1024,128]{1,0:T(8,128)(2,1)}, u32[]{:S(2)}, u32[]{:S(2)}) %collective-permute-start.7) | collective-permute-done | bytes 262176 | tf_op jit(solution)/shard_map/ppermute | solution.py:432
  76.6 2.0 %collective-permute-start.11 = (bf16[1024,128]{1,0:T(8,128)(2,1)}, bf16[1024,128]{1,0:T(8,128)(2,1)S(1)}, u32[]{:S(2)}, u32[]{:S(2)}) collective-permute-start(bf16[1024,128]{1,0:T(8,128)(2,1)} %collective-permute-done.7.refs_9_), channel_id=1, source_target_pairs={{4,0},{8,4},{12,8},{14,12},{10,14},{6,10},{2,6},{0,2},{5,1},{9,5},... | collective-permute-start | bytes 786440 | tf_op jit(solution)/shard_map/ppermute | solution.py:432
  78.6 3.6 %collective-permute-done.6.refs_8_ = bf16[1024,128]{1,0:T(8,128)(2,1)} collective-permute-done((bf16[1024,128]{1,0:T(8,128)(2,1)}, bf16[1024,128]{1,0:T(8,128)(2,1)}, u32[]{:S(2)}, u32[]{:S(2)}) %collective-permute-start.6) | collective-permute-done | bytes 262176 | tf_op jit(solution)/shard_map/ppermute | solution.py:432
  82.2 2.0 %collective-permute-start.10 = (bf16[1024,128]{1,0:T(8,128)(2,1)}, bf16[1024,128]{1,0:T(8,128)(2,1)S(1)}, u32[]{:S(2)}, u32[]{:S(2)}) collective-permute-start(bf16[1024,128]{1,0:T(8,128)(2,1)} %collective-permute-done.6.refs_8_), channel_id=1, source_target_pairs={{4,0},{8,4},{12,8},{14,12},{10,14},{6,10},{2,6},{0,2},{5,1},{9,5},... | collective-permute-start | bytes 786440 | tf_op jit(solution)/shard_map/ppermute | solution.py:432
  84.2 3.5 %collective-permute-done.11.refs_1_ = bf16[1024,128]{1,0:T(8,128)(2,1)S(1)} collective-permute-done((bf16[1024,128]{1,0:T(8,128)(2,1)}, bf16[1024,128]{1,0:T(8,128)(2,1)S(1)}, u32[]{:S(2)}, u32[]{:S(2)}) %collective-permute-start.11) | collective-permute-done | bytes 262176 | tf_op jit(solution)/shard_map/ppermute | solution.py:432
  87.7 2.0 %collective-permute-start.13 = (bf16[1024,128]{1,0:T(8,128)(2,1)S(1)}, bf16[1024,128]{1,0:T(8,128)(2,1)S(1)}, u32[]{:S(2)}, u32[]{:S(2)}) collective-permute-start(bf16[1024,128]{1,0:T(8,128)(2,1)S(1)} %collective-permute-done.11.refs_1_), channel_id=1, source_target_pairs={{4,0},{8,4},{12,8},{14,12},{10,14},{6,10},{2,6},{0,2},{5,1},{9,5},... | collective-permute-start | bytes 786440 | tf_op jit(solution)/shard_map/ppermute | solution.py:438
  89.8 3.3 %shard_map.76.total_ref = f32[1024,512]{1,0:T(8,128)S(1)} custom-call(s32[6]{0:T(128)S(1)} %compare_select_fusion.4.owner_ref, bf16[512,2048]{1,0:T(8,128)(2,1)S(1)} %copy-done.1, bf16[1024,128]{1,0:T(8,128)(2,1)S(1)} %shard_map.74.refs_0_, bf16[1024,128]{1,0:T(8,128)(2,1)S(1)} %shard_map.75.refs_1_, bf16[1024,128]{1,0:T(8,128)(2,1)S(1)} %collective-permute-done.refs_2_, ...), custom_call_target="tpu_custom_call" | custom-call | flops 1610612736 | bytes 6815744 | tf_op jit(solution)/shard_map/pallas_call | solution.py:322
  93.3 3.5 %collective-permute-done.13.refs_3_ = bf16[1024,128]{1,0:T(8,128)(2,1)S(1)} collective-permute-done((bf16[1024,128]{1,0:T(8,128)(2,1)S(1)}, bf16[1024,128]{1,0:T(8,128)(2,1)S(1)}, u32[]{:S(2)}, u32[]{:S(2)}) %collective-permute-start.13) | collective-permute-done | bytes 262176 | tf_op jit(solution)/shard_map/ppermute | solution.py:438
  98.2 1.9 %collective-permute-done.14.other_ref = bf16[1024,256]{1,0:T(8,128)(2,1)S(1)} collective-permute-done((bf16[1024,256]{1,0:T(8,128)(2,1)S(1)}, bf16[1024,256]{1,0:T(8,128)(2,1)S(1)}, u32[]{:S(2)}, u32[]{:S(2)}) %collective-permute-start.14) | collective-permute-done | bytes 524320 | tf_op jit(solution)/shard_map/ppermute | solution.py:452
  100.2 3.5 %collective-permute-start.20 = (bf16[128,256]{1,0:T(8,128)(2,1)S(1)}, bf16[128,256]{1,0:T(8,128)(2,1)S(1)}, u32[]{:S(2)}, u32[]{:S(2)}) collective-permute-start(bf16[128,256]{1,0:T(8,128)(2,1)S(1)} %get-tuple-element.23), channel_id=1, source_target_pairs={{0,14},{2,12},{4,10},{6,8},{8,6},{10,4},{12,2},{14,0},{1,15},{3,13... | collective-permute-start | bytes 196616 | tf_op jit(solution)/shard_map/ppermute | solution.py:456
  107.0 2.4 %collective-permute-start.16 = (bf16[128,256]{1,0:T(8,128)(2,1)S(1)}, bf16[128,256]{1,0:T(8,128)(2,1)S(1)}, u32[]{:S(2)}, u32[]{:S(2)}) collective-permute-start(bf16[128,256]{1,0:T(8,128)(2,1)S(1)} %get-tuple-element.19), channel_id=1, source_target_pairs={{0,10},{2,8},{4,14},{6,12},{8,2},{10,0},{12,6},{14,4},{1,11},{3,9}... | collective-permute-start | bytes 196616 | tf_op jit(solution)/shard_map/ppermute | solution.py:456
  112.4 2.8 %collective-permute-done.16.refs_5_ = bf16[128,256]{1,0:T(8,128)(2,1)S(1)} collective-permute-done((bf16[128,256]{1,0:T(8,128)(2,1)S(1)}, bf16[128,256]{1,0:T(8,128)(2,1)S(1)}, u32[]{:S(2)}, u32[]{:S(2)}) %collective-permute-start.16) | collective-permute-done | bytes 65568 | tf_op jit(solution)/shard_map/ppermute | solution.py:456
  115.2 1.8 %collective-permute-done.15.refs_4_ = bf16[128,256]{1,0:T(8,128)(2,1)S(1)} collective-permute-done((bf16[128,256]{1,0:T(8,128)(2,1)S(1)}, bf16[128,256]{1,0:T(8,128)(2,1)S(1)}, u32[]{:S(2)}, u32[]{:S(2)}) %collective-permute-start.15) | collective-permute-done | bytes 65568 | tf_op jit(solution)/shard_map/ppermute | solution.py:456
  (54 shorter events, 11.5 us)
Async XLA Ops:
  2.8 44.4 %all-to-all-start = ((bf16[8,2,3,128,128]{4,3,2,1,0:T(8,128)(2,1)}), bf16[8,2,3,128,128]{4,3,2,1,0:T(8,128)(2,1)}, u32[]{:S(2)}, u32[]{:S(2)}) async-start(bf16[8,2,3,128,128]{4,3,2,1,0:T(8,128)(2,1)} %shard_map.73), calls=%async_computation | async-start | bytes 3145728 | tf_op jit(solution)/shard_map/all_to_all | solution.py:425
  51.5 8.5 %collective-permute-start = (bf16[1024,128]{1,0:T(8,128)(2,1)S(1)}, bf16[1024,128]{1,0:T(8,128)(2,1)S(1)}, u32[]{:S(2)}, u32[]{:S(2)}) collective-permute-start(bf16[1024,128]{1,0:T(8,128)(2,1)S(1)} %shard_map.74.refs_0_), channel_id=1, source_target_pairs={{0,4},{4,8},{8,12},{12,14},{14,10},{10,6},{6,2},{2,0},{1,5},{5,9},... | collective-permute-start | bytes 786440 | tf_op jit(solution)/shard_map/ppermute | solution.py:431
  55.9 9.3 %collective-permute-start.3 = (bf16[1024,128]{1,0:T(8,128)(2,1)S(1)}, bf16[1024,128]{1,0:T(8,128)(2,1)S(1)}, u32[]{:S(2)}, u32[]{:S(2)}) collective-permute-start(bf16[1024,128]{1,0:T(8,128)(2,1)S(1)} %shard_map.75.refs_1_), channel_id=1, source_target_pairs={{4,0},{8,4},{12,8},{14,12},{10,14},{6,10},{2,6},{0,2},{5,1},{9,5},... | collective-permute-start | bytes 786440 | tf_op jit(solution)/shard_map/ppermute | solution.py:432
  58.0 9.4 %collective-permute-start.1 = (bf16[1024,128]{1,0:T(8,128)(2,1)S(1)}, bf16[1024,128]{1,0:T(8,128)(2,1)}, u32[]{:S(2)}, u32[]{:S(2)}) collective-permute-start(bf16[1024,128]{1,0:T(8,128)(2,1)S(1)} %shard_map.75.refs_1_), channel_id=1, source_target_pairs={{0,4},{4,8},{8,12},{12,14},{14,10},{10,6},{6,2},{2,0},{1,5},{5,9},... | collective-permute-start | bytes 786440 | tf_op jit(solution)/shard_map/ppermute | solution.py:431
  58.0 12.9 %collective-permute-start.2 = (bf16[1024,128]{1,0:T(8,128)(2,1)S(1)}, bf16[1024,128]{1,0:T(8,128)(2,1)}, u32[]{:S(2)}, u32[]{:S(2)}) collective-permute-start(bf16[1024,128]{1,0:T(8,128)(2,1)S(1)} %shard_map.74.refs_0_), channel_id=1, source_target_pairs={{4,0},{8,4},{12,8},{14,12},{10,14},{6,10},{2,6},{0,2},{5,1},{9,5},... | collective-permute-start | bytes 786440 | tf_op jit(solution)/shard_map/ppermute | solution.py:432
  60.0 12.9 %collective-permute-start.4 = (bf16[1024,128]{1,0:T(8,128)(2,1)S(1)}, bf16[1024,128]{1,0:T(8,128)(2,1)}, u32[]{:S(2)}, u32[]{:S(2)}) collective-permute-start(bf16[1024,128]{1,0:T(8,128)(2,1)S(1)} %collective-permute-done.refs_2_), channel_id=1, source_target_pairs={{0,4},{4,8},{8,12},{12,14},{14,10},{10,6},{6,2},{2,0},{1,5},{5,9},... | collective-permute-start | bytes 786440 | tf_op jit(solution)/shard_map/ppermute | solution.py:431
  65.2 11.3 %collective-permute-start.7 = (bf16[1024,128]{1,0:T(8,128)(2,1)S(1)}, bf16[1024,128]{1,0:T(8,128)(2,1)}, u32[]{:S(2)}, u32[]{:S(2)}) collective-permute-start(bf16[1024,128]{1,0:T(8,128)(2,1)S(1)} %collective-permute-done.3.refs_5_), channel_id=1, source_target_pairs={{4,0},{8,4},{12,8},{14,12},{10,14},{6,10},{2,6},{0,2},{5,1},{9,5},... | collective-permute-start | bytes 786440 | tf_op jit(solution)/shard_map/ppermute | solution.py:432
  67.4 11.2 %collective-permute-start.5 = (bf16[1024,128]{1,0:T(8,128)(2,1)}, bf16[1024,128]{1,0:T(8,128)(2,1)}, u32[]{:S(2)}, u32[]{:S(2)}) collective-permute-start(bf16[1024,128]{1,0:T(8,128)(2,1)} %collective-permute-done.1.refs_3_), channel_id=1, source_target_pairs={{0,4},{4,8},{8,12},{12,14},{14,10},{10,6},{6,2},{2,0},{1,5},{5,9},... | collective-permute-start | bytes 786440 | tf_op jit(solution)/shard_map/ppermute | solution.py:431
  71.0 11.2 %collective-permute-start.6 = (bf16[1024,128]{1,0:T(8,128)(2,1)}, bf16[1024,128]{1,0:T(8,128)(2,1)}, u32[]{:S(2)}, u32[]{:S(2)}) collective-permute-start(bf16[1024,128]{1,0:T(8,128)(2,1)} %collective-permute-done.2.refs_4_), channel_id=1, source_target_pairs={{4,0},{8,4},{12,8},{14,12},{10,14},{6,10},{2,6},{0,2},{5,1},{9,5},... | collective-permute-start | bytes 786440 | tf_op jit(solution)/shard_map/ppermute | solution.py:432
  73.0 11.2 %collective-permute-start.8 = (bf16[1024,128]{1,0:T(8,128)(2,1)}, bf16[1024,128]{1,0:T(8,128)(2,1)}, u32[]{:S(2)}, u32[]{:S(2)}) collective-permute-start(bf16[1024,128]{1,0:T(8,128)(2,1)} %collective-permute-done.4.refs_6_), channel_id=1, source_target_pairs={{0,4},{4,8},{8,12},{12,14},{14,10},{10,6},{6,2},{2,0},{1,5},{5,9},... | collective-permute-start | bytes 786440 | tf_op jit(solution)/shard_map/ppermute | solution.py:431
  76.6 11.1 %collective-permute-start.11 = (bf16[1024,128]{1,0:T(8,128)(2,1)}, bf16[1024,128]{1,0:T(8,128)(2,1)S(1)}, u32[]{:S(2)}, u32[]{:S(2)}) collective-permute-start(bf16[1024,128]{1,0:T(8,128)(2,1)} %collective-permute-done.7.refs_9_), channel_id=1, source_target_pairs={{4,0},{8,4},{12,8},{14,12},{10,14},{6,10},{2,6},{0,2},{5,1},{9,5},... | collective-permute-start | bytes 786440 | tf_op jit(solution)/shard_map/ppermute | solution.py:432
  78.6 11.1 %collective-permute-start.9 = (bf16[1024,128]{1,0:T(8,128)(2,1)}, bf16[1024,128]{1,0:T(8,128)(2,1)S(1)}, u32[]{:S(2)}, u32[]{:S(2)}) collective-permute-start(bf16[1024,128]{1,0:T(8,128)(2,1)} %collective-permute-done.5.refs_7_), channel_id=1, source_target_pairs={{0,4},{4,8},{8,12},{12,14},{14,10},{10,6},{6,2},{2,0},{1,5},{5,9},... | collective-permute-start | bytes 786440 | tf_op jit(solution)/shard_map/ppermute | solution.py:431
  82.2 11.1 %collective-permute-start.10 = (bf16[1024,128]{1,0:T(8,128)(2,1)}, bf16[1024,128]{1,0:T(8,128)(2,1)S(1)}, u32[]{:S(2)}, u32[]{:S(2)}) collective-permute-start(bf16[1024,128]{1,0:T(8,128)(2,1)} %collective-permute-done.6.refs_8_), channel_id=1, source_target_pairs={{4,0},{8,4},{12,8},{14,12},{10,14},{6,10},{2,6},{0,2},{5,1},{9,5},... | collective-permute-start | bytes 786440 | tf_op jit(solution)/shard_map/ppermute | solution.py:432
  84.2 9.1 %collective-permute-start.12 = (bf16[1024,128]{1,0:T(8,128)(2,1)}, bf16[1024,128]{1,0:T(8,128)(2,1)S(1)}, u32[]{:S(2)}, u32[]{:S(2)}) collective-permute-start(bf16[1024,128]{1,0:T(8,128)(2,1)} %collective-permute-done.8.refs_10_), channel_id=1, source_target_pairs={{0,4},{4,8},{8,12},{12,14},{14,10},{10,6},{6,2},{2,0},{1,5},{5,9},... | collective-permute-start | bytes 786440 | tf_op jit(solution)/shard_map/ppermute | solution.py:436
  87.7 9.1 %collective-permute-start.13 = (bf16[1024,128]{1,0:T(8,128)(2,1)S(1)}, bf16[1024,128]{1,0:T(8,128)(2,1)S(1)}, u32[]{:S(2)}, u32[]{:S(2)}) collective-permute-start(bf16[1024,128]{1,0:T(8,128)(2,1)S(1)} %collective-permute-done.11.refs_1_), channel_id=1, source_target_pairs={{4,0},{8,4},{12,8},{14,12},{10,14},{6,10},{2,6},{0,2},{5,1},{9,5},... | collective-permute-start | bytes 786440 | tf_op jit(solution)/shard_map/ppermute | solution.py:438
  98.1 2.0 %collective-permute-start.14 = (bf16[1024,256]{1,0:T(8,128)(2,1)S(1)}, bf16[1024,256]{1,0:T(8,128)(2,1)S(1)}, u32[]{:S(2)}, u32[]{:S(2)}) collective-permute-start(bf16[1024,256]{1,0:T(8,128)(2,1)S(1)} %get-tuple-element.16), channel_id=1, source_target_pairs={{0,1},{1,0},{2,3},{3,2},{4,5},{5,4},{6,7},{7,6},{8,9},{9,8},{10,11... | collective-permute-start | bytes 1572872 | tf_op jit(solution)/shard_map/ppermute | solution.py:452
  100.2 9.1 %collective-permute-start.20 = (bf16[128,256]{1,0:T(8,128)(2,1)S(1)}, bf16[128,256]{1,0:T(8,128)(2,1)S(1)}, u32[]{:S(2)}, u32[]{:S(2)}) collective-permute-start(bf16[128,256]{1,0:T(8,128)(2,1)S(1)} %get-tuple-element.23), channel_id=1, source_target_pairs={{0,14},{2,12},{4,10},{6,8},{8,6},{10,4},{12,2},{14,0},{1,15},{3,13... | collective-permute-start | bytes 196616 | tf_op jit(solution)/shard_map/ppermute | solution.py:456
  103.8 7.3 %collective-permute-start.21 = (bf16[128,256]{1,0:T(8,128)(2,1)S(1)}, bf16[128,256]{1,0:T(8,128)(2,1)S(1)}, u32[]{:S(2)}, u32[]{:S(2)}) collective-permute-start(bf16[128,256]{1,0:T(8,128)(2,1)S(1)} %get-tuple-element.24), channel_id=1, source_target_pairs={{0,6},{2,4},{4,2},{6,0},{8,14},{10,12},{12,10},{14,8},{1,7},{3,5},... | collective-permute-start | bytes 196616 | tf_op jit(solution)/shard_map/ppermute | solution.py:456
  105.2 6.6 %collective-permute-start.18 = (bf16[128,256]{1,0:T(8,128)(2,1)S(1)}, bf16[128,256]{1,0:T(8,128)(2,1)S(1)}, u32[]{:S(2)}, u32[]{:S(2)}) collective-permute-start(bf16[128,256]{1,0:T(8,128)(2,1)S(1)} %get-tuple-element.21), channel_id=1, source_target_pairs={{0,12},{2,14},{4,8},{6,10},{8,4},{10,6},{12,0},{14,2},{1,13},{3,15... | collective-permute-start | bytes 196616 | tf_op jit(solution)/shard_map/ppermute | solution.py:456
  106.3 6.1 %collective-permute-start.19 = (bf16[128,256]{1,0:T(8,128)(2,1)S(1)}, bf16[128,256]{1,0:T(8,128)(2,1)S(1)}, u32[]{:S(2)}, u32[]{:S(2)}) collective-permute-start(bf16[128,256]{1,0:T(8,128)(2,1)S(1)} %get-tuple-element.22), channel_id=1, source_target_pairs={{0,4},{2,6},{4,0},{6,2},{8,12},{10,14},{12,8},{14,10},{1,5},{3,7},... | collective-permute-start | bytes 196616 | tf_op jit(solution)/shard_map/ppermute | solution.py:456
  107.0 8.2 %collective-permute-start.16 = (bf16[128,256]{1,0:T(8,128)(2,1)S(1)}, bf16[128,256]{1,0:T(8,128)(2,1)S(1)}, u32[]{:S(2)}, u32[]{:S(2)}) collective-permute-start(bf16[128,256]{1,0:T(8,128)(2,1)S(1)} %get-tuple-element.19), channel_id=1, source_target_pairs={{0,10},{2,8},{4,14},{6,12},{8,2},{10,0},{12,6},{14,4},{1,11},{3,9}... | collective-permute-start | bytes 196616 | tf_op jit(solution)/shard_map/ppermute | solution.py:456
  109.3 5.8 %collective-permute-start.17 = (bf16[128,256]{1,0:T(8,128)(2,1)S(1)}, bf16[128,256]{1,0:T(8,128)(2,1)S(1)}, u32[]{:S(2)}, u32[]{:S(2)}) collective-permute-start(bf16[128,256]{1,0:T(8,128)(2,1)S(1)} %get-tuple-element.20), channel_id=1, source_target_pairs={{0,2},{2,0},{4,6},{6,4},{8,10},{10,8},{12,14},{14,12},{1,3},{3,1},... | collective-permute-start | bytes 196616 | tf_op jit(solution)/shard_map/ppermute | solution.py:456
  111.0 6.0 %collective-permute-start.15 = (bf16[128,256]{1,0:T(8,128)(2,1)S(1)}, bf16[128,256]{1,0:T(8,128)(2,1)S(1)}, u32[]{:S(2)}, u32[]{:S(2)}) collective-permute-start(bf16[128,256]{1,0:T(8,128)(2,1)S(1)} %get-tuple-element.17), channel_id=1, source_target_pairs={{0,8},{2,10},{4,12},{6,14},{8,0},{10,2},{12,4},{14,6},{1,9},{3,11}... | collective-permute-start | bytes 196616 | tf_op jit(solution)/shard_map/ppermute | solution.py:456
  117.1 1.6 %collective-permute-start.22 = (bf16[4,128,256]{2,1,0:T(8,128)(2,1)S(1)}, bf16[4,128,256]{2,1,0:T(8,128)(2,1)S(1)}, u32[]{:S(2)}, u32[]{:S(2)}) collective-permute-start(bf16[4,128,256]{2,1,0:T(8,128)(2,1)S(1)} %pad_maximum_fusion), channel_id=1, source_target_pairs={{0,1},{1,0},{2,3},{3,2},{4,5},{5,4},{6,7},{7,6},{8,9},{9,8},{10,11... | collective-permute-start | bytes 786440 | tf_op jit(solution)/shard_map/ppermute | solution.py:459
  (4 other events, 237.9 us)

commit v4 on v3

--- a/solution.py
+++ b/solution.py
@@ -14,6 +14,9 @@
 VMEM = 20 << 20
 TILE = 256
 EARLY = 6
+PEERS = 8
+EARLY_STEPS = 0
+ROWS_ORDER = (4, 6, 2, 3, 1, 5, 7)
 SEND_ORDER = (4, 6, 5, 7, 2, 3, 1)
 SCALARS = pl.BlockSpec(memory_space=pltpu.SMEM)
 ARRAY = pl.BlockSpec(memory_space=pltpu.VMEM)
@@ -220,64 +223,68 @@
     return summed.T.astype(jnp.bfloat16)
 
 
-def spread_kernel(query_ref, key_ref, value_ref, out_ref):
-    peers, heads, _, _, width = out_ref.shape
-    for which, ref in enumerate((query_ref, key_ref, value_ref)):
-        for peer in range(peers):
-            for head in range(heads):
-                start = (peer * heads + head) * width
-                out_ref[peer, head, which] = ref[:, start : start + width]
-
-
-def spread(query_rows, key_rows, value_rows, peers):
+def spread_kernel(seq_ref, query_ref, key_ref, value_ref, *out_refs):
+    heads = value_ref.shape[1] // HD // PEERS
+    for spot, out_ref in enumerate(out_refs):
+        head, apart = divmod(spot, PEERS)
+        start = ((seq_ref[0] ^ apart) * heads + head) * HD
+        lanes = pl.ds(pl.multiple_of(start, HD), HD)
+        for which, ref in enumerate((query_ref, key_ref, value_ref)):
+            out_ref[which] = ref[:, lanes]
+
+
+def spread(seq_index, query_rows, key_rows, value_rows):
     tokens, features = query_rows.shape
-    heads = features // HD // peers
+    heads = features // HD // PEERS
+    piece = jax.ShapeDtypeStruct((3, tokens, HD), query_rows.dtype)
+    whole = pl.BlockSpec((tokens, features), lambda i: (0, 0))
     return pl.pallas_call(
         spread_kernel,
-        out_shape=jax.ShapeDtypeStruct((peers, heads, 3, tokens, HD), query_rows.dtype),
+        grid=(1,),
+        in_specs=[SCALARS] + [whole] * 3,
+        out_specs=[pl.BlockSpec(piece.shape, lambda i: (0, 0, 0))] * (heads * PEERS),
+        out_shape=[piece] * (heads * PEERS),
         cost_estimate=pl.CostEstimate(
             flops=0, bytes_accessed=12 * tokens * features, transcendentals=0
         ),
-    )(query_rows, key_rows, value_rows)
-
-
-def attend_kernel(head, rows_ref, bias_ref, out_ref):
-    groups = rows_ref.shape[0]
-    tokens = rows_ref.shape[3]
+    )(seq_index[None], query_rows, key_rows, value_rows)
+
+
+def attend_kernel(head, seq_ref, bias_ref, *refs):
+    *pieces, out_ref = refs
+    tokens = pieces[0].shape[1]
     factor = math.log2(math.e) / math.sqrt(HD)
-    keys = jnp.concatenate([rows_ref[group, head, 1] for group in range(groups)], axis=0)
-    values = jnp.concatenate([rows_ref[group, head, 2] for group in range(groups)], axis=0)
-    for group in range(groups):
+    keys = jnp.concatenate([piece[1] for piece in pieces], axis=0)
+    values = jnp.concatenate([piece[2] for piece in pieces], axis=0)
+    for apart, piece in enumerate(pieces):
         scores = lax.dot_general(
-            rows_ref[group, head, 0],
-            keys,
-            (((1,), (1,)), ((), ())),
-            preferred_element_type=jnp.float32,
+            piece[0], keys, (((1,), (1,)), ((), ())), preferred_element_type=jnp.float32
         )
-        scores = scores * factor + bias_ref[head, group : group + 1, :]
+        scores = scores * factor + bias_ref[head, apart : apart + 1, :]
         peak = jnp.max(scores, axis=1, keepdims=True)
         terms = jnp.exp2(scores - peak)
         denom = jnp.sum(terms, axis=1, keepdims=True)
         mixed = jnp.dot(
             terms.astype(jnp.bfloat16), values, preferred_element_type=jnp.float32
         )
-        out_ref[group * tokens : (group + 1) * tokens, :] = (mixed / denom).astype(out_ref.dtype)
-
-
-def attend_head(rows, bias, head):
-    groups, _, _, tokens, _ = rows.shape
-    total = groups * tokens
+        rows = pl.ds(pl.multiple_of((seq_ref[0] ^ apart) * tokens, tokens), tokens)
+        out_ref[rows, :] = (mixed / denom).astype(out_ref.dtype)
+
+
+def attend_head(seq_index, bias, pieces, head):
+    _, tokens, width = pieces[0].shape
+    total = len(pieces) * tokens
     return pl.pallas_call(
         functools.partial(attend_kernel, head),
-        in_specs=[ARRAY] * 2,
-        out_shape=jax.ShapeDtypeStruct((total, HD), rows.dtype),
+        in_specs=[SCALARS] + [ARRAY] * (1 + len(pieces)),
+        out_shape=jax.ShapeDtypeStruct((total, width), pieces[0].dtype),
         compiler_params=pltpu.CompilerParams(vmem_limit_bytes=VMEM),
         cost_estimate=pl.CostEstimate(
-            flops=4 * total * total * HD,
-            bytes_accessed=8 * total * HD,
+            flops=4 * total * total * width,
+            bytes_accessed=8 * total * width,
             transcendentals=total * total,
         ),
-    )(rows, bias)
+    )(seq_index[None], bias, *pieces)
 
 
 def product_tile(owner_ref, pieces, weight_ref, tile):
@@ -393,13 +400,13 @@
     )(seq_index[None], head_index[None], near[None], crossed, *arrived)
 
 
-def key_bias(rand_blocks, head_start, heads):
+def key_bias(rand_blocks, seq_index, head_start, heads):
     block_total = rand_blocks.shape[0]
-    ids = jnp.arange(block_total, dtype=jnp.int32)
+    ids = seq_index ^ jnp.arange(block_total, dtype=jnp.int32)
     near = jnp.abs(ids[:, None] - ids[None, :]) <= 1
     ends = (ids == 0) | (ids == block_total - 1)
     fixed = near | ends[None, :] | ends[:, None]
-    chosen = lax.dynamic_slice_in_dim(rand_blocks, head_start, heads, 1)
+    chosen = lax.dynamic_slice_in_dim(rand_blocks, head_start, heads, 1)[ids]
     named = jnp.any(chosen[:, :, :, None] == ids, axis=2).transpose(1, 0, 2)
     live = named | fixed[None]
     return jnp.repeat(jnp.where(live, 0.0, -1e30).astype(jnp.float32), BLK, axis=2)
@@ -418,13 +425,22 @@
     order = ring_order(peers)
     onward = [(order[i], order[(i + 1) % peers]) for i in range(peers)]
     back = [(target, source) for source, target in onward]
-    outgoing = spread(query_rows, key_rows, value_rows, peers)
-    bias = key_bias(rand_blocks, head_index * (features // HD) + seq_index * heads, heads)
+    outgoing = spread(seq_index, query_rows, key_rows, value_rows)
+    bias = key_bias(rand_blocks, seq_index, head_index * (features // HD) + seq_index * heads, heads)
     reach = peers // 2
     far = {}
-    rows = lax.all_to_all(outgoing, "seq", split_axis=0, concat_axis=0, tiled=True)
+    pieces = {}
     for head in range(heads):
-        mine = attend_head(rows, bias, head)
+        pieces[head, 0] = outgoing[head * peers]
+        for apart in ROWS_ORDER:
+            pairs = [(i, i ^ apart) for i in range(peers)]
+            pieces[head, apart] = lax.ppermute(outgoing[head * peers + apart], "seq", pairs)
+    for head in range(heads):
+        group = [pieces[head, apart] for apart in range(peers)]
+        if head and EARLY_STEPS:
+            held = [far[0, 1], far[0, -1]][:EARLY_STEPS]
+            *group, = lax.optimization_barrier((*group, *held))[:peers]
+        mine = attend_head(seq_index, bias, group, head)
         ahead, behind = (mine, mine)
         far[head, 0] = mine
         for step in range(1, reach):
@@ -464,7 +480,7 @@
     tokens, features = query_rows.shape
     peers = lax.axis_size("seq")
     even = features // HD % peers == 0
-    if tokens == BLK and peers == 8 and lax.axis_size("head") == 2 and even:
+    if tokens == BLK and peers == PEERS and lax.axis_size("head") == 2 and even:
         return local_by_heads(query_rows, key_rows, value_rows, rand_blocks, out_weight)
     return local_by_rows(query_rows, key_rows, value_rows, rand_blocks, out_weight)
 

time: 120 us -> 111 us (0.925)
  waiting for transfers between devices: 68.9 us -> 37.9 us
  starting transfers between devices: 32.8 us -> 56.4 us
  Pallas kernels: 17 us -> 14.3 us
  local copies, waits for them, and re-layouts: 0.35 us -> 1.94 us
    all_to_all x1 -> x0, waiting for transfers between devices: 36.6 us -> none  [local_by_heads(): lax.all_to_all(outgoing, 'seq', split_axis=0, concat_axis=0, tiled=True)]
    ppermute x0 -> x14, starting transfers between devices: none -> 30.2 us  [local_by_heads(): lax.ppermute(outgoing[head * peers + apart], 'seq', pairs)]
    ppermute x6, starting transfers between devices: 0.18 us -> 12.5 us  [local_by_heads(): ahead = lax.ppermute(ahead, 'seq', onward)]
    ppermute x6, starting transfers between devices: 12.1 us -> 0.62 us  [local_by_heads(): behind = lax.ppermute(behind, 'seq', back)]
    all_to_all x1 -> x0, starting transfers between devices: 7.28 us -> none  [local_by_heads(): lax.all_to_all(outgoing, 'seq', split_axis=0, concat_axis=0, tiled=True)]
    ppermute x0 -> x14, waiting for transfers between devices: none -> 5.28 us  [local_by_heads(): lax.ppermute(outgoing[head * peers + apart], 'seq', pairs)]
    pallas_call x3, Pallas kernels: 11.5 us -> 8.77 us  [the longest x2 5.85 us: attend_head(): pl.pallas_call(functools.partial(attend_kernel, head), in_specs=[SCALARS]...]
    ppermute x1, starting transfers between devices: 0.02 us -> 2.02 us  [local_by_heads(): far[head, reach] = lax.ppermute(ahead, 'seq', onward)]
  transfers between devices with their start and end apart: 24 -> 37, of which waited for: 15 -> 15; matrix products, arithmetic and copies ran while one was open for 0% -> 1% of each run, Pallas kernels for 6% -> 8%
where the time goes in v4:
time: 111 us
  starting transfers between devices  56.4 us (51%)
  waiting for transfers between devices  37.9 us (34%)
  Pallas kernels  14.3 us (13%)
  local copies, waits for them, and re-layouts  1.94 us (2%)
    ppermute x14, starting transfers between devices, local_by_heads(): lax.ppermute(outgoing[head * peers + apart], 'seq', pairs)  30.2 us
    ppermute x6, waiting for transfers between devices, local_by_heads(): behind = lax.ppermute(behind, 'seq', back)  20.8 us
    ppermute x6, starting transfers between devices, local_by_heads(): ahead = lax.ppermute(ahead, 'seq', onward)  12.5 us
    ppermute x7, starting transfers between devices, local_by_heads(): arrived[apart] = lax.ppermute(parts[apart], 'seq', pairs)  11 us
    pallas_call x2, Pallas kernels, attend_head(): pl.pallas_call(functools.partial(attend_kernel, head), in_specs=[SCALARS]...  5.85 us
    ppermute x7, waiting for transfers between devices, local_by_heads(): arrived[apart] = lax.ppermute(parts[apart], 'seq', pairs)  5.56 us
    ppermute x14, waiting for transfers between devices, local_by_heads(): lax.ppermute(outgoing[head * peers + apart], 'seq', pairs)  5.28 us
    pallas_call x1, Pallas kernels, project_early(): pl.pallas_call(early_kernel, in_specs=[SCALARS] + [ARRAY] * (1 + len(piec...  3.27 us
  transfers between devices with their start and end apart: 37, of which 15 were waited for; matrix products, arithmetic and copies ran while one was open for 1% of the time, Pallas kernels for 8%

profile of v4, /device:TPU:0, one launch (start us, length us, event | category | flops | bytes accessed | tf_op | source)
XLA Modules:
  0.0 111.1 jit_solution(2711735454307510348)
XLA Ops:
  0.0 2.9 %shard_map.73 = (bf16[3,128,128]{2,1,0:T(8,128)(2,1)}, bf16[3,128,128]{2,1,0:T(8,128)(2,1)}, bf16[3,128,128]{2,1,0:T(8,128)(2,1)}, bf16[3,128,128]{2,1,0:T(8,128...) custom-call(s32[1]{0:T(128)} %bitcast.seq_ref.row_ref, ...), custom_call_target="tpu_custom_call" | custom-call | bytes 3145728 | tf_op jit(solution)/shard_map/pallas_call | solution.py:241
  2.9 3.0 %collective-permute-start = (bf16[3,128,128]{2,1,0:T(8,128)(2,1)}, bf16[3,128,128]{2,1,0:T(8,128)(2,1)S(1)}, u32[]{:S(2)}, u32[]{:S(2)}) collective-permute-start(bf16[3,128,128]{2,1,0:T(8,128)(2,1)} %get-tuple-element.32), channel_id=1, source_target_pairs={{0,2},{2,0},{4,6},{6,4},{8,10},{10,8},{12,14},{14,12},{1,3},{3,1},... | collective-permute-start | bytes 294920 | tf_op jit(solution)/shard_map/ppermute | solution.py:437
  7.5 3.0 %collective-permute-start.3 = (bf16[3,128,128]{2,1,0:T(8,128)(2,1)}, bf16[3,128,128]{2,1,0:T(8,128)(2,1)S(1)}, u32[]{:S(2)}, u32[]{:S(2)}) collective-permute-start(bf16[3,128,128]{2,1,0:T(8,128)(2,1)} %get-tuple-element.35), channel_id=1, source_target_pairs={{0,8},{2,10},{4,12},{6,14},{8,0},{10,2},{12,4},{14,6},{1,9},{3,11}... | collective-permute-start | bytes 294920 | tf_op jit(solution)/shard_map/ppermute | solution.py:437
  12.9 3.7 %collective-permute-start.5 = (bf16[3,128,128]{2,1,0:T(8,128)(2,1)}, bf16[3,128,128]{2,1,0:T(8,128)(2,1)S(1)}, u32[]{:S(2)}, u32[]{:S(2)}) collective-permute-start(bf16[3,128,128]{2,1,0:T(8,128)(2,1)} %get-tuple-element.37), channel_id=1, source_target_pairs={{0,12},{2,14},{4,8},{6,10},{8,4},{10,6},{12,0},{14,2},{1,13},{3,15... | collective-permute-start | bytes 294920 | tf_op jit(solution)/shard_map/ppermute | solution.py:437
  18.3 5.0 %collective-permute-start.8 = (bf16[3,128,128]{2,1,0:T(8,128)(2,1)}, bf16[3,128,128]{2,1,0:T(8,128)(2,1)S(1)}, u32[]{:S(2)}, u32[]{:S(2)}) collective-permute-start(bf16[3,128,128]{2,1,0:T(8,128)(2,1)} %get-tuple-element.41), channel_id=1, source_target_pairs={{0,4},{2,6},{4,0},{6,2},{8,12},{10,14},{12,8},{14,10},{1,5},{3,7},... | collective-permute-start | bytes 294920 | tf_op jit(solution)/shard_map/ppermute | solution.py:437
  23.3 2.6 %collective-permute-done.4.refs_5_ = bf16[3,128,128]{2,1,0:T(8,128)(2,1)S(1)} collective-permute-done((bf16[3,128,128]{2,1,0:T(8,128)(2,1)}, bf16[3,128,128]{2,1,0:T(8,128)(2,1)S(1)}, u32[]{:S(2)}, u32[]{:S(2)}) %collective-permute-start.4) | collective-permute-done | bytes 98336 | tf_op jit(solution)/shard_map/ppermute | solution.py:437
  26.0 3.6 %collective-permute-start.10 = (bf16[3,128,128]{2,1,0:T(8,128)(2,1)}, bf16[3,128,128]{2,1,0:T(8,128)(2,1)S(1)}, u32[]{:S(2)}, u32[]{:S(2)}) collective-permute-start(bf16[3,128,128]{2,1,0:T(8,128)(2,1)} %get-tuple-element.43), channel_id=1, source_target_pairs={{0,8},{2,10},{4,12},{6,14},{8,0},{10,2},{12,4},{14,6},{1,9},{3,11}... | collective-permute-start | bytes 294920 | tf_op jit(solution)/shard_map/ppermute | solution.py:437
  29.6 2.3 %collective-permute-start.11 = (bf16[3,128,128]{2,1,0:T(8,128)(2,1)}, bf16[3,128,128]{2,1,0:T(8,128)(2,1)S(1)}, u32[]{:S(2)}, u32[]{:S(2)}) collective-permute-start(bf16[3,128,128]{2,1,0:T(8,128)(2,1)} %get-tuple-element.44), channel_id=1, source_target_pairs={{0,10},{2,8},{4,14},{6,12},{8,2},{10,0},{12,6},{14,4},{1,11},{3,9}... | collective-permute-start | bytes 294920 | tf_op jit(solution)/shard_map/ppermute | solution.py:437
  33.1 3.8 %collective-permute-start.13 = (bf16[3,128,128]{2,1,0:T(8,128)(2,1)}, bf16[3,128,128]{2,1,0:T(8,128)(2,1)S(1)}, u32[]{:S(2)}, u32[]{:S(2)}) collective-permute-start(bf16[3,128,128]{2,1,0:T(8,128)(2,1)} %get-tuple-element.46), channel_id=1, source_target_pairs={{0,14},{2,12},{4,10},{6,8},{8,6},{10,4},{12,2},{14,0},{1,15},{3,13... | collective-permute-start | bytes 294920 | tf_op jit(solution)/shard_map/ppermute | solution.py:437
  37.9 2.9 %shard_map.74.refs_0_ = bf16[1024,128]{1,0:T(8,128)(2,1)S(1)} custom-call(s32[1]{0:T(128)} %bitcast.seq_ref.row_ref, f32[2,8,1024]{2,1,0:T(8,128)S(1)} %broadcast_bitcast_fusion.bias_ref, bf16[3,128,128]{2,1,0:T(8,128)(2,1)S(1)} %copy-done.3, bf16[3,128,128]{2,1,0:T(8,128)(2,1)S(1)} %collective-permute-done.refs_1_, ...), custom_call_target="tpu_custom_call" | custom-call | flops 536870912 | bytes 1048576 | tf_op jit(solution)/shard_map/pallas_call | solution.py:277
  40.9 2.6 %collective-permute-done.11.refs_5_ = bf16[3,128,128]{2,1,0:T(8,128)(2,1)S(1)} collective-permute-done((bf16[3,128,128]{2,1,0:T(8,128)(2,1)}, bf16[3,128,128]{2,1,0:T(8,128)(2,1)S(1)}, u32[]{:S(2)}, u32[]{:S(2)}) %collective-permute-start.11) | collective-permute-done | bytes 98336 | tf_op jit(solution)/shard_map/ppermute | solution.py:437
  43.5 2.9 %shard_map.75.refs_1_ = bf16[1024,128]{1,0:T(8,128)(2,1)S(1)} custom-call(s32[1]{0:T(128)} %bitcast.seq_ref.row_ref, f32[2,8,1024]{2,1,0:T(8,128)S(1)} %broadcast_bitcast_fusion.bias_ref, bf16[3,128,128]{2,1,0:T(8,128)(2,1)S(1)} %copy-done.2, bf16[3,128,128]{2,1,0:T(8,128)(2,1)S(1)} %collective-permute-done.7.refs_1_, ...), custom_call_target="tpu_custom_call" | custom-call | flops 536870912 | bytes 1048576 | tf_op jit(solution)/shard_map/pallas_call | solution.py:277
  47.1 4.3 %collective-permute-start.15 = (bf16[1024,128]{1,0:T(8,128)(2,1)S(1)}, bf16[1024,128]{1,0:T(8,128)(2,1)}, u32[]{:S(2)}, u32[]{:S(2)}) collective-permute-start(bf16[1024,128]{1,0:T(8,128)(2,1)S(1)} %shard_map.75.refs_1_), channel_id=1, source_target_pairs={{0,4},{4,8},{8,12},{12,14},{14,10},{10,6},{6,2},{2,0},{1,5},{5,9},... | collective-permute-start | bytes 786440 | tf_op jit(solution)/shard_map/ppermute | solution.py:447
  53.4 5.1 %collective-permute-done.17.refs_5_ = bf16[1024,128]{1,0:T(8,128)(2,1)S(1)} collective-permute-done((bf16[1024,128]{1,0:T(8,128)(2,1)S(1)}, bf16[1024,128]{1,0:T(8,128)(2,1)S(1)}, u32[]{:S(2)}, u32[]{:S(2)}) %collective-permute-start.17) | collective-permute-done | bytes 262176 | tf_op jit(solution)/shard_map/ppermute | solution.py:448
  60.6 3.6 %collective-permute-done.16.refs_4_ = bf16[1024,128]{1,0:T(8,128)(2,1)} collective-permute-done((bf16[1024,128]{1,0:T(8,128)(2,1)S(1)}, bf16[1024,128]{1,0:T(8,128)(2,1)}, u32[]{:S(2)}, u32[]{:S(2)}) %collective-permute-start.16) | collective-permute-done | bytes 262176 | tf_op jit(solution)/shard_map/ppermute | solution.py:448
  66.3 3.6 %collective-permute-done.21.refs_9_ = bf16[1024,128]{1,0:T(8,128)(2,1)} collective-permute-done((bf16[1024,128]{1,0:T(8,128)(2,1)S(1)}, bf16[1024,128]{1,0:T(8,128)(2,1)}, u32[]{:S(2)}, u32[]{:S(2)}) %collective-permute-start.21) | collective-permute-done | bytes 262176 | tf_op jit(solution)/shard_map/ppermute | solution.py:448
  71.9 3.6 %collective-permute-done.20.refs_8_ = bf16[1024,128]{1,0:T(8,128)(2,1)} collective-permute-done((bf16[1024,128]{1,0:T(8,128)(2,1)}, bf16[1024,128]{1,0:T(8,128)(2,1)}, u32[]{:S(2)}, u32[]{:S(2)}) %collective-permute-start.20) | collective-permute-done | bytes 262176 | tf_op jit(solution)/shard_map/ppermute | solution.py:448
  77.5 3.5 %collective-permute-done.25.refs_1_ = bf16[1024,128]{1,0:T(8,128)(2,1)S(1)} collective-permute-done((bf16[1024,128]{1,0:T(8,128)(2,1)}, bf16[1024,128]{1,0:T(8,128)(2,1)S(1)}, u32[]{:S(2)}, u32[]{:S(2)}) %collective-permute-start.25) | collective-permute-done | bytes 262176 | tf_op jit(solution)/shard_map/ppermute | solution.py:448
  81.0 3.3 %shard_map.76.total_ref = f32[1024,512]{1,0:T(8,128)S(1)} custom-call(s32[6]{0:T(128)S(1)} %compare_select_fusion.5.owner_ref, bf16[512,2048]{1,0:T(8,128)(2,1)S(1)} %copy-done.1, bf16[1024,128]{1,0:T(8,128)(2,1)S(1)} %shard_map.74.refs_0_, bf16[1024,128]{1,0:T(8,128)(2,1)S(1)} %shard_map.75.refs_1_, bf16[1024,128]{1,0:T(8,128)(2,1)S(1)} %collective-permute-done.14.refs_2_, ...), custom_call_target="tpu_custom_call" | custom-call | flops 1610612736 | bytes 6815744 | tf_op jit(solution)/shard_map/pallas_call | solution.py:329
  85.7 2.8 %collective-permute-done.27.refs_3_ = bf16[1024,128]{1,0:T(8,128)(2,1)S(1)} collective-permute-done((bf16[1024,128]{1,0:T(8,128)(2,1)S(1)}, bf16[1024,128]{1,0:T(8,128)(2,1)S(1)}, u32[]{:S(2)}, u32[]{:S(2)}) %collective-permute-start.27) | collective-permute-done | bytes 262176 | tf_op jit(solution)/shard_map/ppermute | solution.py:454
  91.9 2.7 %collective-permute-start.34 = (bf16[128,256]{1,0:T(8,128)(2,1)S(1)}, bf16[128,256]{1,0:T(8,128)(2,1)S(1)}, u32[]{:S(2)}, u32[]{:S(2)}) collective-permute-start(bf16[128,256]{1,0:T(8,128)(2,1)S(1)} %get-tuple-element.55), channel_id=1, source_target_pairs={{0,14},{2,12},{4,10},{6,8},{8,6},{10,4},{12,2},{14,0},{1,15},{3,13... | collective-permute-start | bytes 196616 | tf_op jit(solution)/shard_map/ppermute | solution.py:472
  94.7 2.3 %collective-permute-start.35 = (bf16[128,256]{1,0:T(8,128)(2,1)S(1)}, bf16[128,256]{1,0:T(8,128)(2,1)S(1)}, u32[]{:S(2)}, u32[]{:S(2)}) collective-permute-start(bf16[128,256]{1,0:T(8,128)(2,1)S(1)} %get-tuple-element.56), channel_id=1, source_target_pairs={{0,6},{2,4},{4,2},{6,0},{8,14},{10,12},{12,10},{14,8},{1,7},{3,5},... | collective-permute-start | bytes 196616 | tf_op jit(solution)/shard_map/ppermute | solution.py:472
  98.1 2.7 %collective-permute-start.30 = (bf16[128,256]{1,0:T(8,128)(2,1)S(1)}, bf16[128,256]{1,0:T(8,128)(2,1)S(1)}, u32[]{:S(2)}, u32[]{:S(2)}) collective-permute-start(bf16[128,256]{1,0:T(8,128)(2,1)S(1)} %get-tuple-element.51), channel_id=1, source_target_pairs={{0,10},{2,8},{4,14},{6,12},{8,2},{10,0},{12,6},{14,4},{1,11},{3,9}... | collective-permute-start | bytes 196616 | tf_op jit(solution)/shard_map/ppermute | solution.py:472
  103.5 3.4 %collective-permute-done.30.refs_5_ = bf16[128,256]{1,0:T(8,128)(2,1)S(1)} collective-permute-done((bf16[128,256]{1,0:T(8,128)(2,1)S(1)}, bf16[128,256]{1,0:T(8,128)(2,1)S(1)}, u32[]{:S(2)}, u32[]{:S(2)}) %collective-permute-start.30) | collective-permute-done | bytes 65568 | tf_op jit(solution)/shard_map/ppermute | solution.py:472
  (89 shorter events, 31.7 us)
Async XLA Ops:
  6.0 10.6 %collective-permute-start.1 = (bf16[3,128,128]{2,1,0:T(8,128)(2,1)}, bf16[3,128,128]{2,1,0:T(8,128)(2,1)S(1)}, u32[]{:S(2)}, u32[]{:S(2)}) collective-permute-start(bf16[3,128,128]{2,1,0:T(8,128)(2,1)} %get-tuple-element.33), channel_id=1, source_target_pairs={{0,4},{2,6},{4,0},{6,2},{8,12},{10,14},{12,8},{14,10},{1,5},{3,7},... | collective-permute-start | bytes 294920 | tf_op jit(solution)/shard_map/ppermute | solution.py:437
  7.5 10.7 %collective-permute-start.3 = (bf16[3,128,128]{2,1,0:T(8,128)(2,1)}, bf16[3,128,128]{2,1,0:T(8,128)(2,1)S(1)}, u32[]{:S(2)}, u32[]{:S(2)}) collective-permute-start(bf16[3,128,128]{2,1,0:T(8,128)(2,1)} %get-tuple-element.35), channel_id=1, source_target_pairs={{0,8},{2,10},{4,12},{6,14},{8,0},{10,2},{12,4},{14,6},{1,9},{3,11}... | collective-permute-start | bytes 294920 | tf_op jit(solution)/shard_map/ppermute | solution.py:437
  10.5 15.4 %collective-permute-start.4 = (bf16[3,128,128]{2,1,0:T(8,128)(2,1)}, bf16[3,128,128]{2,1,0:T(8,128)(2,1)S(1)}, u32[]{:S(2)}, u32[]{:S(2)}) collective-permute-start(bf16[3,128,128]{2,1,0:T(8,128)(2,1)} %get-tuple-element.36), channel_id=1, source_target_pairs={{0,10},{2,8},{4,14},{6,12},{8,2},{10,0},{12,6},{14,4},{1,11},{3,9}... | collective-permute-start | bytes 294920 | tf_op jit(solution)/shard_map/ppermute | solution.py:437
  12.9 13.1 %collective-permute-start.5 = (bf16[3,128,128]{2,1,0:T(8,128)(2,1)}, bf16[3,128,128]{2,1,0:T(8,128)(2,1)S(1)}, u32[]{:S(2)}, u32[]{:S(2)}) collective-permute-start(bf16[3,128,128]{2,1,0:T(8,128)(2,1)} %get-tuple-element.37), channel_id=1, source_target_pairs={{0,12},{2,14},{4,8},{6,10},{8,4},{10,6},{12,0},{14,2},{1,13},{3,15... | collective-permute-start | bytes 294920 | tf_op jit(solution)/shard_map/ppermute | solution.py:437
  16.6 13.0 %collective-permute-start.6 = (bf16[3,128,128]{2,1,0:T(8,128)(2,1)}, bf16[3,128,128]{2,1,0:T(8,128)(2,1)S(1)}, u32[]{:S(2)}, u32[]{:S(2)}) collective-permute-start(bf16[3,128,128]{2,1,0:T(8,128)(2,1)} %get-tuple-element.38), channel_id=1, source_target_pairs={{0,14},{2,12},{4,10},{6,8},{8,6},{10,4},{12,2},{14,0},{1,15},{3,13... | collective-permute-start | bytes 294920 | tf_op jit(solution)/shard_map/ppermute | solution.py:437
  16.6 15.3 %collective-permute-start.7 = (bf16[3,128,128]{2,1,0:T(8,128)(2,1)}, bf16[3,128,128]{2,1,0:T(8,128)(2,1)S(1)}, u32[]{:S(2)}, u32[]{:S(2)}) collective-permute-start(bf16[3,128,128]{2,1,0:T(8,128)(2,1)} %get-tuple-element.40), channel_id=1, source_target_pairs={{0,2},{2,0},{4,6},{6,4},{8,10},{10,8},{12,14},{14,12},{1,3},{3,1},... | collective-permute-start | bytes 294920 | tf_op jit(solution)/shard_map/ppermute | solution.py:437
  18.3 14.8 %collective-permute-start.8 = (bf16[3,128,128]{2,1,0:T(8,128)(2,1)}, bf16[3,128,128]{2,1,0:T(8,128)(2,1)S(1)}, u32[]{:S(2)}, u32[]{:S(2)}) collective-permute-start(bf16[3,128,128]{2,1,0:T(8,128)(2,1)} %get-tuple-element.41), channel_id=1, source_target_pairs={{0,4},{2,6},{4,0},{6,2},{8,12},{10,14},{12,8},{14,10},{1,5},{3,7},... | collective-permute-start | bytes 294920 | tf_op jit(solution)/shard_map/ppermute | solution.py:437
  25.9 14.9 %collective-permute-start.9 = (bf16[3,128,128]{2,1,0:T(8,128)(2,1)}, bf16[3,128,128]{2,1,0:T(8,128)(2,1)S(1)}, u32[]{:S(2)}, u32[]{:S(2)}) collective-permute-start(bf16[3,128,128]{2,1,0:T(8,128)(2,1)} %get-tuple-element.42), channel_id=1, source_target_pairs={{0,6},{2,4},{4,2},{6,0},{8,14},{10,12},{12,10},{14,8},{1,7},{3,5},... | collective-permute-start | bytes 294920 | tf_op jit(solution)/shard_map/ppermute | solution.py:437
  26.0 14.9 %collective-permute-start.10 = (bf16[3,128,128]{2,1,0:T(8,128)(2,1)}, bf16[3,128,128]{2,1,0:T(8,128)(2,1)S(1)}, u32[]{:S(2)}, u32[]{:S(2)}) collective-permute-start(bf16[3,128,128]{2,1,0:T(8,128)(2,1)} %get-tuple-element.43), channel_id=1, source_target_pairs={{0,8},{2,10},{4,12},{6,14},{8,0},{10,2},{12,4},{14,6},{1,9},{3,11}... | collective-permute-start | bytes 294920 | tf_op jit(solution)/shard_map/ppermute | solution.py:437
  29.6 14.0 %collective-permute-start.11 = (bf16[3,128,128]{2,1,0:T(8,128)(2,1)}, bf16[3,128,128]{2,1,0:T(8,128)(2,1)S(1)}, u32[]{:S(2)}, u32[]{:S(2)}) collective-permute-start(bf16[3,128,128]{2,1,0:T(8,128)(2,1)} %get-tuple-element.44), channel_id=1, source_target_pairs={{0,10},{2,8},{4,14},{6,12},{8,2},{10,0},{12,6},{14,4},{1,11},{3,9}... | collective-permute-start | bytes 294920 | tf_op jit(solution)/shard_map/ppermute | solution.py:437
  31.9 11.6 %collective-permute-start.12 = (bf16[3,128,128]{2,1,0:T(8,128)(2,1)}, bf16[3,128,128]{2,1,0:T(8,128)(2,1)S(1)}, u32[]{:S(2)}, u32[]{:S(2)}) collective-permute-start(bf16[3,128,128]{2,1,0:T(8,128)(2,1)} %get-tuple-element.45), channel_id=1, source_target_pairs={{0,12},{2,14},{4,8},{6,10},{8,4},{10,6},{12,0},{14,2},{1,13},{3,15... | collective-permute-start | bytes 294920 | tf_op jit(solution)/shard_map/ppermute | solution.py:437
  33.1 10.4 %collective-permute-start.13 = (bf16[3,128,128]{2,1,0:T(8,128)(2,1)}, bf16[3,128,128]{2,1,0:T(8,128)(2,1)S(1)}, u32[]{:S(2)}, u32[]{:S(2)}) collective-permute-start(bf16[3,128,128]{2,1,0:T(8,128)(2,1)} %get-tuple-element.46), channel_id=1, source_target_pairs={{0,14},{2,12},{4,10},{6,8},{8,6},{10,4},{12,2},{14,0},{1,15},{3,13... | collective-permute-start | bytes 294920 | tf_op jit(solution)/shard_map/ppermute | solution.py:437
  40.8 10.5 %collective-permute-start.14 = (bf16[1024,128]{1,0:T(8,128)(2,1)S(1)}, bf16[1024,128]{1,0:T(8,128)(2,1)S(1)}, u32[]{:S(2)}, u32[]{:S(2)}) collective-permute-start(bf16[1024,128]{1,0:T(8,128)(2,1)S(1)} %shard_map.74.refs_0_), channel_id=1, source_target_pairs={{0,4},{4,8},{8,12},{12,14},{14,10},{10,6},{6,2},{2,0},{1,5},{5,9},... | collective-permute-start | bytes 786440 | tf_op jit(solution)/shard_map/ppermute | solution.py:447
  46.5 12.0 %collective-permute-start.17 = (bf16[1024,128]{1,0:T(8,128)(2,1)S(1)}, bf16[1024,128]{1,0:T(8,128)(2,1)S(1)}, u32[]{:S(2)}, u32[]{:S(2)}) collective-permute-start(bf16[1024,128]{1,0:T(8,128)(2,1)S(1)} %shard_map.75.refs_1_), channel_id=1, source_target_pairs={{4,0},{8,4},{12,8},{14,12},{10,14},{6,10},{2,6},{0,2},{5,1},{9,5},... | collective-permute-start | bytes 786440 | tf_op jit(solution)/shard_map/ppermute | solution.py:448
  47.1 11.4 %collective-permute-start.15 = (bf16[1024,128]{1,0:T(8,128)(2,1)S(1)}, bf16[1024,128]{1,0:T(8,128)(2,1)}, u32[]{:S(2)}, u32[]{:S(2)}) collective-permute-start(bf16[1024,128]{1,0:T(8,128)(2,1)S(1)} %shard_map.75.refs_1_), channel_id=1, source_target_pairs={{0,4},{4,8},{8,12},{12,14},{14,10},{10,6},{6,2},{2,0},{1,5},{5,9},... | collective-permute-start | bytes 786440 | tf_op jit(solution)/shard_map/ppermute | solution.py:447
  51.4 12.9 %collective-permute-start.16 = (bf16[1024,128]{1,0:T(8,128)(2,1)S(1)}, bf16[1024,128]{1,0:T(8,128)(2,1)}, u32[]{:S(2)}, u32[]{:S(2)}) collective-permute-start(bf16[1024,128]{1,0:T(8,128)(2,1)S(1)} %shard_map.74.refs_0_), channel_id=1, source_target_pairs={{4,0},{8,4},{12,8},{14,12},{10,14},{6,10},{2,6},{0,2},{5,1},{9,5},... | collective-permute-start | bytes 786440 | tf_op jit(solution)/shard_map/ppermute | solution.py:448
  51.4 12.9 %collective-permute-start.18 = (bf16[1024,128]{1,0:T(8,128)(2,1)S(1)}, bf16[1024,128]{1,0:T(8,128)(2,1)}, u32[]{:S(2)}, u32[]{:S(2)}) collective-permute-start(bf16[1024,128]{1,0:T(8,128)(2,1)S(1)} %collective-permute-done.14.refs_2_), channel_id=1, source_target_pairs={{0,4},{4,8},{8,12},{12,14},{14,10},{10,6},{6,2},{2,0},{1,5},{5,9},... | collective-permute-start | bytes 786440 | tf_op jit(solution)/shard_map/ppermute | solution.py:447
  58.5 11.3 %collective-permute-start.21 = (bf16[1024,128]{1,0:T(8,128)(2,1)S(1)}, bf16[1024,128]{1,0:T(8,128)(2,1)}, u32[]{:S(2)}, u32[]{:S(2)}) collective-permute-start(bf16[1024,128]{1,0:T(8,128)(2,1)S(1)} %collective-permute-done.17.refs_5_), channel_id=1, source_target_pairs={{4,0},{8,4},{12,8},{14,12},{10,14},{6,10},{2,6},{0,2},{5,1},{9,5},... | collective-permute-start | bytes 786440 | tf_op jit(solution)/shard_map/ppermute | solution.py:448
  58.5 11.3 %collective-permute-start.19 = (bf16[1024,128]{1,0:T(8,128)(2,1)}, bf16[1024,128]{1,0:T(8,128)(2,1)}, u32[]{:S(2)}, u32[]{:S(2)}) collective-permute-start(bf16[1024,128]{1,0:T(8,128)(2,1)} %collective-permute-done.15.refs_3_), channel_id=1, source_target_pairs={{0,4},{4,8},{8,12},{12,14},{14,10},{10,6},{6,2},{2,0},{1,5},{5,9},... | collective-permute-start | bytes 786440 | tf_op jit(solution)/shard_map/ppermute | solution.py:447
  64.2 11.2 %collective-permute-start.20 = (bf16[1024,128]{1,0:T(8,128)(2,1)}, bf16[1024,128]{1,0:T(8,128)(2,1)}, u32[]{:S(2)}, u32[]{:S(2)}) collective-permute-start(bf16[1024,128]{1,0:T(8,128)(2,1)} %collective-permute-done.16.refs_4_), channel_id=1, source_target_pairs={{4,0},{8,4},{12,8},{14,12},{10,14},{6,10},{2,6},{0,2},{5,1},{9,5},... | collective-permute-start | bytes 786440 | tf_op jit(solution)/shard_map/ppermute | solution.py:448
  64.2 11.2 %collective-permute-start.22 = (bf16[1024,128]{1,0:T(8,128)(2,1)}, bf16[1024,128]{1,0:T(8,128)(2,1)}, u32[]{:S(2)}, u32[]{:S(2)}) collective-permute-start(bf16[1024,128]{1,0:T(8,128)(2,1)} %collective-permute-done.18.refs_6_), channel_id=1, source_target_pairs={{0,4},{4,8},{8,12},{12,14},{14,10},{10,6},{6,2},{2,0},{1,5},{5,9},... | collective-permute-start | bytes 786440 | tf_op jit(solution)/shard_map/ppermute | solution.py:447
  69.9 11.1 %collective-permute-start.25 = (bf16[1024,128]{1,0:T(8,128)(2,1)}, bf16[1024,128]{1,0:T(8,128)(2,1)S(1)}, u32[]{:S(2)}, u32[]{:S(2)}) collective-permute-start(bf16[1024,128]{1,0:T(8,128)(2,1)} %collective-permute-done.21.refs_9_), channel_id=1, source_target_pairs={{4,0},{8,4},{12,8},{14,12},{10,14},{6,10},{2,6},{0,2},{5,1},{9,5},... | collective-permute-start | bytes 786440 | tf_op jit(solution)/shard_map/ppermute | solution.py:448
  69.9 11.1 %collective-permute-start.23 = (bf16[1024,128]{1,0:T(8,128)(2,1)}, bf16[1024,128]{1,0:T(8,128)(2,1)S(1)}, u32[]{:S(2)}, u32[]{:S(2)}) collective-permute-start(bf16[1024,128]{1,0:T(8,128)(2,1)} %collective-permute-done.19.refs_7_), channel_id=1, source_target_pairs={{0,4},{4,8},{8,12},{12,14},{14,10},{10,6},{6,2},{2,0},{1,5},{5,9},... | collective-permute-start | bytes 786440 | tf_op jit(solution)/shard_map/ppermute | solution.py:447
  75.5 10.2 %collective-permute-start.24 = (bf16[1024,128]{1,0:T(8,128)(2,1)}, bf16[1024,128]{1,0:T(8,128)(2,1)S(1)}, u32[]{:S(2)}, u32[]{:S(2)}) collective-permute-start(bf16[1024,128]{1,0:T(8,128)(2,1)} %collective-permute-done.20.refs_8_), channel_id=1, source_target_pairs={{4,0},{8,4},{12,8},{14,12},{10,14},{6,10},{2,6},{0,2},{5,1},{9,5},... | collective-permute-start | bytes 786440 | tf_op jit(solution)/shard_map/ppermute | solution.py:448
  (19 other events, 364.1 us)

commit v5 on v4

--- a/solution.py
+++ b/solution.py
@@ -16,7 +16,8 @@
 EARLY = 6
 PEERS = 8
 EARLY_STEPS = 0
-ROWS_ORDER = (4, 6, 2, 3, 1, 5, 7)
+HELD = 2
+ROWS_ORDER = ((4, 6, 2, 3, 1, 5, 7), (4, 6, 2, 3, 1, 5, 7))
 SEND_ORDER = (4, 6, 5, 7, 2, 3, 1)
 SCALARS = pl.BlockSpec(memory_space=pltpu.SMEM)
 ARRAY = pl.BlockSpec(memory_space=pltpu.VMEM)
@@ -223,27 +224,25 @@
     return summed.T.astype(jnp.bfloat16)
 
 
-def spread_kernel(seq_ref, query_ref, key_ref, value_ref, *out_refs):
+def spread_kernel(head, seq_ref, query_ref, key_ref, value_ref, *out_refs):
     heads = value_ref.shape[1] // HD // PEERS
-    for spot, out_ref in enumerate(out_refs):
-        head, apart = divmod(spot, PEERS)
+    for apart, out_ref in enumerate(out_refs):
         start = ((seq_ref[0] ^ apart) * heads + head) * HD
         lanes = pl.ds(pl.multiple_of(start, HD), HD)
         for which, ref in enumerate((query_ref, key_ref, value_ref)):
             out_ref[which] = ref[:, lanes]
 
 
-def spread(seq_index, query_rows, key_rows, value_rows):
+def spread(seq_index, query_rows, key_rows, value_rows, head):
     tokens, features = query_rows.shape
-    heads = features // HD // PEERS
     piece = jax.ShapeDtypeStruct((3, tokens, HD), query_rows.dtype)
     whole = pl.BlockSpec((tokens, features), lambda i: (0, 0))
     return pl.pallas_call(
-        spread_kernel,
+        functools.partial(spread_kernel, head),
         grid=(1,),
         in_specs=[SCALARS] + [whole] * 3,
-        out_specs=[pl.BlockSpec(piece.shape, lambda i: (0, 0, 0))] * (heads * PEERS),
-        out_shape=[piece] * (heads * PEERS),
+        out_specs=[pl.BlockSpec(piece.shape, lambda i: (0, 0, 0))] * PEERS,
+        out_shape=[piece] * PEERS,
         cost_estimate=pl.CostEstimate(
             flops=0, bytes_accessed=12 * tokens * features, transcendentals=0
         ),
@@ -425,17 +424,28 @@
     order = ring_order(peers)
     onward = [(order[i], order[(i + 1) % peers]) for i in range(peers)]
     back = [(target, source) for source, target in onward]
-    outgoing = spread(seq_index, query_rows, key_rows, value_rows)
+    outgoing = []
+    for head in range(heads):
+        if head:
+            query_rows, _ = lax.optimization_barrier((query_rows, outgoing[0]))
+        outgoing += spread(seq_index, query_rows, key_rows, value_rows, head)
     bias = key_bias(rand_blocks, seq_index, head_index * (features // HD) + seq_index * heads, heads)
     reach = peers // 2
     far = {}
     pieces = {}
     for head in range(heads):
         pieces[head, 0] = outgoing[head * peers]
-        for apart in ROWS_ORDER:
+        for spot, apart in enumerate(ROWS_ORDER[head % 2]):
+            if head and spot >= len(ROWS_ORDER[0]) - HELD:
+                continue
             pairs = [(i, i ^ apart) for i in range(peers)]
             pieces[head, apart] = lax.ppermute(outgoing[head * peers + apart], "seq", pairs)
     for head in range(heads):
+        if head:
+            for apart in ROWS_ORDER[head % 2][len(ROWS_ORDER[0]) - HELD :]:
+                pairs = [(i, i ^ apart) for i in range(peers)]
+                piece, _ = lax.optimization_barrier((outgoing[head * peers + apart], far[0, 0]))
+                pieces[head, apart] = lax.ppermute(piece, "seq", pairs)
         group = [pieces[head, apart] for apart in range(peers)]
         if head and EARLY_STEPS:
             held = [far[0, 1], far[0, -1]][:EARLY_STEPS]

time: 111 us -> 110 us (level)
  starting transfers between devices: 56.4 us -> 53.9 us
  Pallas kernels: 14.3 us -> 16.3 us
  waiting for transfers between devices: 37.9 us -> 36.5 us
    ppermute x14 -> x12, starting transfers between devices: 30.2 us -> 19.6 us  [local_by_heads(): lax.ppermute(outgoing[head * peers + apart], 'seq', pairs)]
    ppermute x6, starting transfers between devices: 12.5 us -> 4.12 us  [local_by_heads(): ahead = lax.ppermute(ahead, 'seq', onward)]
    ppermute x6, starting transfers between devices: 0.62 us -> 8.63 us  [local_by_heads(): behind = lax.ppermute(behind, 'seq', back)]
    ppermute x0 -> x2, starting transfers between devices: none -> 7.8 us  [local_by_heads(): pieces[head, apart] = lax.ppermute(piece, 'seq', pairs)]
    ppermute x0 -> x2, waiting for transfers between devices: none -> 3.97 us  [local_by_heads(): pieces[head, apart] = lax.ppermute(piece, 'seq', pairs)]
    ppermute x6, waiting for transfers between devices: 20.8 us -> 17.5 us  [local_by_heads(): behind = lax.ppermute(behind, 'seq', back)]
    pallas_call x1 -> x2, Pallas kernels: 2.92 us -> 4.95 us  [spread(): pl.pallas_call(functools.partial(spread_kernel, head), grid=(1,), in_spec...]
    ppermute x14 -> x12, waiting for transfers between devices: 5.28 us -> 3.96 us  [local_by_heads(): lax.ppermute(outgoing[head * peers + apart], 'seq', pairs)]
  transfers between devices with their start and end apart: 37 -> 37, of which waited for: 15 -> 18; matrix products, arithmetic and copies ran while one was open for 1% -> 1% of each run, Pallas kernels for 8% -> 11%
where the time goes in v5:
time: 110 us
  starting transfers between devices  53.9 us (49%)
  waiting for transfers between devices  36.5 us (33%)
  Pallas kernels  16.3 us (15%)
  local copies, waits for them, and re-layouts  2.83 us (3%)
    ppermute x12, starting transfers between devices, local_by_heads(): lax.ppermute(outgoing[head * peers + apart], 'seq', pairs)  19.6 us
    ppermute x6, waiting for transfers between devices, local_by_heads(): behind = lax.ppermute(behind, 'seq', back)  17.5 us
    ppermute x7, starting transfers between devices, local_by_heads(): arrived[apart] = lax.ppermute(parts[apart], 'seq', pairs)  11.5 us
    ppermute x6, starting transfers between devices, local_by_heads(): behind = lax.ppermute(behind, 'seq', back)  8.63 us
    ppermute x2, starting transfers between devices, local_by_heads(): pieces[head, apart] = lax.ppermute(piece, 'seq', pairs)  7.8 us
    pallas_call x2, Pallas kernels, attend_head(): pl.pallas_call(functools.partial(attend_kernel, head), in_specs=[SCALARS]...  5.81 us
    ppermute x7, waiting for transfers between devices, local_by_heads(): arrived[apart] = lax.ppermute(parts[apart], 'seq', pairs)  5.2 us
    pallas_call x2, Pallas kernels, spread(): pl.pallas_call(functools.partial(spread_kernel, head), grid=(1,), in_spec...  4.95 us
  transfers between devices with their start and end apart: 37, of which 18 were waited for; matrix products, arithmetic and copies ran while one was open for 1% of the time, Pallas kernels for 11%

profile of v5, /device:TPU:0, one launch (start us, length us, event | category | flops | bytes accessed | tf_op | source)
XLA Modules:
  0.0 110.0 jit_solution(7911956980521682526)
XLA Ops:
  0.0 2.4 %shard_map.73 = (bf16[3,128,128]{2,1,0:T(8,128)(2,1)}, bf16[3,128,128]{2,1,0:T(8,128)(2,1)}, bf16[3,128,128]{2,1,0:T(8,128)(2,1)}, bf16[3,128,128]{2,1,0:T(8,128...) custom-call(s32[1]{0:T(128)} %bitcast.seq_ref.row_ref, ...), custom_call_target="tpu_custom_call" | custom-call | bytes 3145728 | tf_op jit(solution)/shard_map/pallas_call | solution.py:240
  2.4 3.0 %collective-permute-start = (bf16[3,128,128]{2,1,0:T(8,128)(2,1)}, bf16[3,128,128]{2,1,0:T(8,128)(2,1)S(1)}, u32[]{:S(2)}, u32[]{:S(2)}) collective-permute-start(bf16[3,128,128]{2,1,0:T(8,128)(2,1)} %get-tuple-element.35), channel_id=1, source_target_pairs={{0,2},{2,0},{4,6},{6,4},{8,10},{10,8},{12,14},{14,12},{1,3},{3,1},... | collective-permute-start | bytes 294920 | tf_op jit(solution)/shard_map/ppermute | solution.py:442
  7.0 3.0 %collective-permute-start.3 = (bf16[3,128,128]{2,1,0:T(8,128)(2,1)}, bf16[3,128,128]{2,1,0:T(8,128)(2,1)S(1)}, u32[]{:S(2)}, u32[]{:S(2)}) collective-permute-start(bf16[3,128,128]{2,1,0:T(8,128)(2,1)} %get-tuple-element.38), channel_id=1, source_target_pairs={{0,8},{2,10},{4,12},{6,14},{8,0},{10,2},{12,4},{14,6},{1,9},{3,11}... | collective-permute-start | bytes 294920 | tf_op jit(solution)/shard_map/ppermute | solution.py:442
  12.4 2.5 %shard_map.75 = (bf16[3,128,128]{2,1,0:T(8,128)(2,1)}, bf16[3,128,128]{2,1,0:T(8,128)(2,1)}, bf16[3,128,128]{2,1,0:T(8,128)(2,1)}, bf16[3,128,128]{2,1,0:T(8,128...) custom-call(s32[1]{0:T(128)} %bitcast.seq_ref.row_ref, ...), custom_call_target="tpu_custom_call" | custom-call | bytes 3145728 | tf_op jit(solution)/shard_map/pallas_call | solution.py:240
  15.0 3.7 %collective-permute-start.5 = (bf16[3,128,128]{2,1,0:T(8,128)(2,1)}, bf16[3,128,128]{2,1,0:T(8,128)(2,1)S(1)}, u32[]{:S(2)}, u32[]{:S(2)}) collective-permute-start(bf16[3,128,128]{2,1,0:T(8,128)(2,1)} %get-tuple-element.40), channel_id=1, source_target_pairs={{0,12},{2,14},{4,8},{6,10},{8,4},{10,6},{12,0},{14,2},{1,13},{3,15... | collective-permute-start | bytes 294920 | tf_op jit(solution)/shard_map/ppermute | solution.py:442
  20.4 3.9 %collective-permute-done.4.refs_5_ = bf16[3,128,128]{2,1,0:T(8,128)(2,1)S(1)} collective-permute-done((bf16[3,128,128]{2,1,0:T(8,128)(2,1)}, bf16[3,128,128]{2,1,0:T(8,128)(2,1)S(1)}, u32[]{:S(2)}, u32[]{:S(2)}) %collective-permute-start.4) | collective-permute-done | bytes 98336 | tf_op jit(solution)/shard_map/ppermute | solution.py:442
  24.8 4.1 %collective-permute-start.10 = (bf16[3,128,128]{2,1,0:T(8,128)(2,1)}, bf16[3,128,128]{2,1,0:T(8,128)(2,1)S(1)}, u32[]{:S(2)}, u32[]{:S(2)}) collective-permute-start(bf16[3,128,128]{2,1,0:T(8,128)(2,1)} %get-tuple-element.47), channel_id=1, source_target_pairs={{0,8},{2,10},{4,12},{6,14},{8,0},{10,2},{12,4},{14,6},{1,9},{3,11}... | collective-permute-start | bytes 294920 | tf_op jit(solution)/shard_map/ppermute | solution.py:442
  30.6 2.9 %shard_map.74.refs_0_ = bf16[1024,128]{1,0:T(8,128)(2,1)S(1)} custom-call(s32[1]{0:T(128)} %bitcast.seq_ref.row_ref, f32[2,8,1024]{2,1,0:T(8,128)S(1)} %broadcast_bitcast_fusion.bias_ref, bf16[3,128,128]{2,1,0:T(8,128)(2,1)S(1)} %copy-done.2, bf16[3,128,128]{2,1,0:T(8,128)(2,1)S(1)} %collective-permute-done.refs_1_, ...), custom_call_target="tpu_custom_call" | custom-call | flops 536870912 | bytes 1048576 | tf_op jit(solution)/shard_map/pallas_call | solution.py:276
  33.5 4.2 %collective-permute-start.11 = (bf16[3,128,128]{2,1,0:T(8,128)(2,1)}, bf16[3,128,128]{2,1,0:T(8,128)(2,1)S(1)}, u32[]{:S(2)}, u32[]{:S(2)}) collective-permute-start(bf16[3,128,128]{2,1,0:T(8,128)(2,1)} %get-tuple-element.49), channel_id=1, source_target_pairs={{0,10},{2,8},{4,14},{6,12},{8,2},{10,0},{12,6},{14,4},{1,11},{3,9}... | collective-permute-start | bytes 294920 | tf_op jit(solution)/shard_map/ppermute | solution.py:448
  37.7 3.6 %collective-permute-start.13 = (bf16[3,128,128]{2,1,0:T(8,128)(2,1)}, bf16[3,128,128]{2,1,0:T(8,128)(2,1)S(1)}, u32[]{:S(2)}, u32[]{:S(2)}) collective-permute-start(bf16[3,128,128]{2,1,0:T(8,128)(2,1)} %get-tuple-element.52), channel_id=1, source_target_pairs={{0,14},{2,12},{4,10},{6,8},{8,6},{10,4},{12,2},{14,0},{1,15},{3,13... | collective-permute-start | bytes 294920 | tf_op jit(solution)/shard_map/ppermute | solution.py:448
  42.7 2.7 %collective-permute-done.13.refs_7_ = bf16[3,128,128]{2,1,0:T(8,128)(2,1)S(1)} collective-permute-done((bf16[3,128,128]{2,1,0:T(8,128)(2,1)}, bf16[3,128,128]{2,1,0:T(8,128)(2,1)S(1)}, u32[]{:S(2)}, u32[]{:S(2)}) %collective-permute-start.13) | collective-permute-done | bytes 98336 | tf_op jit(solution)/shard_map/ppermute | solution.py:448
  46.2 2.9 %shard_map.76.refs_1_ = bf16[1024,128]{1,0:T(8,128)(2,1)S(1)} custom-call(s32[1]{0:T(128)} %bitcast.seq_ref.row_ref, f32[2,8,1024]{2,1,0:T(8,128)S(1)} %broadcast_bitcast_fusion.bias_ref, bf16[3,128,128]{2,1,0:T(8,128)(2,1)S(1)} %copy-done.3, bf16[3,128,128]{2,1,0:T(8,128)(2,1)S(1)} %collective-permute-done.7.refs_1_, ...), custom_call_target="tpu_custom_call" | custom-call | flops 536870912 | bytes 1048576 | tf_op jit(solution)/shard_map/pallas_call | solution.py:276
  53.4 4.7 %collective-permute-done.17.refs_5_ = bf16[1024,128]{1,0:T(8,128)(2,1)S(1)} collective-permute-done((bf16[1024,128]{1,0:T(8,128)(2,1)S(1)}, bf16[1024,128]{1,0:T(8,128)(2,1)S(1)}, u32[]{:S(2)}, u32[]{:S(2)}) %collective-permute-start.17) | collective-permute-done | bytes 262176 | tf_op jit(solution)/shard_map/ppermute | solution.py:458
  60.6 3.3 %collective-permute-done.16.refs_4_ = bf16[1024,128]{1,0:T(8,128)(2,1)} collective-permute-done((bf16[1024,128]{1,0:T(8,128)(2,1)S(1)}, bf16[1024,128]{1,0:T(8,128)(2,1)}, u32[]{:S(2)}, u32[]{:S(2)}) %collective-permute-start.16) | collective-permute-done | bytes 262176 | tf_op jit(solution)/shard_map/ppermute | solution.py:458
  66.3 3.2 %collective-permute-done.21.refs_9_ = bf16[1024,128]{1,0:T(8,128)(2,1)} collective-permute-done((bf16[1024,128]{1,0:T(8,128)(2,1)S(1)}, bf16[1024,128]{1,0:T(8,128)(2,1)}, u32[]{:S(2)}, u32[]{:S(2)}) %collective-permute-start.21) | collective-permute-done | bytes 262176 | tf_op jit(solution)/shard_map/ppermute | solution.py:458
  71.9 3.2 %collective-permute-done.20.refs_8_ = bf16[1024,128]{1,0:T(8,128)(2,1)} collective-permute-done((bf16[1024,128]{1,0:T(8,128)(2,1)}, bf16[1024,128]{1,0:T(8,128)(2,1)}, u32[]{:S(2)}, u32[]{:S(2)}) %collective-permute-start.20) | collective-permute-done | bytes 262176 | tf_op jit(solution)/shard_map/ppermute | solution.py:458
  77.5 3.1 %collective-permute-done.25.refs_1_ = bf16[1024,128]{1,0:T(8,128)(2,1)S(1)} collective-permute-done((bf16[1024,128]{1,0:T(8,128)(2,1)}, bf16[1024,128]{1,0:T(8,128)(2,1)S(1)}, u32[]{:S(2)}, u32[]{:S(2)}) %collective-permute-start.25) | collective-permute-done | bytes 262176 | tf_op jit(solution)/shard_map/ppermute | solution.py:458
  82.0 3.3 %shard_map.77.total_ref = f32[1024,512]{1,0:T(8,128)S(1)} custom-call(s32[6]{0:T(128)S(1)} %compare_select_fusion.5.owner_ref, bf16[512,2048]{1,0:T(8,128)(2,1)S(1)} %copy-done.1, bf16[1024,128]{1,0:T(8,128)(2,1)S(1)} %shard_map.74.refs_0_, bf16[1024,128]{1,0:T(8,128)(2,1)S(1)} %shard_map.76.refs_1_, bf16[1024,128]{1,0:T(8,128)(2,1)S(1)} %collective-permute-done.14.refs_2_, ...), custom_call_target="tpu_custom_call" | custom-call | flops 1610612736 | bytes 6815744 | tf_op jit(solution)/shard_map/pallas_call | solution.py:328
  85.3 2.1 %collective-permute-done.27.refs_3_ = bf16[1024,128]{1,0:T(8,128)(2,1)S(1)} collective-permute-done((bf16[1024,128]{1,0:T(8,128)(2,1)S(1)}, bf16[1024,128]{1,0:T(8,128)(2,1)S(1)}, u32[]{:S(2)}, u32[]{:S(2)}) %collective-permute-start.27) | collective-permute-done | bytes 262176 | tf_op jit(solution)/shard_map/ppermute | solution.py:464
  88.8 1.9 %collective-permute-done.28.other_ref = bf16[1024,256]{1,0:T(8,128)(2,1)S(1)} collective-permute-done((bf16[1024,256]{1,0:T(8,128)(2,1)S(1)}, bf16[1024,256]{1,0:T(8,128)(2,1)S(1)}, u32[]{:S(2)}, u32[]{:S(2)}) %collective-permute-start.28) | collective-permute-done | bytes 524320 | tf_op jit(solution)/shard_map/ppermute | solution.py:478
  90.8 3.7 %collective-permute-start.34 = (bf16[128,256]{1,0:T(8,128)(2,1)S(1)}, bf16[128,256]{1,0:T(8,128)(2,1)S(1)}, u32[]{:S(2)}, u32[]{:S(2)}) collective-permute-start(bf16[128,256]{1,0:T(8,128)(2,1)S(1)} %get-tuple-element.61), channel_id=1, source_target_pairs={{0,14},{2,12},{4,10},{6,8},{8,6},{10,4},{12,2},{14,0},{1,15},{3,13... | collective-permute-start | bytes 196616 | tf_op jit(solution)/shard_map/ppermute | solution.py:482
  97.5 2.8 %collective-permute-start.30 = (bf16[128,256]{1,0:T(8,128)(2,1)S(1)}, bf16[128,256]{1,0:T(8,128)(2,1)S(1)}, u32[]{:S(2)}, u32[]{:S(2)}) collective-permute-start(bf16[128,256]{1,0:T(8,128)(2,1)S(1)} %get-tuple-element.57), channel_id=1, source_target_pairs={{0,10},{2,8},{4,14},{6,12},{8,2},{10,0},{12,6},{14,4},{1,11},{3,9}... | collective-permute-start | bytes 196616 | tf_op jit(solution)/shard_map/ppermute | solution.py:482
  100.3 1.9 %collective-permute-start.31 = (bf16[128,256]{1,0:T(8,128)(2,1)S(1)}, bf16[128,256]{1,0:T(8,128)(2,1)S(1)}, u32[]{:S(2)}, u32[]{:S(2)}) collective-permute-start(bf16[128,256]{1,0:T(8,128)(2,1)S(1)} %get-tuple-element.58), channel_id=1, source_target_pairs={{0,2},{2,0},{4,6},{6,4},{8,10},{10,8},{12,14},{14,12},{1,3},{3,1},... | collective-permute-start | bytes 196616 | tf_op jit(solution)/shard_map/ppermute | solution.py:482
  103.2 2.5 %collective-permute-done.30.refs_5_ = bf16[128,256]{1,0:T(8,128)(2,1)S(1)} collective-permute-done((bf16[128,256]{1,0:T(8,128)(2,1)S(1)}, bf16[128,256]{1,0:T(8,128)(2,1)S(1)}, u32[]{:S(2)}, u32[]{:S(2)}) %collective-permute-start.30) | collective-permute-done | bytes 65568 | tf_op jit(solution)/shard_map/ppermute | solution.py:482
  (90 shorter events, 35.3 us)
Async XLA Ops:
  2.4 12.5 %collective-permute-start = (bf16[3,128,128]{2,1,0:T(8,128)(2,1)}, bf16[3,128,128]{2,1,0:T(8,128)(2,1)S(1)}, u32[]{:S(2)}, u32[]{:S(2)}) collective-permute-start(bf16[3,128,128]{2,1,0:T(8,128)(2,1)} %get-tuple-element.35), channel_id=1, source_target_pairs={{0,2},{2,0},{4,6},{6,4},{8,10},{10,8},{12,14},{14,12},{1,3},{3,1},... | collective-permute-start | bytes 294920 | tf_op jit(solution)/shard_map/ppermute | solution.py:442
  5.4 13.2 %collective-permute-start.1 = (bf16[3,128,128]{2,1,0:T(8,128)(2,1)}, bf16[3,128,128]{2,1,0:T(8,128)(2,1)S(1)}, u32[]{:S(2)}, u32[]{:S(2)}) collective-permute-start(bf16[3,128,128]{2,1,0:T(8,128)(2,1)} %get-tuple-element.36), channel_id=1, source_target_pairs={{0,4},{2,6},{4,0},{6,2},{8,12},{10,14},{12,8},{14,10},{1,5},{3,7},... | collective-permute-start | bytes 294920 | tf_op jit(solution)/shard_map/ppermute | solution.py:442
  7.0 11.7 %collective-permute-start.2 = (bf16[3,128,128]{2,1,0:T(8,128)(2,1)}, bf16[3,128,128]{2,1,0:T(8,128)(2,1)S(1)}, u32[]{:S(2)}, u32[]{:S(2)}) collective-permute-start(bf16[3,128,128]{2,1,0:T(8,128)(2,1)} %get-tuple-element.37), channel_id=1, source_target_pairs={{0,6},{2,4},{4,2},{6,0},{8,14},{10,12},{12,10},{14,8},{1,7},{3,5},... | collective-permute-start | bytes 294920 | tf_op jit(solution)/shard_map/ppermute | solution.py:442
  7.0 13.3 %collective-permute-start.3 = (bf16[3,128,128]{2,1,0:T(8,128)(2,1)}, bf16[3,128,128]{2,1,0:T(8,128)(2,1)S(1)}, u32[]{:S(2)}, u32[]{:S(2)}) collective-permute-start(bf16[3,128,128]{2,1,0:T(8,128)(2,1)} %get-tuple-element.38), channel_id=1, source_target_pairs={{0,8},{2,10},{4,12},{6,14},{8,0},{10,2},{12,4},{14,6},{1,9},{3,11}... | collective-permute-start | bytes 294920 | tf_op jit(solution)/shard_map/ppermute | solution.py:442
  10.0 14.4 %collective-permute-start.4 = (bf16[3,128,128]{2,1,0:T(8,128)(2,1)}, bf16[3,128,128]{2,1,0:T(8,128)(2,1)S(1)}, u32[]{:S(2)}, u32[]{:S(2)}) collective-permute-start(bf16[3,128,128]{2,1,0:T(8,128)(2,1)} %get-tuple-element.39), channel_id=1, source_target_pairs={{0,10},{2,8},{4,14},{6,12},{8,2},{10,0},{12,6},{14,4},{1,11},{3,9}... | collective-permute-start | bytes 294920 | tf_op jit(solution)/shard_map/ppermute | solution.py:442
  15.0 9.9 %collective-permute-start.5 = (bf16[3,128,128]{2,1,0:T(8,128)(2,1)}, bf16[3,128,128]{2,1,0:T(8,128)(2,1)S(1)}, u32[]{:S(2)}, u32[]{:S(2)}) collective-permute-start(bf16[3,128,128]{2,1,0:T(8,128)(2,1)} %get-tuple-element.40), channel_id=1, source_target_pairs={{0,12},{2,14},{4,8},{6,10},{8,4},{10,6},{12,0},{14,2},{1,13},{3,15... | collective-permute-start | bytes 294920 | tf_op jit(solution)/shard_map/ppermute | solution.py:442
  18.6 10.3 %collective-permute-start.6 = (bf16[3,128,128]{2,1,0:T(8,128)(2,1)}, bf16[3,128,128]{2,1,0:T(8,128)(2,1)S(1)}, u32[]{:S(2)}, u32[]{:S(2)}) collective-permute-start(bf16[3,128,128]{2,1,0:T(8,128)(2,1)} %get-tuple-element.41), channel_id=1, source_target_pairs={{0,14},{2,12},{4,10},{6,8},{8,6},{10,4},{12,2},{14,0},{1,15},{3,13... | collective-permute-start | bytes 294920 | tf_op jit(solution)/shard_map/ppermute | solution.py:442
  18.7 14.9 %collective-permute-start.7 = (bf16[3,128,128]{2,1,0:T(8,128)(2,1)}, bf16[3,128,128]{2,1,0:T(8,128)(2,1)S(1)}, u32[]{:S(2)}, u32[]{:S(2)}) collective-permute-start(bf16[3,128,128]{2,1,0:T(8,128)(2,1)} %get-tuple-element.44), channel_id=1, source_target_pairs={{0,2},{2,0},{4,6},{6,4},{8,10},{10,8},{12,14},{14,12},{1,3},{3,1},... | collective-permute-start | bytes 294920 | tf_op jit(solution)/shard_map/ppermute | solution.py:442
  20.3 17.4 %collective-permute-start.8 = (bf16[3,128,128]{2,1,0:T(8,128)(2,1)}, bf16[3,128,128]{2,1,0:T(8,128)(2,1)S(1)}, u32[]{:S(2)}, u32[]{:S(2)}) collective-permute-start(bf16[3,128,128]{2,1,0:T(8,128)(2,1)} %get-tuple-element.45), channel_id=1, source_target_pairs={{0,4},{2,6},{4,0},{6,2},{8,12},{10,14},{12,8},{14,10},{1,5},{3,7},... | collective-permute-start | bytes 294920 | tf_op jit(solution)/shard_map/ppermute | solution.py:442
  24.3 17.0 %collective-permute-start.9 = (bf16[3,128,128]{2,1,0:T(8,128)(2,1)}, bf16[3,128,128]{2,1,0:T(8,128)(2,1)S(1)}, u32[]{:S(2)}, u32[]{:S(2)}) collective-permute-start(bf16[3,128,128]{2,1,0:T(8,128)(2,1)} %get-tuple-element.46), channel_id=1, source_target_pairs={{0,6},{2,4},{4,2},{6,0},{8,14},{10,12},{12,10},{14,8},{1,7},{3,5},... | collective-permute-start | bytes 294920 | tf_op jit(solution)/shard_map/ppermute | solution.py:442
  24.8 16.5 %collective-permute-start.10 = (bf16[3,128,128]{2,1,0:T(8,128)(2,1)}, bf16[3,128,128]{2,1,0:T(8,128)(2,1)S(1)}, u32[]{:S(2)}, u32[]{:S(2)}) collective-permute-start(bf16[3,128,128]{2,1,0:T(8,128)(2,1)} %get-tuple-element.47), channel_id=1, source_target_pairs={{0,8},{2,10},{4,12},{6,14},{8,0},{10,2},{12,4},{14,6},{1,9},{3,11}... | collective-permute-start | bytes 294920 | tf_op jit(solution)/shard_map/ppermute | solution.py:442
  28.9 12.4 %collective-permute-start.12 = (bf16[3,128,128]{2,1,0:T(8,128)(2,1)}, bf16[3,128,128]{2,1,0:T(8,128)(2,1)S(1)}, u32[]{:S(2)}, u32[]{:S(2)}) collective-permute-start(bf16[3,128,128]{2,1,0:T(8,128)(2,1)} %get-tuple-element.50), channel_id=1, source_target_pairs={{0,12},{2,14},{4,8},{6,10},{8,4},{10,6},{12,0},{14,2},{1,13},{3,15... | collective-permute-start | bytes 294920 | tf_op jit(solution)/shard_map/ppermute | solution.py:442
  41.3 11.2 %collective-permute-start.14 = (bf16[1024,128]{1,0:T(8,128)(2,1)S(1)}, bf16[1024,128]{1,0:T(8,128)(2,1)S(1)}, u32[]{:S(2)}, u32[]{:S(2)}) collective-permute-start(bf16[1024,128]{1,0:T(8,128)(2,1)S(1)} %shard_map.74.refs_0_), channel_id=1, source_target_pairs={{0,4},{4,8},{8,12},{12,14},{14,10},{10,6},{6,2},{2,0},{1,5},{5,9},... | collective-permute-start | bytes 786440 | tf_op jit(solution)/shard_map/ppermute | solution.py:457
  50.5 9.3 %collective-permute-start.15 = (bf16[1024,128]{1,0:T(8,128)(2,1)S(1)}, bf16[1024,128]{1,0:T(8,128)(2,1)}, u32[]{:S(2)}, u32[]{:S(2)}) collective-permute-start(bf16[1024,128]{1,0:T(8,128)(2,1)S(1)} %shard_map.76.refs_1_), channel_id=1, source_target_pairs={{0,4},{4,8},{8,12},{12,14},{14,10},{10,6},{6,2},{2,0},{1,5},{5,9},... | collective-permute-start | bytes 786440 | tf_op jit(solution)/shard_map/ppermute | solution.py:457
  51.4 12.5 %collective-permute-start.16 = (bf16[1024,128]{1,0:T(8,128)(2,1)S(1)}, bf16[1024,128]{1,0:T(8,128)(2,1)}, u32[]{:S(2)}, u32[]{:S(2)}) collective-permute-start(bf16[1024,128]{1,0:T(8,128)(2,1)S(1)} %shard_map.74.refs_0_), channel_id=1, source_target_pairs={{4,0},{8,4},{12,8},{14,12},{10,14},{6,10},{2,6},{0,2},{5,1},{9,5},... | collective-permute-start | bytes 786440 | tf_op jit(solution)/shard_map/ppermute | solution.py:458
  52.5 12.9 %collective-permute-start.18 = (bf16[1024,128]{1,0:T(8,128)(2,1)S(1)}, bf16[1024,128]{1,0:T(8,128)(2,1)}, u32[]{:S(2)}, u32[]{:S(2)}) collective-permute-start(bf16[1024,128]{1,0:T(8,128)(2,1)S(1)} %collective-permute-done.14.refs_2_), channel_id=1, source_target_pairs={{0,4},{4,8},{8,12},{12,14},{14,10},{10,6},{6,2},{2,0},{1,5},{5,9},... | collective-permute-start | bytes 786440 | tf_op jit(solution)/shard_map/ppermute | solution.py:457
  58.1 11.3 %collective-permute-start.21 = (bf16[1024,128]{1,0:T(8,128)(2,1)S(1)}, bf16[1024,128]{1,0:T(8,128)(2,1)}, u32[]{:S(2)}, u32[]{:S(2)}) collective-permute-start(bf16[1024,128]{1,0:T(8,128)(2,1)S(1)} %collective-permute-done.17.refs_5_), channel_id=1, source_target_pairs={{4,0},{8,4},{12,8},{14,12},{10,14},{6,10},{2,6},{0,2},{5,1},{9,5},... | collective-permute-start | bytes 786440 | tf_op jit(solution)/shard_map/ppermute | solution.py:458
  59.8 11.2 %collective-permute-start.19 = (bf16[1024,128]{1,0:T(8,128)(2,1)}, bf16[1024,128]{1,0:T(8,128)(2,1)}, u32[]{:S(2)}, u32[]{:S(2)}) collective-permute-start(bf16[1024,128]{1,0:T(8,128)(2,1)} %collective-permute-done.15.refs_3_), channel_id=1, source_target_pairs={{0,4},{4,8},{8,12},{12,14},{14,10},{10,6},{6,2},{2,0},{1,5},{5,9},... | collective-permute-start | bytes 786440 | tf_op jit(solution)/shard_map/ppermute | solution.py:457
  63.9 11.2 %collective-permute-start.20 = (bf16[1024,128]{1,0:T(8,128)(2,1)}, bf16[1024,128]{1,0:T(8,128)(2,1)}, u32[]{:S(2)}, u32[]{:S(2)}) collective-permute-start(bf16[1024,128]{1,0:T(8,128)(2,1)} %collective-permute-done.16.refs_4_), channel_id=1, source_target_pairs={{4,0},{8,4},{12,8},{14,12},{10,14},{6,10},{2,6},{0,2},{5,1},{9,5},... | collective-permute-start | bytes 786440 | tf_op jit(solution)/shard_map/ppermute | solution.py:458
  65.5 11.2 %collective-permute-start.22 = (bf16[1024,128]{1,0:T(8,128)(2,1)}, bf16[1024,128]{1,0:T(8,128)(2,1)}, u32[]{:S(2)}, u32[]{:S(2)}) collective-permute-start(bf16[1024,128]{1,0:T(8,128)(2,1)} %collective-permute-done.18.refs_6_), channel_id=1, source_target_pairs={{0,4},{4,8},{8,12},{12,14},{14,10},{10,6},{6,2},{2,0},{1,5},{5,9},... | collective-permute-start | bytes 786440 | tf_op jit(solution)/shard_map/ppermute | solution.py:457
  69.5 11.1 %collective-permute-start.25 = (bf16[1024,128]{1,0:T(8,128)(2,1)}, bf16[1024,128]{1,0:T(8,128)(2,1)S(1)}, u32[]{:S(2)}, u32[]{:S(2)}) collective-permute-start(bf16[1024,128]{1,0:T(8,128)(2,1)} %collective-permute-done.21.refs_9_), channel_id=1, source_target_pairs={{4,0},{8,4},{12,8},{14,12},{10,14},{6,10},{2,6},{0,2},{5,1},{9,5},... | collective-permute-start | bytes 786440 | tf_op jit(solution)/shard_map/ppermute | solution.py:458
  71.1 10.9 %collective-permute-start.23 = (bf16[1024,128]{1,0:T(8,128)(2,1)}, bf16[1024,128]{1,0:T(8,128)(2,1)S(1)}, u32[]{:S(2)}, u32[]{:S(2)}) collective-permute-start(bf16[1024,128]{1,0:T(8,128)(2,1)} %collective-permute-done.19.refs_7_), channel_id=1, source_target_pairs={{0,4},{4,8},{8,12},{12,14},{14,10},{10,6},{6,2},{2,0},{1,5},{5,9},... | collective-permute-start | bytes 786440 | tf_op jit(solution)/shard_map/ppermute | solution.py:457
  75.1 10.2 %collective-permute-start.24 = (bf16[1024,128]{1,0:T(8,128)(2,1)}, bf16[1024,128]{1,0:T(8,128)(2,1)S(1)}, u32[]{:S(2)}, u32[]{:S(2)}) collective-permute-start(bf16[1024,128]{1,0:T(8,128)(2,1)} %collective-permute-done.20.refs_8_), channel_id=1, source_target_pairs={{4,0},{8,4},{12,8},{14,12},{10,14},{6,10},{2,6},{0,2},{5,1},{9,5},... | collective-permute-start | bytes 786440 | tf_op jit(solution)/shard_map/ppermute | solution.py:458
  90.8 9.5 %collective-permute-start.34 = (bf16[128,256]{1,0:T(8,128)(2,1)S(1)}, bf16[128,256]{1,0:T(8,128)(2,1)S(1)}, u32[]{:S(2)}, u32[]{:S(2)}) collective-permute-start(bf16[128,256]{1,0:T(8,128)(2,1)S(1)} %get-tuple-element.61), channel_id=1, source_target_pairs={{0,14},{2,12},{4,10},{6,8},{8,6},{10,4},{12,2},{14,0},{1,15},{3,13... | collective-permute-start | bytes 196616 | tf_op jit(solution)/shard_map/ppermute | solution.py:482
  (19 other events, 292.9 us)

commit v6 on v5

--- a/solution.py
+++ b/solution.py
@@ -310,16 +310,13 @@
 
 
 def late_kernel(owner_ref, side_ref, weight_ref, total_ref, *refs):
-    *pieces, send_ref, keep_ref = refs
-    half = send_ref.shape[1]
+    *pieces, out_ref = refs
+    half = out_ref.shape[1]
+    outs = pl.ds(pl.multiple_of(side_ref[0] * half, half), half)
     for start in range(0, total_ref.shape[0], TILE):
         tile = slice(start, start + TILE)
-        summed = total_ref[tile, :] + product_tile(owner_ref, pieces, weight_ref, tile)
-        low = summed[:, :half].astype(send_ref.dtype)
-        high = summed[:, half:].astype(send_ref.dtype)
-        first = side_ref[0] == 0
-        send_ref[tile, :] = jnp.where(first, high, low)
-        keep_ref[tile, :] = jnp.where(first, low, high)
+        product = product_tile(owner_ref, pieces, weight_ref.at[outs, :], tile)
+        out_ref[tile, :] = (total_ref[tile, outs] + product).astype(out_ref.dtype)
 
 
 def project_early(owners, pieces, weight):
@@ -344,10 +341,10 @@
     return pl.pallas_call(
         late_kernel,
         in_specs=[SCALARS] * 2 + [ARRAY] * (2 + len(pieces)),
-        out_shape=[jax.ShapeDtypeStruct((total, outs // 2), pieces[0].dtype)] * 2,
+        out_shape=jax.ShapeDtypeStruct((total, outs // 2), pieces[0].dtype),
         compiler_params=pltpu.CompilerParams(vmem_limit_bytes=VMEM),
         cost_estimate=pl.CostEstimate(
-            flops=2 * total * outs * width * len(pieces),
+            flops=total * outs * width * len(pieces),
             bytes_accessed=2 * len(pieces) * width * (total + outs) + 6 * total * outs,
             transcendentals=0,
         ),
@@ -473,9 +470,11 @@
     owners, pieces = gather_args(steps[:EARLY])
     so_far = project_early(owners, pieces, out_weight)
     owners, pieces = gather_args(steps[EARLY:])
-    send, keep = project_late(owners, head_index[None], pieces, out_weight, so_far)
+    send = project_late(owners, 1 - head_index[None], pieces, out_weight, so_far)
     swap = [(0, 1), (1, 0)]
-    parts = add_and_part(seq_index, keep, lax.ppermute(send, "head", swap), peers)
+    other = lax.ppermute(send, "head", swap)
+    keep = project_late(owners, head_index[None], pieces, out_weight, so_far)
+    parts = add_and_part(seq_index, keep, other, peers)
     arrived = {0: parts[0]}
     for apart in SEND_ORDER:
         pairs = [(i, i ^ apart) for i in range(peers)]

time: 110 us -> 110 us (level)
  waiting for transfers between devices: 36.5 us -> 35.4 us
  transfers between devices with their start and end apart: 37 -> 37, of which waited for: 18 -> 18; matrix products, arithmetic and copies ran while one was open for 1% -> 1% of each run, Pallas kernels for 11% -> 12%
where the time goes in v6:
time: 110 us
  starting transfers between devices  53.9 us (49%)
  waiting for transfers between devices  35.4 us (32%)
  Pallas kernels  17.1 us (16%)
  local copies, waits for them, and re-layouts  2.83 us (3%)
    ppermute x12, starting transfers between devices, local_by_heads(): lax.ppermute(outgoing[head * peers + apart], 'seq', pairs)  19.6 us
    ppermute x6, waiting for transfers between devices, local_by_heads(): behind = lax.ppermute(behind, 'seq', back)  17.5 us
    ppermute x7, starting transfers between devices, local_by_heads(): arrived[apart] = lax.ppermute(parts[apart], 'seq', pairs)  11.5 us
    ppermute x6, starting transfers between devices, local_by_heads(): behind = lax.ppermute(behind, 'seq', back)  8.55 us
    ppermute x2, starting transfers between devices, local_by_heads(): pieces[head, apart] = lax.ppermute(piece, 'seq', pairs)  7.8 us
    pallas_call x2, Pallas kernels, attend_head(): pl.pallas_call(functools.partial(attend_kernel, head), in_specs=[SCALARS]...  5.81 us
    ppermute x7, waiting for transfers between devices, local_by_heads(): arrived[apart] = lax.ppermute(parts[apart], 'seq', pairs)  5.19 us
    pallas_call x2, Pallas kernels, spread(): pl.pallas_call(functools.partial(spread_kernel, head), grid=(1,), in_spec...  4.93 us
  transfers between devices with their start and end apart: 37, of which 18 were waited for; matrix products, arithmetic and copies ran while one was open for 1% of the time, Pallas kernels for 12%

profile of v6, /device:TPU:0, one launch (start us, length us, event | category | flops | bytes accessed | tf_op | source)
XLA Modules:
  0.0 109.7 jit_solution(12970019122771329202)
XLA Ops:
  0.0 2.4 %shard_map.73 = (bf16[3,128,128]{2,1,0:T(8,128)(2,1)}, bf16[3,128,128]{2,1,0:T(8,128)(2,1)}, bf16[3,128,128]{2,1,0:T(8,128)(2,1)}, bf16[3,128,128]{2,1,0:T(8,128...) custom-call(s32[1]{0:T(128)} %bitcast.seq_ref.row_ref, ...), custom_call_target="tpu_custom_call" | custom-call | bytes 3145728 | tf_op jit(solution)/shard_map/pallas_call | solution.py:240
  2.4 3.0 %collective-permute-start = (bf16[3,128,128]{2,1,0:T(8,128)(2,1)}, bf16[3,128,128]{2,1,0:T(8,128)(2,1)S(1)}, u32[]{:S(2)}, u32[]{:S(2)}) collective-permute-start(bf16[3,128,128]{2,1,0:T(8,128)(2,1)} %get-tuple-element.33), channel_id=1, source_target_pairs={{0,2},{2,0},{4,6},{6,4},{8,10},{10,8},{12,14},{14,12},{1,3},{3,1},... | collective-permute-start | bytes 294920 | tf_op jit(solution)/shard_map/ppermute | solution.py:439
  7.0 3.0 %collective-permute-start.3 = (bf16[3,128,128]{2,1,0:T(8,128)(2,1)}, bf16[3,128,128]{2,1,0:T(8,128)(2,1)S(1)}, u32[]{:S(2)}, u32[]{:S(2)}) collective-permute-start(bf16[3,128,128]{2,1,0:T(8,128)(2,1)} %get-tuple-element.36), channel_id=1, source_target_pairs={{0,8},{2,10},{4,12},{6,14},{8,0},{10,2},{12,4},{14,6},{1,9},{3,11}... | collective-permute-start | bytes 294920 | tf_op jit(solution)/shard_map/ppermute | solution.py:439
  12.4 2.5 %shard_map.75 = (bf16[3,128,128]{2,1,0:T(8,128)(2,1)}, bf16[3,128,128]{2,1,0:T(8,128)(2,1)}, bf16[3,128,128]{2,1,0:T(8,128)(2,1)}, bf16[3,128,128]{2,1,0:T(8,128...) custom-call(s32[1]{0:T(128)} %bitcast.seq_ref.row_ref, ...), custom_call_target="tpu_custom_call" | custom-call | bytes 3145728 | tf_op jit(solution)/shard_map/pallas_call | solution.py:240
  14.9 3.7 %collective-permute-start.5 = (bf16[3,128,128]{2,1,0:T(8,128)(2,1)}, bf16[3,128,128]{2,1,0:T(8,128)(2,1)S(1)}, u32[]{:S(2)}, u32[]{:S(2)}) collective-permute-start(bf16[3,128,128]{2,1,0:T(8,128)(2,1)} %get-tuple-element.38), channel_id=1, source_target_pairs={{0,12},{2,14},{4,8},{6,10},{8,4},{10,6},{12,0},{14,2},{1,13},{3,15... | collective-permute-start | bytes 294920 | tf_op jit(solution)/shard_map/ppermute | solution.py:439
  20.4 3.9 %collective-permute-done.4.refs_5_ = bf16[3,128,128]{2,1,0:T(8,128)(2,1)S(1)} collective-permute-done((bf16[3,128,128]{2,1,0:T(8,128)(2,1)}, bf16[3,128,128]{2,1,0:T(8,128)(2,1)S(1)}, u32[]{:S(2)}, u32[]{:S(2)}) %collective-permute-start.4) | collective-permute-done | bytes 98336 | tf_op jit(solution)/shard_map/ppermute | solution.py:439
  24.8 4.1 %collective-permute-start.10 = (bf16[3,128,128]{2,1,0:T(8,128)(2,1)}, bf16[3,128,128]{2,1,0:T(8,128)(2,1)S(1)}, u32[]{:S(2)}, u32[]{:S(2)}) collective-permute-start(bf16[3,128,128]{2,1,0:T(8,128)(2,1)} %get-tuple-element.45), channel_id=1, source_target_pairs={{0,8},{2,10},{4,12},{6,14},{8,0},{10,2},{12,4},{14,6},{1,9},{3,11}... | collective-permute-start | bytes 294920 | tf_op jit(solution)/shard_map/ppermute | solution.py:439
  30.6 2.9 %shard_map.74.refs_0_ = bf16[1024,128]{1,0:T(8,128)(2,1)S(1)} custom-call(s32[1]{0:T(128)} %bitcast.seq_ref.row_ref, f32[2,8,1024]{2,1,0:T(8,128)S(1)} %broadcast_bitcast_fusion.bias_ref, bf16[3,128,128]{2,1,0:T(8,128)(2,1)S(1)} %copy-done.2, bf16[3,128,128]{2,1,0:T(8,128)(2,1)S(1)} %collective-permute-done.refs_1_, ...), custom_call_target="tpu_custom_call" | custom-call | flops 536870912 | bytes 1048576 | tf_op jit(solution)/shard_map/pallas_call | solution.py:276
  33.5 4.2 %collective-permute-start.11 = (bf16[3,128,128]{2,1,0:T(8,128)(2,1)}, bf16[3,128,128]{2,1,0:T(8,128)(2,1)S(1)}, u32[]{:S(2)}, u32[]{:S(2)}) collective-permute-start(bf16[3,128,128]{2,1,0:T(8,128)(2,1)} %get-tuple-element.47), channel_id=1, source_target_pairs={{0,10},{2,8},{4,14},{6,12},{8,2},{10,0},{12,6},{14,4},{1,11},{3,9}... | collective-permute-start | bytes 294920 | tf_op jit(solution)/shard_map/ppermute | solution.py:445
  37.7 3.6 %collective-permute-start.13 = (bf16[3,128,128]{2,1,0:T(8,128)(2,1)}, bf16[3,128,128]{2,1,0:T(8,128)(2,1)S(1)}, u32[]{:S(2)}, u32[]{:S(2)}) collective-permute-start(bf16[3,128,128]{2,1,0:T(8,128)(2,1)} %get-tuple-element.50), channel_id=1, source_target_pairs={{0,14},{2,12},{4,10},{6,8},{8,6},{10,4},{12,2},{14,0},{1,15},{3,13... | collective-permute-start | bytes 294920 | tf_op jit(solution)/shard_map/ppermute | solution.py:445
  42.7 2.7 %collective-permute-done.13.refs_7_ = bf16[3,128,128]{2,1,0:T(8,128)(2,1)S(1)} collective-permute-done((bf16[3,128,128]{2,1,0:T(8,128)(2,1)}, bf16[3,128,128]{2,1,0:T(8,128)(2,1)S(1)}, u32[]{:S(2)}, u32[]{:S(2)}) %collective-permute-start.13) | collective-permute-done | bytes 98336 | tf_op jit(solution)/shard_map/ppermute | solution.py:445
  46.2 2.9 %shard_map.76.refs_1_ = bf16[1024,128]{1,0:T(8,128)(2,1)S(1)} custom-call(s32[1]{0:T(128)} %bitcast.seq_ref.row_ref, f32[2,8,1024]{2,1,0:T(8,128)S(1)} %broadcast_bitcast_fusion.bias_ref, bf16[3,128,128]{2,1,0:T(8,128)(2,1)S(1)} %copy-done.3, bf16[3,128,128]{2,1,0:T(8,128)(2,1)S(1)} %collective-permute-done.7.refs_1_, ...), custom_call_target="tpu_custom_call" | custom-call | flops 536870912 | bytes 1048576 | tf_op jit(solution)/shard_map/pallas_call | solution.py:276
  53.4 4.7 %collective-permute-done.17.refs_5_ = bf16[1024,128]{1,0:T(8,128)(2,1)S(1)} collective-permute-done((bf16[1024,128]{1,0:T(8,128)(2,1)S(1)}, bf16[1024,128]{1,0:T(8,128)(2,1)S(1)}, u32[]{:S(2)}, u32[]{:S(2)}) %collective-permute-start.17) | collective-permute-done | bytes 262176 | tf_op jit(solution)/shard_map/ppermute | solution.py:455
  60.5 3.3 %collective-permute-done.16.refs_4_ = bf16[1024,128]{1,0:T(8,128)(2,1)} collective-permute-done((bf16[1024,128]{1,0:T(8,128)(2,1)S(1)}, bf16[1024,128]{1,0:T(8,128)(2,1)}, u32[]{:S(2)}, u32[]{:S(2)}) %collective-permute-start.16) | collective-permute-done | bytes 262176 | tf_op jit(solution)/shard_map/ppermute | solution.py:455
  66.3 3.2 %collective-permute-done.21.refs_9_ = bf16[1024,128]{1,0:T(8,128)(2,1)} collective-permute-done((bf16[1024,128]{1,0:T(8,128)(2,1)S(1)}, bf16[1024,128]{1,0:T(8,128)(2,1)}, u32[]{:S(2)}, u32[]{:S(2)}) %collective-permute-start.21) | collective-permute-done | bytes 262176 | tf_op jit(solution)/shard_map/ppermute | solution.py:455
  71.9 3.2 %collective-permute-done.20.refs_8_ = bf16[1024,128]{1,0:T(8,128)(2,1)} collective-permute-done((bf16[1024,128]{1,0:T(8,128)(2,1)}, bf16[1024,128]{1,0:T(8,128)(2,1)}, u32[]{:S(2)}, u32[]{:S(2)}) %collective-permute-start.20) | collective-permute-done | bytes 262176 | tf_op jit(solution)/shard_map/ppermute | solution.py:455
  77.5 3.1 %collective-permute-done.25.refs_1_ = bf16[1024,128]{1,0:T(8,128)(2,1)S(1)} collective-permute-done((bf16[1024,128]{1,0:T(8,128)(2,1)}, bf16[1024,128]{1,0:T(8,128)(2,1)S(1)}, u32[]{:S(2)}, u32[]{:S(2)}) %collective-permute-start.25) | collective-permute-done | bytes 262176 | tf_op jit(solution)/shard_map/ppermute | solution.py:455
  81.9 3.3 %shard_map.77.total_ref = f32[1024,512]{1,0:T(8,128)S(1)} custom-call(s32[6]{0:T(128)S(1)} %compare_select_fusion.5.owner_ref, bf16[512,2048]{1,0:T(8,128)(2,1)S(1)} %copy-done.1, bf16[1024,128]{1,0:T(8,128)(2,1)S(1)} %shard_map.74.refs_0_, bf16[1024,128]{1,0:T(8,128)(2,1)S(1)} %shard_map.76.refs_1_, bf16[1024,128]{1,0:T(8,128)(2,1)S(1)} %collective-permute-done.14.refs_2_, ...), custom_call_target="tpu_custom_call" | custom-call | flops 1610612736 | bytes 6815744 | tf_op jit(solution)/shard_map/pallas_call | solution.py:325
  85.3 2.1 %collective-permute-done.27.refs_3_ = bf16[1024,128]{1,0:T(8,128)(2,1)S(1)} collective-permute-done((bf16[1024,128]{1,0:T(8,128)(2,1)S(1)}, bf16[1024,128]{1,0:T(8,128)(2,1)S(1)}, u32[]{:S(2)}, u32[]{:S(2)}) %collective-permute-start.27) | collective-permute-done | bytes 262176 | tf_op jit(solution)/shard_map/ppermute | solution.py:461
  90.5 3.7 %collective-permute-start.34 = (bf16[128,256]{1,0:T(8,128)(2,1)S(1)}, bf16[128,256]{1,0:T(8,128)(2,1)S(1)}, u32[]{:S(2)}, u32[]{:S(2)}) collective-permute-start(bf16[128,256]{1,0:T(8,128)(2,1)S(1)} %get-tuple-element.57), channel_id=1, source_target_pairs={{0,14},{2,12},{4,10},{6,8},{8,6},{10,4},{12,2},{14,0},{1,15},{3,13... | collective-permute-start | bytes 196616 | tf_op jit(solution)/shard_map/ppermute | solution.py:481
  94.2 1.8 %collective-permute-start.35 = (bf16[128,256]{1,0:T(8,128)(2,1)S(1)}, bf16[128,256]{1,0:T(8,128)(2,1)S(1)}, u32[]{:S(2)}, u32[]{:S(2)}) collective-permute-start(bf16[128,256]{1,0:T(8,128)(2,1)S(1)} %get-tuple-element.58), channel_id=1, source_target_pairs={{0,6},{2,4},{4,2},{6,0},{8,14},{10,12},{12,10},{14,8},{1,7},{3,5},... | collective-permute-start | bytes 196616 | tf_op jit(solution)/shard_map/ppermute | solution.py:481
  97.2 2.8 %collective-permute-start.30 = (bf16[128,256]{1,0:T(8,128)(2,1)S(1)}, bf16[128,256]{1,0:T(8,128)(2,1)S(1)}, u32[]{:S(2)}, u32[]{:S(2)}) collective-permute-start(bf16[128,256]{1,0:T(8,128)(2,1)S(1)} %get-tuple-element.53), channel_id=1, source_target_pairs={{0,10},{2,8},{4,14},{6,12},{8,2},{10,0},{12,6},{14,4},{1,11},{3,9}... | collective-permute-start | bytes 196616 | tf_op jit(solution)/shard_map/ppermute | solution.py:481
  100.1 1.8 %collective-permute-start.31 = (bf16[128,256]{1,0:T(8,128)(2,1)S(1)}, bf16[128,256]{1,0:T(8,128)(2,1)S(1)}, u32[]{:S(2)}, u32[]{:S(2)}) collective-permute-start(bf16[128,256]{1,0:T(8,128)(2,1)S(1)} %get-tuple-element.54), channel_id=1, source_target_pairs={{0,2},{2,0},{4,6},{6,4},{8,10},{10,8},{12,14},{14,12},{1,3},{3,1},... | collective-permute-start | bytes 196616 | tf_op jit(solution)/shard_map/ppermute | solution.py:481
  102.9 2.5 %collective-permute-done.30.refs_5_ = bf16[128,256]{1,0:T(8,128)(2,1)S(1)} collective-permute-done((bf16[128,256]{1,0:T(8,128)(2,1)S(1)}, bf16[128,256]{1,0:T(8,128)(2,1)S(1)}, u32[]{:S(2)}, u32[]{:S(2)}) %collective-permute-start.30) | collective-permute-done | bytes 65568 | tf_op jit(solution)/shard_map/ppermute | solution.py:481
  (91 shorter events, 35.1 us)
Async XLA Ops:
  2.4 12.5 %collective-permute-start = (bf16[3,128,128]{2,1,0:T(8,128)(2,1)}, bf16[3,128,128]{2,1,0:T(8,128)(2,1)S(1)}, u32[]{:S(2)}, u32[]{:S(2)}) collective-permute-start(bf16[3,128,128]{2,1,0:T(8,128)(2,1)} %get-tuple-element.33), channel_id=1, source_target_pairs={{0,2},{2,0},{4,6},{6,4},{8,10},{10,8},{12,14},{14,12},{1,3},{3,1},... | collective-permute-start | bytes 294920 | tf_op jit(solution)/shard_map/ppermute | solution.py:439
  5.4 13.2 %collective-permute-start.1 = (bf16[3,128,128]{2,1,0:T(8,128)(2,1)}, bf16[3,128,128]{2,1,0:T(8,128)(2,1)S(1)}, u32[]{:S(2)}, u32[]{:S(2)}) collective-permute-start(bf16[3,128,128]{2,1,0:T(8,128)(2,1)} %get-tuple-element.34), channel_id=1, source_target_pairs={{0,4},{2,6},{4,0},{6,2},{8,12},{10,14},{12,8},{14,10},{1,5},{3,7},... | collective-permute-start | bytes 294920 | tf_op jit(solution)/shard_map/ppermute | solution.py:439
  7.0 11.7 %collective-permute-start.2 = (bf16[3,128,128]{2,1,0:T(8,128)(2,1)}, bf16[3,128,128]{2,1,0:T(8,128)(2,1)S(1)}, u32[]{:S(2)}, u32[]{:S(2)}) collective-permute-start(bf16[3,128,128]{2,1,0:T(8,128)(2,1)} %get-tuple-element.35), channel_id=1, source_target_pairs={{0,6},{2,4},{4,2},{6,0},{8,14},{10,12},{12,10},{14,8},{1,7},{3,5},... | collective-permute-start | bytes 294920 | tf_op jit(solution)/shard_map/ppermute | solution.py:439
  7.0 13.3 %collective-permute-start.3 = (bf16[3,128,128]{2,1,0:T(8,128)(2,1)}, bf16[3,128,128]{2,1,0:T(8,128)(2,1)S(1)}, u32[]{:S(2)}, u32[]{:S(2)}) collective-permute-start(bf16[3,128,128]{2,1,0:T(8,128)(2,1)} %get-tuple-element.36), channel_id=1, source_target_pairs={{0,8},{2,10},{4,12},{6,14},{8,0},{10,2},{12,4},{14,6},{1,9},{3,11}... | collective-permute-start | bytes 294920 | tf_op jit(solution)/shard_map/ppermute | solution.py:439
  10.0 14.4 %collective-permute-start.4 = (bf16[3,128,128]{2,1,0:T(8,128)(2,1)}, bf16[3,128,128]{2,1,0:T(8,128)(2,1)S(1)}, u32[]{:S(2)}, u32[]{:S(2)}) collective-permute-start(bf16[3,128,128]{2,1,0:T(8,128)(2,1)} %get-tuple-element.37), channel_id=1, source_target_pairs={{0,10},{2,8},{4,14},{6,12},{8,2},{10,0},{12,6},{14,4},{1,11},{3,9}... | collective-permute-start | bytes 294920 | tf_op jit(solution)/shard_map/ppermute | solution.py:439
  14.9 9.9 %collective-permute-start.5 = (bf16[3,128,128]{2,1,0:T(8,128)(2,1)}, bf16[3,128,128]{2,1,0:T(8,128)(2,1)S(1)}, u32[]{:S(2)}, u32[]{:S(2)}) collective-permute-start(bf16[3,128,128]{2,1,0:T(8,128)(2,1)} %get-tuple-element.38), channel_id=1, source_target_pairs={{0,12},{2,14},{4,8},{6,10},{8,4},{10,6},{12,0},{14,2},{1,13},{3,15... | collective-permute-start | bytes 294920 | tf_op jit(solution)/shard_map/ppermute | solution.py:439
  18.6 10.3 %collective-permute-start.6 = (bf16[3,128,128]{2,1,0:T(8,128)(2,1)}, bf16[3,128,128]{2,1,0:T(8,128)(2,1)S(1)}, u32[]{:S(2)}, u32[]{:S(2)}) collective-permute-start(bf16[3,128,128]{2,1,0:T(8,128)(2,1)} %get-tuple-element.39), channel_id=1, source_target_pairs={{0,14},{2,12},{4,10},{6,8},{8,6},{10,4},{12,2},{14,0},{1,15},{3,13... | collective-permute-start | bytes 294920 | tf_op jit(solution)/shard_map/ppermute | solution.py:439
  18.6 14.9 %collective-permute-start.7 = (bf16[3,128,128]{2,1,0:T(8,128)(2,1)}, bf16[3,128,128]{2,1,0:T(8,128)(2,1)S(1)}, u32[]{:S(2)}, u32[]{:S(2)}) collective-permute-start(bf16[3,128,128]{2,1,0:T(8,128)(2,1)} %get-tuple-element.42), channel_id=1, source_target_pairs={{0,2},{2,0},{4,6},{6,4},{8,10},{10,8},{12,14},{14,12},{1,3},{3,1},... | collective-permute-start | bytes 294920 | tf_op jit(solution)/shard_map/ppermute | solution.py:439
  20.3 17.4 %collective-permute-start.8 = (bf16[3,128,128]{2,1,0:T(8,128)(2,1)}, bf16[3,128,128]{2,1,0:T(8,128)(2,1)S(1)}, u32[]{:S(2)}, u32[]{:S(2)}) collective-permute-start(bf16[3,128,128]{2,1,0:T(8,128)(2,1)} %get-tuple-element.43), channel_id=1, source_target_pairs={{0,4},{2,6},{4,0},{6,2},{8,12},{10,14},{12,8},{14,10},{1,5},{3,7},... | collective-permute-start | bytes 294920 | tf_op jit(solution)/shard_map/ppermute | solution.py:439
  24.3 17.0 %collective-permute-start.9 = (bf16[3,128,128]{2,1,0:T(8,128)(2,1)}, bf16[3,128,128]{2,1,0:T(8,128)(2,1)S(1)}, u32[]{:S(2)}, u32[]{:S(2)}) collective-permute-start(bf16[3,128,128]{2,1,0:T(8,128)(2,1)} %get-tuple-element.44), channel_id=1, source_target_pairs={{0,6},{2,4},{4,2},{6,0},{8,14},{10,12},{12,10},{14,8},{1,7},{3,5},... | collective-permute-start | bytes 294920 | tf_op jit(solution)/shard_map/ppermute | solution.py:439
  24.8 16.5 %collective-permute-start.10 = (bf16[3,128,128]{2,1,0:T(8,128)(2,1)}, bf16[3,128,128]{2,1,0:T(8,128)(2,1)S(1)}, u32[]{:S(2)}, u32[]{:S(2)}) collective-permute-start(bf16[3,128,128]{2,1,0:T(8,128)(2,1)} %get-tuple-element.45), channel_id=1, source_target_pairs={{0,8},{2,10},{4,12},{6,14},{8,0},{10,2},{12,4},{14,6},{1,9},{3,11}... | collective-permute-start | bytes 294920 | tf_op jit(solution)/shard_map/ppermute | solution.py:439
  28.9 12.4 %collective-permute-start.12 = (bf16[3,128,128]{2,1,0:T(8,128)(2,1)}, bf16[3,128,128]{2,1,0:T(8,128)(2,1)S(1)}, u32[]{:S(2)}, u32[]{:S(2)}) collective-permute-start(bf16[3,128,128]{2,1,0:T(8,128)(2,1)} %get-tuple-element.48), channel_id=1, source_target_pairs={{0,12},{2,14},{4,8},{6,10},{8,4},{10,6},{12,0},{14,2},{1,13},{3,15... | collective-permute-start | bytes 294920 | tf_op jit(solution)/shard_map/ppermute | solution.py:439
  41.3 11.1 %collective-permute-start.14 = (bf16[1024,128]{1,0:T(8,128)(2,1)S(1)}, bf16[1024,128]{1,0:T(8,128)(2,1)S(1)}, u32[]{:S(2)}, u32[]{:S(2)}) collective-permute-start(bf16[1024,128]{1,0:T(8,128)(2,1)S(1)} %shard_map.74.refs_0_), channel_id=1, source_target_pairs={{0,4},{4,8},{8,12},{12,14},{14,10},{10,6},{6,2},{2,0},{1,5},{5,9},... | collective-permute-start | bytes 786440 | tf_op jit(solution)/shard_map/ppermute | solution.py:454
  50.5 9.4 %collective-permute-start.15 = (bf16[1024,128]{1,0:T(8,128)(2,1)S(1)}, bf16[1024,128]{1,0:T(8,128)(2,1)}, u32[]{:S(2)}, u32[]{:S(2)}) collective-permute-start(bf16[1024,128]{1,0:T(8,128)(2,1)S(1)} %shard_map.76.refs_1_), channel_id=1, source_target_pairs={{0,4},{4,8},{8,12},{12,14},{14,10},{10,6},{6,2},{2,0},{1,5},{5,9},... | collective-permute-start | bytes 786440 | tf_op jit(solution)/shard_map/ppermute | solution.py:454
  51.4 12.5 %collective-permute-start.16 = (bf16[1024,128]{1,0:T(8,128)(2,1)S(1)}, bf16[1024,128]{1,0:T(8,128)(2,1)}, u32[]{:S(2)}, u32[]{:S(2)}) collective-permute-start(bf16[1024,128]{1,0:T(8,128)(2,1)S(1)} %shard_map.74.refs_0_), channel_id=1, source_target_pairs={{4,0},{8,4},{12,8},{14,12},{10,14},{6,10},{2,6},{0,2},{5,1},{9,5},... | collective-permute-start | bytes 786440 | tf_op jit(solution)/shard_map/ppermute | solution.py:455
  52.5 12.9 %collective-permute-start.18 = (bf16[1024,128]{1,0:T(8,128)(2,1)S(1)}, bf16[1024,128]{1,0:T(8,128)(2,1)}, u32[]{:S(2)}, u32[]{:S(2)}) collective-permute-start(bf16[1024,128]{1,0:T(8,128)(2,1)S(1)} %collective-permute-done.14.refs_2_), channel_id=1, source_target_pairs={{0,4},{4,8},{8,12},{12,14},{14,10},{10,6},{6,2},{2,0},{1,5},{5,9},... | collective-permute-start | bytes 786440 | tf_op jit(solution)/shard_map/ppermute | solution.py:454
  58.1 11.3 %collective-permute-start.21 = (bf16[1024,128]{1,0:T(8,128)(2,1)S(1)}, bf16[1024,128]{1,0:T(8,128)(2,1)}, u32[]{:S(2)}, u32[]{:S(2)}) collective-permute-start(bf16[1024,128]{1,0:T(8,128)(2,1)S(1)} %collective-permute-done.17.refs_5_), channel_id=1, source_target_pairs={{4,0},{8,4},{12,8},{14,12},{10,14},{6,10},{2,6},{0,2},{5,1},{9,5},... | collective-permute-start | bytes 786440 | tf_op jit(solution)/shard_map/ppermute | solution.py:455
  59.8 11.2 %collective-permute-start.19 = (bf16[1024,128]{1,0:T(8,128)(2,1)}, bf16[1024,128]{1,0:T(8,128)(2,1)}, u32[]{:S(2)}, u32[]{:S(2)}) collective-permute-start(bf16[1024,128]{1,0:T(8,128)(2,1)} %collective-permute-done.15.refs_3_), channel_id=1, source_target_pairs={{0,4},{4,8},{8,12},{12,14},{14,10},{10,6},{6,2},{2,0},{1,5},{5,9},... | collective-permute-start | bytes 786440 | tf_op jit(solution)/shard_map/ppermute | solution.py:454
  63.8 11.2 %collective-permute-start.20 = (bf16[1024,128]{1,0:T(8,128)(2,1)}, bf16[1024,128]{1,0:T(8,128)(2,1)}, u32[]{:S(2)}, u32[]{:S(2)}) collective-permute-start(bf16[1024,128]{1,0:T(8,128)(2,1)} %collective-permute-done.16.refs_4_), channel_id=1, source_target_pairs={{4,0},{8,4},{12,8},{14,12},{10,14},{6,10},{2,6},{0,2},{5,1},{9,5},... | collective-permute-start | bytes 786440 | tf_op jit(solution)/shard_map/ppermute | solution.py:455
  65.4 11.2 %collective-permute-start.22 = (bf16[1024,128]{1,0:T(8,128)(2,1)}, bf16[1024,128]{1,0:T(8,128)(2,1)}, u32[]{:S(2)}, u32[]{:S(2)}) collective-permute-start(bf16[1024,128]{1,0:T(8,128)(2,1)} %collective-permute-done.18.refs_6_), channel_id=1, source_target_pairs={{0,4},{4,8},{8,12},{12,14},{14,10},{10,6},{6,2},{2,0},{1,5},{5,9},... | collective-permute-start | bytes 786440 | tf_op jit(solution)/shard_map/ppermute | solution.py:454
  69.5 11.1 %collective-permute-start.25 = (bf16[1024,128]{1,0:T(8,128)(2,1)}, bf16[1024,128]{1,0:T(8,128)(2,1)S(1)}, u32[]{:S(2)}, u32[]{:S(2)}) collective-permute-start(bf16[1024,128]{1,0:T(8,128)(2,1)} %collective-permute-done.21.refs_9_), channel_id=1, source_target_pairs={{4,0},{8,4},{12,8},{14,12},{10,14},{6,10},{2,6},{0,2},{5,1},{9,5},... | collective-permute-start | bytes 786440 | tf_op jit(solution)/shard_map/ppermute | solution.py:455
  71.0 10.9 %collective-permute-start.23 = (bf16[1024,128]{1,0:T(8,128)(2,1)}, bf16[1024,128]{1,0:T(8,128)(2,1)S(1)}, u32[]{:S(2)}, u32[]{:S(2)}) collective-permute-start(bf16[1024,128]{1,0:T(8,128)(2,1)} %collective-permute-done.19.refs_7_), channel_id=1, source_target_pairs={{0,4},{4,8},{8,12},{12,14},{14,10},{10,6},{6,2},{2,0},{1,5},{5,9},... | collective-permute-start | bytes 786440 | tf_op jit(solution)/shard_map/ppermute | solution.py:454
  75.1 10.2 %collective-permute-start.24 = (bf16[1024,128]{1,0:T(8,128)(2,1)}, bf16[1024,128]{1,0:T(8,128)(2,1)S(1)}, u32[]{:S(2)}, u32[]{:S(2)}) collective-permute-start(bf16[1024,128]{1,0:T(8,128)(2,1)} %collective-permute-done.20.refs_8_), channel_id=1, source_target_pairs={{4,0},{8,4},{12,8},{14,12},{10,14},{6,10},{2,6},{0,2},{5,1},{9,5},... | collective-permute-start | bytes 786440 | tf_op jit(solution)/shard_map/ppermute | solution.py:455
  90.5 9.5 %collective-permute-start.34 = (bf16[128,256]{1,0:T(8,128)(2,1)S(1)}, bf16[128,256]{1,0:T(8,128)(2,1)S(1)}, u32[]{:S(2)}, u32[]{:S(2)}) collective-permute-start(bf16[128,256]{1,0:T(8,128)(2,1)S(1)} %get-tuple-element.57), channel_id=1, source_target_pairs={{0,14},{2,12},{4,10},{6,8},{8,6},{10,4},{12,2},{14,0},{1,15},{3,13... | collective-permute-start | bytes 196616 | tf_op jit(solution)/shard_map/ppermute | solution.py:481
  (19 other events, 292.9 us)

commit v7 on v6

--- a/solution.py
+++ b/solution.py
@@ -18,7 +18,7 @@
 EARLY_STEPS = 0
 HELD = 2
 ROWS_ORDER = ((4, 6, 2, 3, 1, 5, 7), (4, 6, 2, 3, 1, 5, 7))
-SEND_ORDER = (4, 6, 5, 7, 2, 3, 1)
+SEND_ORDER = (2, 4, 1, 6, 3, 5, 7)
 SCALARS = pl.BlockSpec(memory_space=pltpu.SMEM)
 ARRAY = pl.BlockSpec(memory_space=pltpu.VMEM)
 

time: 110 us -> 110 us (level)
  no operation moved by 1% of the time
where the time goes in v7:
time: 110 us
  starting transfers between devices  53.9 us (49%)
  waiting for transfers between devices  35.4 us (32%)
  Pallas kernels  17.1 us (16%)
  local copies, waits for them, and re-layouts  2.83 us (3%)
    ppermute x12, starting transfers between devices, local_by_heads(): lax.ppermute(outgoing[head * peers + apart], 'seq', pairs)  19.6 us
    ppermute x6, waiting for transfers between devices, local_by_heads(): behind = lax.ppermute(behind, 'seq', back)  17.5 us
    ppermute x7, starting transfers between devices, local_by_heads(): arrived[apart] = lax.ppermute(parts[apart], 'seq', pairs)  11.5 us
    ppermute x6, starting transfers between devices, local_by_heads(): behind = lax.ppermute(behind, 'seq', back)  8.55 us
    ppermute x2, starting transfers between devices, local_by_heads(): pieces[head, apart] = lax.ppermute(piece, 'seq', pairs)  7.8 us
    pallas_call x2, Pallas kernels, attend_head(): pl.pallas_call(functools.partial(attend_kernel, head), in_specs=[SCALARS]...  5.81 us
    ppermute x7, waiting for transfers between devices, local_by_heads(): arrived[apart] = lax.ppermute(parts[apart], 'seq', pairs)  5.19 us
    pallas_call x2, Pallas kernels, spread(): pl.pallas_call(functools.partial(spread_kernel, head), grid=(1,), in_spec...  4.93 us
  transfers between devices with their start and end apart: 37, of which 18 were waited for; matrix products, arithmetic and copies ran while one was open for 1% of the time, Pallas kernels for 12%

profile of v7, /device:TPU:0, one launch (start us, length us, event | category | flops | bytes accessed | tf_op | source)
XLA Modules:
  0.0 109.7 jit_solution(12970019122771329202)
XLA Ops:
  0.0 2.4 %shard_map.73 = (bf16[3,128,128]{2,1,0:T(8,128)(2,1)}, bf16[3,128,128]{2,1,0:T(8,128)(2,1)}, bf16[3,128,128]{2,1,0:T(8,128)(2,1)}, bf16[3,128,128]{2,1,0:T(8,128...) custom-call(s32[1]{0:T(128)} %bitcast.seq_ref.row_ref, ...), custom_call_target="tpu_custom_call" | custom-call | bytes 3145728 | tf_op jit(solution)/shard_map/pallas_call | solution.py:240
  2.4 3.0 %collective-permute-start = (bf16[3,128,128]{2,1,0:T(8,128)(2,1)}, bf16[3,128,128]{2,1,0:T(8,128)(2,1)S(1)}, u32[]{:S(2)}, u32[]{:S(2)}) collective-permute-start(bf16[3,128,128]{2,1,0:T(8,128)(2,1)} %get-tuple-element.33), channel_id=1, source_target_pairs={{0,2},{2,0},{4,6},{6,4},{8,10},{10,8},{12,14},{14,12},{1,3},{3,1},... | collective-permute-start | bytes 294920 | tf_op jit(solution)/shard_map/ppermute | solution.py:439
  7.0 3.0 %collective-permute-start.3 = (bf16[3,128,128]{2,1,0:T(8,128)(2,1)}, bf16[3,128,128]{2,1,0:T(8,128)(2,1)S(1)}, u32[]{:S(2)}, u32[]{:S(2)}) collective-permute-start(bf16[3,128,128]{2,1,0:T(8,128)(2,1)} %get-tuple-element.36), channel_id=1, source_target_pairs={{0,8},{2,10},{4,12},{6,14},{8,0},{10,2},{12,4},{14,6},{1,9},{3,11}... | collective-permute-start | bytes 294920 | tf_op jit(solution)/shard_map/ppermute | solution.py:439
  12.4 2.5 %shard_map.75 = (bf16[3,128,128]{2,1,0:T(8,128)(2,1)}, bf16[3,128,128]{2,1,0:T(8,128)(2,1)}, bf16[3,128,128]{2,1,0:T(8,128)(2,1)}, bf16[3,128,128]{2,1,0:T(8,128...) custom-call(s32[1]{0:T(128)} %bitcast.seq_ref.row_ref, ...), custom_call_target="tpu_custom_call" | custom-call | bytes 3145728 | tf_op jit(solution)/shard_map/pallas_call | solution.py:240
  14.9 3.7 %collective-permute-start.5 = (bf16[3,128,128]{2,1,0:T(8,128)(2,1)}, bf16[3,128,128]{2,1,0:T(8,128)(2,1)S(1)}, u32[]{:S(2)}, u32[]{:S(2)}) collective-permute-start(bf16[3,128,128]{2,1,0:T(8,128)(2,1)} %get-tuple-element.38), channel_id=1, source_target_pairs={{0,12},{2,14},{4,8},{6,10},{8,4},{10,6},{12,0},{14,2},{1,13},{3,15... | collective-permute-start | bytes 294920 | tf_op jit(solution)/shard_map/ppermute | solution.py:439
  20.4 3.9 %collective-permute-done.4.refs_5_ = bf16[3,128,128]{2,1,0:T(8,128)(2,1)S(1)} collective-permute-done((bf16[3,128,128]{2,1,0:T(8,128)(2,1)}, bf16[3,128,128]{2,1,0:T(8,128)(2,1)S(1)}, u32[]{:S(2)}, u32[]{:S(2)}) %collective-permute-start.4) | collective-permute-done | bytes 98336 | tf_op jit(solution)/shard_map/ppermute | solution.py:439
  24.8 4.1 %collective-permute-start.10 = (bf16[3,128,128]{2,1,0:T(8,128)(2,1)}, bf16[3,128,128]{2,1,0:T(8,128)(2,1)S(1)}, u32[]{:S(2)}, u32[]{:S(2)}) collective-permute-start(bf16[3,128,128]{2,1,0:T(8,128)(2,1)} %get-tuple-element.45), channel_id=1, source_target_pairs={{0,8},{2,10},{4,12},{6,14},{8,0},{10,2},{12,4},{14,6},{1,9},{3,11}... | collective-permute-start | bytes 294920 | tf_op jit(solution)/shard_map/ppermute | solution.py:439
  30.6 2.9 %shard_map.74.refs_0_ = bf16[1024,128]{1,0:T(8,128)(2,1)S(1)} custom-call(s32[1]{0:T(128)} %bitcast.seq_ref.row_ref, f32[2,8,1024]{2,1,0:T(8,128)S(1)} %broadcast_bitcast_fusion.bias_ref, bf16[3,128,128]{2,1,0:T(8,128)(2,1)S(1)} %copy-done.2, bf16[3,128,128]{2,1,0:T(8,128)(2,1)S(1)} %collective-permute-done.refs_1_, ...), custom_call_target="tpu_custom_call" | custom-call | flops 536870912 | bytes 1048576 | tf_op jit(solution)/shard_map/pallas_call | solution.py:276
  33.5 4.2 %collective-permute-start.11 = (bf16[3,128,128]{2,1,0:T(8,128)(2,1)}, bf16[3,128,128]{2,1,0:T(8,128)(2,1)S(1)}, u32[]{:S(2)}, u32[]{:S(2)}) collective-permute-start(bf16[3,128,128]{2,1,0:T(8,128)(2,1)} %get-tuple-element.47), channel_id=1, source_target_pairs={{0,10},{2,8},{4,14},{6,12},{8,2},{10,0},{12,6},{14,4},{1,11},{3,9}... | collective-permute-start | bytes 294920 | tf_op jit(solution)/shard_map/ppermute | solution.py:445
  37.7 3.6 %collective-permute-start.13 = (bf16[3,128,128]{2,1,0:T(8,128)(2,1)}, bf16[3,128,128]{2,1,0:T(8,128)(2,1)S(1)}, u32[]{:S(2)}, u32[]{:S(2)}) collective-permute-start(bf16[3,128,128]{2,1,0:T(8,128)(2,1)} %get-tuple-element.50), channel_id=1, source_target_pairs={{0,14},{2,12},{4,10},{6,8},{8,6},{10,4},{12,2},{14,0},{1,15},{3,13... | collective-permute-start | bytes 294920 | tf_op jit(solution)/shard_map/ppermute | solution.py:445
  42.7 2.7 %collective-permute-done.13.refs_7_ = bf16[3,128,128]{2,1,0:T(8,128)(2,1)S(1)} collective-permute-done((bf16[3,128,128]{2,1,0:T(8,128)(2,1)}, bf16[3,128,128]{2,1,0:T(8,128)(2,1)S(1)}, u32[]{:S(2)}, u32[]{:S(2)}) %collective-permute-start.13) | collective-permute-done | bytes 98336 | tf_op jit(solution)/shard_map/ppermute | solution.py:445
  46.2 2.9 %shard_map.76.refs_1_ = bf16[1024,128]{1,0:T(8,128)(2,1)S(1)} custom-call(s32[1]{0:T(128)} %bitcast.seq_ref.row_ref, f32[2,8,1024]{2,1,0:T(8,128)S(1)} %broadcast_bitcast_fusion.bias_ref, bf16[3,128,128]{2,1,0:T(8,128)(2,1)S(1)} %copy-done.3, bf16[3,128,128]{2,1,0:T(8,128)(2,1)S(1)} %collective-permute-done.7.refs_1_, ...), custom_call_target="tpu_custom_call" | custom-call | flops 536870912 | bytes 1048576 | tf_op jit(solution)/shard_map/pallas_call | solution.py:276
  53.4 4.7 %collective-permute-done.17.refs_5_ = bf16[1024,128]{1,0:T(8,128)(2,1)S(1)} collective-permute-done((bf16[1024,128]{1,0:T(8,128)(2,1)S(1)}, bf16[1024,128]{1,0:T(8,128)(2,1)S(1)}, u32[]{:S(2)}, u32[]{:S(2)}) %collective-permute-start.17) | collective-permute-done | bytes 262176 | tf_op jit(solution)/shard_map/ppermute | solution.py:455
  60.5 3.3 %collective-permute-done.16.refs_4_ = bf16[1024,128]{1,0:T(8,128)(2,1)} collective-permute-done((bf16[1024,128]{1,0:T(8,128)(2,1)S(1)}, bf16[1024,128]{1,0:T(8,128)(2,1)}, u32[]{:S(2)}, u32[]{:S(2)}) %collective-permute-start.16) | collective-permute-done | bytes 262176 | tf_op jit(solution)/shard_map/ppermute | solution.py:455
  66.3 3.2 %collective-permute-done.21.refs_9_ = bf16[1024,128]{1,0:T(8,128)(2,1)} collective-permute-done((bf16[1024,128]{1,0:T(8,128)(2,1)S(1)}, bf16[1024,128]{1,0:T(8,128)(2,1)}, u32[]{:S(2)}, u32[]{:S(2)}) %collective-permute-start.21) | collective-permute-done | bytes 262176 | tf_op jit(solution)/shard_map/ppermute | solution.py:455
  71.9 3.2 %collective-permute-done.20.refs_8_ = bf16[1024,128]{1,0:T(8,128)(2,1)} collective-permute-done((bf16[1024,128]{1,0:T(8,128)(2,1)}, bf16[1024,128]{1,0:T(8,128)(2,1)}, u32[]{:S(2)}, u32[]{:S(2)}) %collective-permute-start.20) | collective-permute-done | bytes 262176 | tf_op jit(solution)/shard_map/ppermute | solution.py:455
  77.5 3.1 %collective-permute-done.25.refs_1_ = bf16[1024,128]{1,0:T(8,128)(2,1)S(1)} collective-permute-done((bf16[1024,128]{1,0:T(8,128)(2,1)}, bf16[1024,128]{1,0:T(8,128)(2,1)S(1)}, u32[]{:S(2)}, u32[]{:S(2)}) %collective-permute-start.25) | collective-permute-done | bytes 262176 | tf_op jit(solution)/shard_map/ppermute | solution.py:455
  81.9 3.3 %shard_map.77.total_ref = f32[1024,512]{1,0:T(8,128)S(1)} custom-call(s32[6]{0:T(128)S(1)} %compare_select_fusion.5.owner_ref, bf16[512,2048]{1,0:T(8,128)(2,1)S(1)} %copy-done.1, bf16[1024,128]{1,0:T(8,128)(2,1)S(1)} %shard_map.74.refs_0_, bf16[1024,128]{1,0:T(8,128)(2,1)S(1)} %shard_map.76.refs_1_, bf16[1024,128]{1,0:T(8,128)(2,1)S(1)} %collective-permute-done.14.refs_2_, ...), custom_call_target="tpu_custom_call" | custom-call | flops 1610612736 | bytes 6815744 | tf_op jit(solution)/shard_map/pallas_call | solution.py:325
  85.3 2.1 %collective-permute-done.27.refs_3_ = bf16[1024,128]{1,0:T(8,128)(2,1)S(1)} collective-permute-done((bf16[1024,128]{1,0:T(8,128)(2,1)S(1)}, bf16[1024,128]{1,0:T(8,128)(2,1)S(1)}, u32[]{:S(2)}, u32[]{:S(2)}) %collective-permute-start.27) | collective-permute-done | bytes 262176 | tf_op jit(solution)/shard_map/ppermute | solution.py:461
  90.5 3.7 %collective-permute-start.34 = (bf16[128,256]{1,0:T(8,128)(2,1)S(1)}, bf16[128,256]{1,0:T(8,128)(2,1)S(1)}, u32[]{:S(2)}, u32[]{:S(2)}) collective-permute-start(bf16[128,256]{1,0:T(8,128)(2,1)S(1)} %get-tuple-element.57), channel_id=1, source_target_pairs={{0,14},{2,12},{4,10},{6,8},{8,6},{10,4},{12,2},{14,0},{1,15},{3,13... | collective-permute-start | bytes 196616 | tf_op jit(solution)/shard_map/ppermute | solution.py:481
  94.2 1.8 %collective-permute-start.35 = (bf16[128,256]{1,0:T(8,128)(2,1)S(1)}, bf16[128,256]{1,0:T(8,128)(2,1)S(1)}, u32[]{:S(2)}, u32[]{:S(2)}) collective-permute-start(bf16[128,256]{1,0:T(8,128)(2,1)S(1)} %get-tuple-element.58), channel_id=1, source_target_pairs={{0,6},{2,4},{4,2},{6,0},{8,14},{10,12},{12,10},{14,8},{1,7},{3,5},... | collective-permute-start | bytes 196616 | tf_op jit(solution)/shard_map/ppermute | solution.py:481
  97.2 2.8 %collective-permute-start.30 = (bf16[128,256]{1,0:T(8,128)(2,1)S(1)}, bf16[128,256]{1,0:T(8,128)(2,1)S(1)}, u32[]{:S(2)}, u32[]{:S(2)}) collective-permute-start(bf16[128,256]{1,0:T(8,128)(2,1)S(1)} %get-tuple-element.53), channel_id=1, source_target_pairs={{0,10},{2,8},{4,14},{6,12},{8,2},{10,0},{12,6},{14,4},{1,11},{3,9}... | collective-permute-start | bytes 196616 | tf_op jit(solution)/shard_map/ppermute | solution.py:481
  100.1 1.8 %collective-permute-start.31 = (bf16[128,256]{1,0:T(8,128)(2,1)S(1)}, bf16[128,256]{1,0:T(8,128)(2,1)S(1)}, u32[]{:S(2)}, u32[]{:S(2)}) collective-permute-start(bf16[128,256]{1,0:T(8,128)(2,1)S(1)} %get-tuple-element.54), channel_id=1, source_target_pairs={{0,2},{2,0},{4,6},{6,4},{8,10},{10,8},{12,14},{14,12},{1,3},{3,1},... | collective-permute-start | bytes 196616 | tf_op jit(solution)/shard_map/ppermute | solution.py:481
  102.9 2.5 %collective-permute-done.30.refs_5_ = bf16[128,256]{1,0:T(8,128)(2,1)S(1)} collective-permute-done((bf16[128,256]{1,0:T(8,128)(2,1)S(1)}, bf16[128,256]{1,0:T(8,128)(2,1)S(1)}, u32[]{:S(2)}, u32[]{:S(2)}) %collective-permute-start.30) | collective-permute-done | bytes 65568 | tf_op jit(solution)/shard_map/ppermute | solution.py:481
  (91 shorter events, 35.1 us)
Async XLA Ops:
  2.4 12.5 %collective-permute-start = (bf16[3,128,128]{2,1,0:T(8,128)(2,1)}, bf16[3,128,128]{2,1,0:T(8,128)(2,1)S(1)}, u32[]{:S(2)}, u32[]{:S(2)}) collective-permute-start(bf16[3,128,128]{2,1,0:T(8,128)(2,1)} %get-tuple-element.33), channel_id=1, source_target_pairs={{0,2},{2,0},{4,6},{6,4},{8,10},{10,8},{12,14},{14,12},{1,3},{3,1},... | collective-permute-start | bytes 294920 | tf_op jit(solution)/shard_map/ppermute | solution.py:439
  5.4 13.2 %collective-permute-start.1 = (bf16[3,128,128]{2,1,0:T(8,128)(2,1)}, bf16[3,128,128]{2,1,0:T(8,128)(2,1)S(1)}, u32[]{:S(2)}, u32[]{:S(2)}) collective-permute-start(bf16[3,128,128]{2,1,0:T(8,128)(2,1)} %get-tuple-element.34), channel_id=1, source_target_pairs={{0,4},{2,6},{4,0},{6,2},{8,12},{10,14},{12,8},{14,10},{1,5},{3,7},... | collective-permute-start | bytes 294920 | tf_op jit(solution)/shard_map/ppermute | solution.py:439
  7.0 11.7 %collective-permute-start.2 = (bf16[3,128,128]{2,1,0:T(8,128)(2,1)}, bf16[3,128,128]{2,1,0:T(8,128)(2,1)S(1)}, u32[]{:S(2)}, u32[]{:S(2)}) collective-permute-start(bf16[3,128,128]{2,1,0:T(8,128)(2,1)} %get-tuple-element.35), channel_id=1, source_target_pairs={{0,6},{2,4},{4,2},{6,0},{8,14},{10,12},{12,10},{14,8},{1,7},{3,5},... | collective-permute-start | bytes 294920 | tf_op jit(solution)/shard_map/ppermute | solution.py:439
  7.0 13.3 %collective-permute-start.3 = (bf16[3,128,128]{2,1,0:T(8,128)(2,1)}, bf16[3,128,128]{2,1,0:T(8,128)(2,1)S(1)}, u32[]{:S(2)}, u32[]{:S(2)}) collective-permute-start(bf16[3,128,128]{2,1,0:T(8,128)(2,1)} %get-tuple-element.36), channel_id=1, source_target_pairs={{0,8},{2,10},{4,12},{6,14},{8,0},{10,2},{12,4},{14,6},{1,9},{3,11}... | collective-permute-start | bytes 294920 | tf_op jit(solution)/shard_map/ppermute | solution.py:439
  10.0 14.4 %collective-permute-start.4 = (bf16[3,128,128]{2,1,0:T(8,128)(2,1)}, bf16[3,128,128]{2,1,0:T(8,128)(2,1)S(1)}, u32[]{:S(2)}, u32[]{:S(2)}) collective-permute-start(bf16[3,128,128]{2,1,0:T(8,128)(2,1)} %get-tuple-element.37), channel_id=1, source_target_pairs={{0,10},{2,8},{4,14},{6,12},{8,2},{10,0},{12,6},{14,4},{1,11},{3,9}... | collective-permute-start | bytes 294920 | tf_op jit(solution)/shard_map/ppermute | solution.py:439
  14.9 9.9 %collective-permute-start.5 = (bf16[3,128,128]{2,1,0:T(8,128)(2,1)}, bf16[3,128,128]{2,1,0:T(8,128)(2,1)S(1)}, u32[]{:S(2)}, u32[]{:S(2)}) collective-permute-start(bf16[3,128,128]{2,1,0:T(8,128)(2,1)} %get-tuple-element.38), channel_id=1, source_target_pairs={{0,12},{2,14},{4,8},{6,10},{8,4},{10,6},{12,0},{14,2},{1,13},{3,15... | collective-permute-start | bytes 294920 | tf_op jit(solution)/shard_map/ppermute | solution.py:439
  18.6 10.3 %collective-permute-start.6 = (bf16[3,128,128]{2,1,0:T(8,128)(2,1)}, bf16[3,128,128]{2,1,0:T(8,128)(2,1)S(1)}, u32[]{:S(2)}, u32[]{:S(2)}) collective-permute-start(bf16[3,128,128]{2,1,0:T(8,128)(2,1)} %get-tuple-element.39), channel_id=1, source_target_pairs={{0,14},{2,12},{4,10},{6,8},{8,6},{10,4},{12,2},{14,0},{1,15},{3,13... | collective-permute-start | bytes 294920 | tf_op jit(solution)/shard_map/ppermute | solution.py:439
  18.6 14.9 %collective-permute-start.7 = (bf16[3,128,128]{2,1,0:T(8,128)(2,1)}, bf16[3,128,128]{2,1,0:T(8,128)(2,1)S(1)}, u32[]{:S(2)}, u32[]{:S(2)}) collective-permute-start(bf16[3,128,128]{2,1,0:T(8,128)(2,1)} %get-tuple-element.42), channel_id=1, source_target_pairs={{0,2},{2,0},{4,6},{6,4},{8,10},{10,8},{12,14},{14,12},{1,3},{3,1},... | collective-permute-start | bytes 294920 | tf_op jit(solution)/shard_map/ppermute | solution.py:439
  20.3 17.4 %collective-permute-start.8 = (bf16[3,128,128]{2,1,0:T(8,128)(2,1)}, bf16[3,128,128]{2,1,0:T(8,128)(2,1)S(1)}, u32[]{:S(2)}, u32[]{:S(2)}) collective-permute-start(bf16[3,128,128]{2,1,0:T(8,128)(2,1)} %get-tuple-element.43), channel_id=1, source_target_pairs={{0,4},{2,6},{4,0},{6,2},{8,12},{10,14},{12,8},{14,10},{1,5},{3,7},... | collective-permute-start | bytes 294920 | tf_op jit(solution)/shard_map/ppermute | solution.py:439
  24.3 17.0 %collective-permute-start.9 = (bf16[3,128,128]{2,1,0:T(8,128)(2,1)}, bf16[3,128,128]{2,1,0:T(8,128)(2,1)S(1)}, u32[]{:S(2)}, u32[]{:S(2)}) collective-permute-start(bf16[3,128,128]{2,1,0:T(8,128)(2,1)} %get-tuple-element.44), channel_id=1, source_target_pairs={{0,6},{2,4},{4,2},{6,0},{8,14},{10,12},{12,10},{14,8},{1,7},{3,5},... | collective-permute-start | bytes 294920 | tf_op jit(solution)/shard_map/ppermute | solution.py:439
  24.8 16.5 %collective-permute-start.10 = (bf16[3,128,128]{2,1,0:T(8,128)(2,1)}, bf16[3,128,128]{2,1,0:T(8,128)(2,1)S(1)}, u32[]{:S(2)}, u32[]{:S(2)}) collective-permute-start(bf16[3,128,128]{2,1,0:T(8,128)(2,1)} %get-tuple-element.45), channel_id=1, source_target_pairs={{0,8},{2,10},{4,12},{6,14},{8,0},{10,2},{12,4},{14,6},{1,9},{3,11}... | collective-permute-start | bytes 294920 | tf_op jit(solution)/shard_map/ppermute | solution.py:439
  28.9 12.4 %collective-permute-start.12 = (bf16[3,128,128]{2,1,0:T(8,128)(2,1)}, bf16[3,128,128]{2,1,0:T(8,128)(2,1)S(1)}, u32[]{:S(2)}, u32[]{:S(2)}) collective-permute-start(bf16[3,128,128]{2,1,0:T(8,128)(2,1)} %get-tuple-element.48), channel_id=1, source_target_pairs={{0,12},{2,14},{4,8},{6,10},{8,4},{10,6},{12,0},{14,2},{1,13},{3,15... | collective-permute-start | bytes 294920 | tf_op jit(solution)/shard_map/ppermute | solution.py:439
  41.3 11.1 %collective-permute-start.14 = (bf16[1024,128]{1,0:T(8,128)(2,1)S(1)}, bf16[1024,128]{1,0:T(8,128)(2,1)S(1)}, u32[]{:S(2)}, u32[]{:S(2)}) collective-permute-start(bf16[1024,128]{1,0:T(8,128)(2,1)S(1)} %shard_map.74.refs_0_), channel_id=1, source_target_pairs={{0,4},{4,8},{8,12},{12,14},{14,10},{10,6},{6,2},{2,0},{1,5},{5,9},... | collective-permute-start | bytes 786440 | tf_op jit(solution)/shard_map/ppermute | solution.py:454
  50.5 9.4 %collective-permute-start.15 = (bf16[1024,128]{1,0:T(8,128)(2,1)S(1)}, bf16[1024,128]{1,0:T(8,128)(2,1)}, u32[]{:S(2)}, u32[]{:S(2)}) collective-permute-start(bf16[1024,128]{1,0:T(8,128)(2,1)S(1)} %shard_map.76.refs_1_), channel_id=1, source_target_pairs={{0,4},{4,8},{8,12},{12,14},{14,10},{10,6},{6,2},{2,0},{1,5},{5,9},... | collective-permute-start | bytes 786440 | tf_op jit(solution)/shard_map/ppermute | solution.py:454
  51.4 12.5 %collective-permute-start.16 = (bf16[1024,128]{1,0:T(8,128)(2,1)S(1)}, bf16[1024,128]{1,0:T(8,128)(2,1)}, u32[]{:S(2)}, u32[]{:S(2)}) collective-permute-start(bf16[1024,128]{1,0:T(8,128)(2,1)S(1)} %shard_map.74.refs_0_), channel_id=1, source_target_pairs={{4,0},{8,4},{12,8},{14,12},{10,14},{6,10},{2,6},{0,2},{5,1},{9,5},... | collective-permute-start | bytes 786440 | tf_op jit(solution)/shard_map/ppermute | solution.py:455
  52.5 12.9 %collective-permute-start.18 = (bf16[1024,128]{1,0:T(8,128)(2,1)S(1)}, bf16[1024,128]{1,0:T(8,128)(2,1)}, u32[]{:S(2)}, u32[]{:S(2)}) collective-permute-start(bf16[1024,128]{1,0:T(8,128)(2,1)S(1)} %collective-permute-done.14.refs_2_), channel_id=1, source_target_pairs={{0,4},{4,8},{8,12},{12,14},{14,10},{10,6},{6,2},{2,0},{1,5},{5,9},... | collective-permute-start | bytes 786440 | tf_op jit(solution)/shard_map/ppermute | solution.py:454
  58.1 11.3 %collective-permute-start.21 = (bf16[1024,128]{1,0:T(8,128)(2,1)S(1)}, bf16[1024,128]{1,0:T(8,128)(2,1)}, u32[]{:S(2)}, u32[]{:S(2)}) collective-permute-start(bf16[1024,128]{1,0:T(8,128)(2,1)S(1)} %collective-permute-done.17.refs_5_), channel_id=1, source_target_pairs={{4,0},{8,4},{12,8},{14,12},{10,14},{6,10},{2,6},{0,2},{5,1},{9,5},... | collective-permute-start | bytes 786440 | tf_op jit(solution)/shard_map/ppermute | solution.py:455
  59.8 11.2 %collective-permute-start.19 = (bf16[1024,128]{1,0:T(8,128)(2,1)}, bf16[1024,128]{1,0:T(8,128)(2,1)}, u32[]{:S(2)}, u32[]{:S(2)}) collective-permute-start(bf16[1024,128]{1,0:T(8,128)(2,1)} %collective-permute-done.15.refs_3_), channel_id=1, source_target_pairs={{0,4},{4,8},{8,12},{12,14},{14,10},{10,6},{6,2},{2,0},{1,5},{5,9},... | collective-permute-start | bytes 786440 | tf_op jit(solution)/shard_map/ppermute | solution.py:454
  63.8 11.2 %collective-permute-start.20 = (bf16[1024,128]{1,0:T(8,128)(2,1)}, bf16[1024,128]{1,0:T(8,128)(2,1)}, u32[]{:S(2)}, u32[]{:S(2)}) collective-permute-start(bf16[1024,128]{1,0:T(8,128)(2,1)} %collective-permute-done.16.refs_4_), channel_id=1, source_target_pairs={{4,0},{8,4},{12,8},{14,12},{10,14},{6,10},{2,6},{0,2},{5,1},{9,5},... | collective-permute-start | bytes 786440 | tf_op jit(solution)/shard_map/ppermute | solution.py:455
  65.4 11.2 %collective-permute-start.22 = (bf16[1024,128]{1,0:T(8,128)(2,1)}, bf16[1024,128]{1,0:T(8,128)(2,1)}, u32[]{:S(2)}, u32[]{:S(2)}) collective-permute-start(bf16[1024,128]{1,0:T(8,128)(2,1)} %collective-permute-done.18.refs_6_), channel_id=1, source_target_pairs={{0,4},{4,8},{8,12},{12,14},{14,10},{10,6},{6,2},{2,0},{1,5},{5,9},... | collective-permute-start | bytes 786440 | tf_op jit(solution)/shard_map/ppermute | solution.py:454
  69.5 11.1 %collective-permute-start.25 = (bf16[1024,128]{1,0:T(8,128)(2,1)}, bf16[1024,128]{1,0:T(8,128)(2,1)S(1)}, u32[]{:S(2)}, u32[]{:S(2)}) collective-permute-start(bf16[1024,128]{1,0:T(8,128)(2,1)} %collective-permute-done.21.refs_9_), channel_id=1, source_target_pairs={{4,0},{8,4},{12,8},{14,12},{10,14},{6,10},{2,6},{0,2},{5,1},{9,5},... | collective-permute-start | bytes 786440 | tf_op jit(solution)/shard_map/ppermute | solution.py:455
  71.0 10.9 %collective-permute-start.23 = (bf16[1024,128]{1,0:T(8,128)(2,1)}, bf16[1024,128]{1,0:T(8,128)(2,1)S(1)}, u32[]{:S(2)}, u32[]{:S(2)}) collective-permute-start(bf16[1024,128]{1,0:T(8,128)(2,1)} %collective-permute-done.19.refs_7_), channel_id=1, source_target_pairs={{0,4},{4,8},{8,12},{12,14},{14,10},{10,6},{6,2},{2,0},{1,5},{5,9},... | collective-permute-start | bytes 786440 | tf_op jit(solution)/shard_map/ppermute | solution.py:454
  75.1 10.2 %collective-permute-start.24 = (bf16[1024,128]{1,0:T(8,128)(2,1)}, bf16[1024,128]{1,0:T(8,128)(2,1)S(1)}, u32[]{:S(2)}, u32[]{:S(2)}) collective-permute-start(bf16[1024,128]{1,0:T(8,128)(2,1)} %collective-permute-done.20.refs_8_), channel_id=1, source_target_pairs={{4,0},{8,4},{12,8},{14,12},{10,14},{6,10},{2,6},{0,2},{5,1},{9,5},... | collective-permute-start | bytes 786440 | tf_op jit(solution)/shard_map/ppermute | solution.py:455
  90.5 9.5 %collective-permute-start.34 = (bf16[128,256]{1,0:T(8,128)(2,1)S(1)}, bf16[128,256]{1,0:T(8,128)(2,1)S(1)}, u32[]{:S(2)}, u32[]{:S(2)}) collective-permute-start(bf16[128,256]{1,0:T(8,128)(2,1)S(1)} %get-tuple-element.57), channel_id=1, source_target_pairs={{0,14},{2,12},{4,10},{6,8},{8,6},{10,4},{12,2},{14,0},{1,15},{3,13... | collective-permute-start | bytes 196616 | tf_op jit(solution)/shard_map/ppermute | solution.py:481
  (19 other events, 292.9 us)
